TPU v7x, 512 devices: a whole 4x8x8 slice. The times are simulated.
512 devices in a mesh: orb: 32 (over y, z_hi, core), aux: 16 (over x, z_lo).
Axes of the slice: x: 4, y: 8, z: 8 (z_hi: 2, z_lo: 4; z = z_hi * 4 + z_lo), core: 2. Of those that a mesh axis runs over, the one named last changes fastest.
Arguments:
- orbital_slabs: float32 [32, 8192, 1024], P('orb', 'aux'), may hold values from -0.625 to 0.625
- occupied_energy: float32 [32], replicated, may hold values from -1.5 to -0.3
- virtual_energy: float32 [1024], replicated, may hold values from 0.3 to 2.5
- virtual_count: int32 [32], replicated, may hold values from 512 to 1024, as said below
Outputs:
- density: float32 [32, 8192, 1024], P('orb', 'aux')
Inputs may be any that keep to these rules, and one draw needn't show every extreme that they name: `virtual_count`: the largest count is 1024 in every draw.
All inputs are finite; a program needn't handle non-finite values.
Results may differ from a plain program's by a relative error of at most 0.0003.
Values sent between devices are 32-bit elements; how exact they have to be, the bound alone decides.
No kernel may reach another device: no remote copies, remote signals or barrier semaphores. Data moves between devices by JAX's collectives and lax.ppermute only.
A program may use at most 64 MiB of HBM per device.

v0:
```python
import jax
import jax.numpy as jnp
from jax import lax
from jax.sharding import PartitionSpec as P

highest_mode = lax.Precision.HIGHEST


def from_behind(block, axis, distance):
    devices = range(lax.axis_size(axis))
    route = [((i - distance) % len(devices), i) for i in devices]
    return lax.ppermute(block, axis, route)


def pair_amplitude(
    slab_one, slab_two, occupied_energy, virtual_energy, virtual_count, orbital_one, orbital_two
):
    partial_sum = lax.dot_general(
        slab_one,
        slab_two,
        (((0,), (0,)), ((), ())),
        precision=highest_mode,
        preferred_element_type=jnp.float32,
    )
    virtuals = virtual_energy.shape[0]
    positions = jnp.arange(virtuals, dtype=jnp.int32)
    mask_two = (positions < virtual_count[orbital_two]).astype(jnp.float32)
    pair_energy = occupied_energy[orbital_one] + occupied_energy[orbital_two]
    coupling = lax.psum(partial_sum, "aux")
    mask_one = (positions < virtual_count[orbital_one]).astype(jnp.float32)
    denominator = virtual_energy[:, None] + virtual_energy[None, :] - pair_energy
    return (2.0 * coupling - coupling.T) * mask_one[:, None] * mask_two[None, :] / denominator


def shards(orbital_slabs, occupied_energy, virtual_energy, virtual_count):
    own_slab = orbital_slabs[0]
    groups = lax.axis_size("orb")
    position = lax.axis_index("orb")
    partner = from_behind(own_slab, "orb", -1)
    later = (position + 1) % groups
    amplitude = pair_amplitude(
        own_slab, partner, occupied_energy, virtual_energy, virtual_count, position, later
    )
    density = lax.dot_general(
        partner,
        amplitude,
        (((1,), (1,)), ((), ())),
        precision=highest_mode,
        preferred_element_type=jnp.float32,
    )
    outgoing = jnp.dot(
        own_slab, amplitude, precision=highest_mode, preferred_element_type=jnp.float32
    )
    density = density + from_behind(outgoing, "orb", 1)
    return density[None]


def solution(mesh):
    placed = (P("orb", "aux", None), P(), P(), P())
    return jax.shard_map(
        shards, mesh=mesh, in_specs=placed, out_specs=P("orb", "aux", None), check_vma=False
    )
```

profile of v0, /device:TPU:32, one launch (start us, length us, event | category | flops | bytes accessed | tf_op | source)
XLA Modules:
  0.0 379.6 jit_solution(10791628282540740961)
XLA Ops:
  6.5 0.0 all-reduce.2.cloned.1.call-start
  6.5 10.2 %collective-permute-start = (f32[512,1024]{1,0:T(8,128)}, f32[512,1024]{1,0:T(8,128)S(1)}, u32[]{:S(2)}, u32[]{:S(2)}) collective-permute-start(f32[512,1024]{1,0:T(8,128)} %bitcast.28), channel_id=1, source_target_pairs={{16,0},{32,16},{48,32},{64,48},{80,64},{96,80},{112,96},{128,112},... | collective-permute-start | bytes 6291464 | tf_op jit(solution)/shard_map/ppermute | solution.py:12
  16.8 43.6 %collective-permute-done = f32[512,1024]{1,0:T(8,128)S(1)} collective-permute-done((f32[512,1024]{1,0:T(8,128)}, f32[512,1024]{1,0:T(8,128)S(1)}, u32[]{:S(2)}, u32[]{:S(2)}) %collective-permute-start) | collective-permute-done | bytes 2097184 | tf_op jit(solution)/shard_map/ppermute | solution.py:12
  60.4 0.0 copy-start
  60.4 1.3 copy-done
  61.7 9.6 %fusion.7 = f32[1024,1024]{1,0:T(8,128)} fusion(f32[512,1024]{1,0:T(8,128)S(1)} %collective-permute-done, f32[1,512,1024]{2,1,0:T(8,128)} %param.4), kind=kOutput, calls=%fused_computation.12 | convolution fusion | flops 6442450944 | bytes 8388608 | tf_op jit(solution)/shard_map/dot_general | solution.py:18
  71.3 0.0 copy-start.4
  71.3 0.0 copy-start.5
  71.3 0.0 all-reduce.2.cloned.1.call-update
  71.4 0.6 copy-done.4
  72.0 0.7 fusion.10
  74.0 0.0 copy-done.5
  74.0 0.7 fusion.9
  74.6 1.3 fusion.4
  75.9 0.0 copy-start.3
  76.0 211.0 %all-reduce.2.cloned.1.call-done = f32[1024,1024]{1,0:T(8,128)} async-done(((f32[1024,1024]{1,0:T(8,128)}), f32[1024,1024]{1,0:T(8,128)}) %all-reduce.2.cloned.1.call-update) | async-done | bytes 4194320 | tf_op jit(solution)/shard_map/psum | solution.py:29
  286.9 5.4 %copy.5 = f32[1024,1024]{0,1:T(8,128)} copy(f32[1024,1024]{1,0:T(8,128)} %all-reduce.2.cloned.1.call-done) | data formatting | bytes 8388608 | tf_op jit(solution)/shard_map/psum | solution.py:29
  292.3 0.0 copy-done.3
  292.3 0.0 copy-start.2
  292.3 4.4 %fusion.2 = f32[1024,1024]{0,1:T(8,128)S(1)} fusion(f32[1024,1024]{1,0:T(8,128)} %all-reduce.2.cloned.1.call-done, f32[1024,1024]{0,1:T(8,128)} %copy.5, f32[]{:T(128)} %bitcast.4, f32[1024]{0:T(1024)S(1)} %copy-done.3, f32[1024]{0:T(1024)S(1)} %get-tuple-element.10, f32[1024]{0:T(1024)S(1)} %get-tuple-element.9), kind=kLoop, calls=%fused_computation.3 | loop fusion | flops 7340032 | bytes 12595204 | tf_op jit(solution)/shard_map/div | solution.py:32
  296.7 0.0 copy-done.2
  296.7 0.0 copy-start.1
  296.7 6.7 %convolution_bitcast_fusion = f32[512,1024]{0,1:T(8,128)S(1)} fusion(f32[1024,1024]{0,1:T(8,128)S(1)} %fusion.2, f32[1,512,1024]{2,1,0:T(8,128)S(1)} %copy-done.2), kind=kOutput, calls=%fused_computation.6 | convolution fusion | flops 6442450944 | bytes 8388608 | tf_op jit(solution)/shard_map/dot_general | solution.py:51
  303.4 2.1 collective-permute-start.1
  305.6 51.8 %collective-permute-done.1 = f32[512,1024]{0,1:T(8,128)S(1)} collective-permute-done((f32[512,1024]{0,1:T(8,128)S(1)}, f32[512,1024]{0,1:T(8,128)S(1)}, u32[]{:S(2)}, u32[]{:S(2)}) %collective-permute-start.1) | collective-permute-done | bytes 2097184 | tf_op jit(solution)/shard_map/ppermute | solution.py:12
  357.3 0.0 copy-done.1
  357.3 13.7 %fusion.3 = f32[1,512,1024]{1,2,0:T(8,128)S(1)} fusion(f32[512,1024]{0,1:T(8,128)S(1)} %collective-permute-done.1, f32[1024,1024]{0,1:T(8,128)S(1)} %fusion.2, f32[512,1024]{1,0:T(8,128)S(1)} %copy-done.1), kind=kOutput, calls=%fused_computation.5 | convolution fusion | flops 6442975232 | bytes 10485760 | tf_op jit(solution)/shard_map/dot_general | solution.py:44
  371.0 1.8 copy.6
Async XLA Ops:
  6.5 280.4 %all-reduce.2.cloned.1.call-start = ((), (), s32[]{:S(2)}) async-start(), calls=%async_computation | async-start | bytes 8388608 | tf_op jit(solution)/shard_map/psum | solution.py:29
  6.5 53.9 %collective-permute-start = (f32[512,1024]{1,0:T(8,128)}, f32[512,1024]{1,0:T(8,128)S(1)}, u32[]{:S(2)}, u32[]{:S(2)}) collective-permute-start(f32[512,1024]{1,0:T(8,128)} %bitcast.28), channel_id=1, source_target_pairs={{16,0},{32,16},{48,32},{64,48},{80,64},{96,80},{112,96},{128,112},... | collective-permute-start | bytes 6291464 | tf_op jit(solution)/shard_map/ppermute | solution.py:12
  60.4 1.3 copy-start
  71.3 0.7 copy-start.4
  71.3 2.6 copy-start.5
  75.9 216.4 %copy-start.3 = (f32[1024]{0:T(1024)S(1)}, f32[1024]{0:T(1024)}, u32[]{:S(2)}) copy-start(f32[1024]{0:T(1024)} %param.6) | copy-start | bytes 12292
  292.3 4.4 %copy-start.2 = (f32[1,512,1024]{2,1,0:T(8,128)S(1)}, f32[1,512,1024]{2,1,0:T(8,128)}, u32[]{:S(2)}) copy-start(f32[1,512,1024]{2,1,0:T(8,128)} %param.4) | copy-start | bytes 6291460
  296.7 60.6 %copy-start.1 = (f32[512,1024]{1,0:T(8,128)S(1)}, f32[512,1024]{1,0:T(8,128)}, u32[]{:S(2)}) copy-start(f32[512,1024]{1,0:T(8,128)} %copy-done) | copy-start | bytes 6291460
  303.4 53.9 %collective-permute-start.1 = (f32[512,1024]{0,1:T(8,128)S(1)}, f32[512,1024]{0,1:T(8,128)S(1)}, u32[]{:S(2)}, u32[]{:S(2)}) collective-permute-start(f32[512,1024]{0,1:T(8,128)S(1)} %convolution_bitcast_fusion), channel_id=1, source_target_pairs={{496,0},{0,16},{16,32},{32,48},{48,64},{64,80},{80,96},{96,112},{1... | collective-permute-start | bytes 6291464 | tf_op jit(solution)/shard_map/ppermute | solution.py:12
Sparse Core Ops, SparseCore 0:
  71.5 215.4 all-reduce.1
where the time goes:
time: 380 us
  waiting for transfers between devices  306 us (81%)
  matrix products  30 us (8%)
  between operations  14.8 us (4%)
  starting transfers between devices  12.3 us (3%)
  local copies, waits for them, and re-layouts  10.5 us (3%)
  other arithmetic  5.69 us (1%)
    psum x1, waiting for transfers between devices, pair_amplitude(): coupling = lax.psum(partial_sum, 'aux')  211 us
    ppermute x2, waiting for transfers between devices, from_behind(): return lax.ppermute(block, axis, route)  95.4 us
    dot_general x1, matrix products, shards(): lax.dot_general(partner, amplitude, (((1,), (1,)), ((), ())), precision=h...  13.7 us
    ppermute x2, starting transfers between devices, from_behind(): return lax.ppermute(block, axis, route)  12.3 us
    dot_general x1, matrix products, pair_amplitude(): lax.dot_general(slab_one, slab_two, (((0,), (0,)), ((), ())), precision=h...  9.6 us
  transfers between devices with their start and end apart: 3, of which 3 were waited for; matrix products, arithmetic and copies ran while one was open for 1% of the time, Pallas kernels for 0%

commit v1 on v0

v1 whole, which is shorter than its diff:
```python
import jax
import jax.numpy as jnp
from jax import lax
from jax.sharding import PartitionSpec as P


ORB, AUX = 32, 16
AXES = ("orb", "aux")
X, ZL = 4, 4
QUARTER, HALF_Q, COLS = 256, 128, 512
ROWS = 256


def route(step):
    pairs = []
    for orbital in range(ORB):
        for shard in range(AUX):
            target = step(orbital, shard // ZL, shard % ZL)
            if target is not None:
                o, x, z = target
                pairs.append((orbital * AUX + shard, o % ORB * AUX + x % X * ZL + z))
    return pairs


SWAP = route(lambda o, x, z: (o ^ 1, x, z))
DOWN = [route(lambda o, x, z: (o - 2 + c, x, z) if o % 2 == 0 else None) for c in (0, 1)]
UP = [route(lambda o, x, z: (o + 2 - c, x, z) if o % 2 == c else None) for c in (0, 1)]
AROUND = [route(lambda o, x, z: (o, x + r, z)) for r in range(X)]
ALONG = [route(lambda o, x, z: (o, x, z ^ d)) for d in range(ZL)]


def move(block, pairs):
    return lax.ppermute(block, AXES, pairs)


def dot(a, b, da, db):
    return lax.dot_general(
        a,
        b,
        (((da,), (db,)), ((), ())),
        precision=lax.Precision.HIGH,
        preferred_element_type=jnp.float32,
    )


def rows_at(block, start, size):
    return lax.dynamic_slice_in_dim(block, start, size, 0)


def cols_at(block, start, size):
    return lax.dynamic_slice_in_dim(block, start, size, 1)


def after(value, *earlier):
    return lax.optimization_barrier((value, earlier))[0]


def pair_term(one, two, two_cols, one_cols):
    return 2.0 * dot(one, two_cols, 0, 0) - dot(two, one_cols, 0, 0)


def shards(orbital_slabs, occupied_energy, virtual_energy, virtual_count):
    own = orbital_slabs[0]
    orbital = lax.axis_index("orb")
    shard = lax.axis_index("aux")
    core, base = orbital % 2, orbital - orbital % 2
    px, pz = shard // ZL, shard % ZL
    bit = pz % 2
    first = core == 0
    at = core * COLS

    def send_x(term):
        return [rows_at(term, (px + r) % X * QUARTER, QUARTER) for r in range(X)]

    def add_x(parts):
        return (parts[0] + parts[1]) + (parts[2] + parts[3])

    def around(parts):
        return [parts[0]] + [move(parts[r], AROUND[r]) for r in (1, 2, 3)]

    def halves(total):
        return rows_at(total, bit * HALF_Q, HALF_Q), rows_at(
            total, (1 - bit) * HALF_Q, HALF_Q
        )

    def amplitude(term, left, right, col):
        row = px * QUARTER + bit * HALF_Q
        rows = row + jnp.arange(term.shape[0], dtype=jnp.int32)
        cols = col + jnp.arange(term.shape[1], dtype=jnp.int32)
        energy_rows = lax.dynamic_slice_in_dim(virtual_energy, row, term.shape[0])
        energy_cols = lax.dynamic_slice_in_dim(virtual_energy, col, term.shape[1])
        keep_rows = (rows < virtual_count[left]).astype(jnp.float32)
        keep_cols = (cols < virtual_count[right]).astype(jnp.float32)
        denominator = (
            energy_rows[:, None]
            + energy_cols[None, :]
            - occupied_energy[left]
            - occupied_energy[right]
        )
        return term * keep_rows[:, None] * keep_cols[None, :] / denominator

    def join(part, other):
        return jnp.where(
            bit == 0,
            jnp.concatenate([part, other], 0),
            jnp.concatenate([other, part], 0),
        )

    def in_order(pieces):
        whole = jnp.zeros((X * QUARTER, pieces[0].shape[1]), jnp.float32)
        for r, piece in enumerate(pieces):
            whole = lax.dynamic_update_slice_in_dim(
                whole, piece, (px - r) % X * QUARTER, 0
            )
        return whole

    one, two, three = base, base + 1, (base + 2) % ORB

    arrived = [move(own[c * ROWS : (c + 1) * ROWS], DOWN[c]) for c in (0, 1)]
    other = move(own, SWAP)
    slab_one = jnp.where(first, own, other)
    slab_two = jnp.where(first, other, own)
    one_cols = cols_at(slab_one, at, COLS)
    two_cols = cols_at(slab_two, at, COLS)

    inner_sends = send_x(pair_term(slab_one, slab_two, two_cols, one_cols))
    inner_parts = around(inner_sends)
    inner_kept, inner_sent = halves(add_x(inner_parts))
    inner_kept_next = inner_kept + move(inner_sent, ALONG[1])

    near_two = rows_at(slab_two, core * ROWS, ROWS)
    far_two = rows_at(slab_two, (1 - core) * ROWS, ROWS)
    near_two_cols, far_two_cols = cols_at(near_two, at, COLS), cols_at(far_two, at, COLS)
    arrived = after(arrived, inner_sent, near_two, far_two, near_two_cols, far_two_cols)
    near = jnp.where(first, arrived[0], arrived[1])
    far = move(near, SWAP)
    near_cols = cols_at(near, at, COLS)
    outer_near = pair_term(near_two, near, near_cols, near_two_cols)
    far = after(far, outer_near)
    far_cols = cols_at(far, at, COLS)
    outer = outer_near + pair_term(far_two, far, far_cols, far_two_cols)
    outer_sends = send_x(outer)
    outer_parts = around(outer_sends)

    inner_kept = after(inner_kept_next, outer_sends)
    inner_kept = inner_kept + move(inner_kept, ALONG[2])
    inner_t = amplitude(inner_kept, one, two, at)
    inner_other = move(inner_t, ALONG[1])

    outer_kept, outer_sent = halves(add_x(after(outer_parts, inner_t)))
    outer_other = move(outer_sent, ALONG[1])
    inner_quarter = join(inner_t, after(inner_other, outer_sent))
    inner_pieces = around([inner_quarter] * X)
    outer_kept = outer_kept + after(outer_other, inner_quarter)
    outer_kept = outer_kept + move(outer_kept, ALONG[2])
    outer_t = amplitude(outer_kept, two, three, at)
    outer_quarter = join(outer_t, move(outer_t, ALONG[1]))
    outer_pieces = around([outer_quarter] * X)

    inner_all = in_order(after(inner_pieces, outer_quarter))
    to_one = dot(two_cols, inner_all, 1, 1)
    to_two = dot(slab_one, inner_all, 1, 0)

    outer_all = in_order(after(outer_pieces, to_one, to_two))
    outgoing = dot(slab_two, outer_all, 1, 0)
    incoming = [move(outgoing, UP[c]) for c in (0, 1)]

    three_cols = jnp.where(
        first,
        jnp.concatenate([near_cols, far_cols], 0),
        jnp.concatenate([far_cols, near_cols], 0),
    )
    beyond = dot(three_cols, after(outer_all, outgoing), 1, 1)
    blank = jnp.zeros_like(to_two)
    to_two = beyond + jnp.where(
        first,
        jnp.concatenate([to_two, blank], 1),
        jnp.concatenate([blank, to_two], 1),
    )
    crossed = move(jnp.where(first, to_two, to_one), SWAP)
    density = jnp.where(first, to_one, to_two) + crossed
    density = density + jnp.concatenate(after(incoming, density), 1)
    return density[None]


def solution(mesh):
    placed = (P("orb", "aux", None), P(), P(), P())
    return jax.shard_map(
        shards, mesh=mesh, in_specs=placed, out_specs=P("orb", "aux", None), check_vma=False
    )
```

time: 380 us -> 252 us (0.66)
  the two profiles are of different devices: /device:TPU:32 before, /device:TPU:152 now
where the time goes in v1:
time: 252 us; the launch traced here: 251 us
  waiting for transfers between devices  101 us (40%)
  starting transfers between devices  92.4 us (37%)
  other arithmetic  19.6 us (8%)
  matrix products  18.6 us (7%)
  local copies, waits for them, and re-layouts  18.1 us (7%)
    ppermute x25, waiting for transfers between devices, move(): return lax.ppermute(block, AXES, pairs)  101 us
    ppermute x25, starting transfers between devices, move(): return lax.ppermute(block, AXES, pairs)  92.4 us
    dot_general x10, matrix products, dot(): lax.dot_general(a, b, (((da,), (db,)), ((), ())), precision=lax.Precision...  18.6 us
  transfers between devices with their start and end apart: 25, of which 14 were waited for; matrix products, arithmetic and copies ran while one was open for 18% of the time, Pallas kernels for 0%

profile of v1, /device:TPU:152, one launch (start us, length us, event | category | flops | bytes accessed | tf_op | source)
XLA Modules:
  0.0 250.9 jit_solution(15703510347800940365)
XLA Ops:
  0.0 1.9 collective-permute-start
  1.9 3.1 %slice_bitcast_fusion = (f32[256,1024]{1,0:T(8,128)}, f32[256,1024]{1,0:T(8,128)}) fusion(f32[1,512,1024]{2,1,0:T(8,128)} %param.4), kind=kLoop, calls=%fused_computation.15 | loop fusion | bytes 4194304 | tf_op jit(solution)/shard_map/slice | solution.py:119
  5.1 9.0 %collective-permute-start.5 = (f32[256,1024]{1,0:T(8,128)}, f32[256,1024]{1,0:T(8,128)S(1)}, u32[]{:S(2)}, u32[]{:S(2)}) collective-permute-start(f32[256,1024]{1,0:T(8,128)} %get-tuple-element.58), channel_id=1, source_target_pairs={{0,480},{1,481},{2,482},{3,483},{4,484},{5,485},{6,486},{7,487},{8... | collective-permute-start | bytes 3145736 | tf_op jit(solution)/shard_map/ppermute | solution.py:33
  14.1 2.3 collective-permute-start.6
  16.4 2.9 %broadcast_select_fusion.1 = (f32[512,1024]{1,0:T(8,128)S(1)}, f32[512,1024]{1,0:T(8,128)S(1)}) fusion(f32[512,1024]{1,0:T(8,128)} %collective-permute-done, pred[]{:T(512)S(6)} %eq.29, f32[1,512,1024]{2,1,0:T(8,128)} %param.4), kind=kLoop, calls=%fused_computation.20 | loop fusion | flops 1048576 | bytes 8388609 | tf_op jit(solution)/shard_map/jit(_where)/select_n | solution.py:122
  19.2 1.8 fusion.14
  21.1 1.9 multiply_subtract_fusion.1
  23.0 1.3 copy-done.2
  24.4 1.2 constant_dynamic-slice_fusion.12
  25.5 3.4 %collective-permute-start.1 = (f32[256,512]{1,0:T(8,128)}, f32[256,512]{1,0:T(8,128)}, u32[]{:S(2)}, u32[]{:S(2)}) collective-permute-start(f32[256,512]{1,0:T(8,128)} %get-tuple-element.59), channel_id=1, source_target_pairs={{0,4},{1,5},{2,6},{3,7},{4,8},{5,9},{6,10},{7,11},{8,12},{9,13},{1... | collective-permute-start | bytes 1572872 | tf_op jit(solution)/shard_map/ppermute | solution.py:33
  29.0 4.6 %collective-permute-start.2 = (f32[256,512]{1,0:T(8,128)}, f32[256,512]{1,0:T(8,128)}, u32[]{:S(2)}, u32[]{:S(2)}) collective-permute-start(f32[256,512]{1,0:T(8,128)} %get-tuple-element.61), channel_id=1, source_target_pairs={{0,8},{1,9},{2,10},{3,11},{4,12},{5,13},{6,14},{7,15},{8,0},{9,1},... | collective-permute-start | bytes 1572872 | tf_op jit(solution)/shard_map/ppermute | solution.py:33
  33.6 3.3 %collective-permute-start.3 = (f32[256,512]{1,0:T(8,128)}, f32[256,512]{1,0:T(8,128)}, u32[]{:S(2)}, u32[]{:S(2)}) collective-permute-start(f32[256,512]{1,0:T(8,128)} %get-tuple-element.60), channel_id=1, source_target_pairs={{0,12},{1,13},{2,14},{3,15},{4,0},{5,1},{6,2},{7,3},{8,4},{9,5},{1... | collective-permute-start | bytes 1572872 | tf_op jit(solution)/shard_map/ppermute | solution.py:33
  37.0 1.4 fusion.29
  38.4 1.6 constant_dynamic-slice_fusion.7
  40.7 5.6 %collective-permute-done.2 = f32[256,512]{1,0:T(8,128)} collective-permute-done((f32[256,512]{1,0:T(8,128)}, f32[256,512]{1,0:T(8,128)}, u32[]{:S(2)}, u32[]{:S(2)}) %collective-permute-start.2) | collective-permute-done | bytes 524320 | tf_op jit(solution)/shard_map/ppermute | solution.py:33
  46.3 1.6 collective-permute-done.3
  47.9 1.7 add_add_fusion.1
  49.7 1.9 collective-permute-done.5
  51.6 8.7 %collective-permute-done.6 = f32[256,1024]{1,0:T(8,128)} collective-permute-done((f32[256,1024]{1,0:T(8,128)}, f32[256,1024]{1,0:T(8,128)}, u32[]{:S(2)}, u32[]{:S(2)}) %collective-permute-start.6) | collective-permute-done | bytes 1048608 | tf_op jit(solution)/shard_map/ppermute | solution.py:33
  60.3 1.4 broadcast_select_fusion.2
  61.7 10.2 %collective-permute-start.7 = (f32[256,1024]{1,0:T(8,128)S(1)}, f32[256,1024]{1,0:T(8,128)}, u32[]{:S(2)}, u32[]{:S(2)}) collective-permute-start(f32[256,1024]{1,0:T(8,128)S(1)} %broadcast_select_fusion.2), channel_id=1, source_target_pairs={{0,16},{1,17},{2,18},{3,19},{4,20},{5,21},{6,22},{7,23},{8,24},{9,... | collective-permute-start | bytes 3145736 | tf_op jit(solution)/shard_map/ppermute | solution.py:33
  71.9 1.9 collective-permute-start.4
  74.6 2.3 fusion.32
  77.0 1.1 multiply_subtract_fusion
  78.1 1.1 constant_dynamic-slice_fusion.5
  80.3 2.5 %subtract_add_fusion = f32[1024,512]{1,0:T(8,128)S(1)} fusion(f32[1024,512]{1,0:T(8,128)S(1)} %multiply_subtract_fusion, f32[1024,512]{1,0:T(8,128)S(1)} %fusion.33, f32[256,1024]{1,0:T(8,128)} %collective-permute-done.7, f32[256,512]{1,0:T(8,128)S(1)} %copy-done.9), kind=kOutput, calls=%fused_computation.4 | convolution fusion | flops 806879232 | bytes 7864320 | tf_op jit(solution)/shard_map/dot_general | solution.py:37
  82.9 1.4 constant_dynamic-slice_fusion.1
  84.2 3.4 %collective-permute-start.10 = (f32[256,512]{1,0:T(8,128)}, f32[256,512]{1,0:T(8,128)}, u32[]{:S(2)}, u32[]{:S(2)}) collective-permute-start(f32[256,512]{1,0:T(8,128)} %get-tuple-element.51), channel_id=1, source_target_pairs={{0,4},{1,5},{2,6},{3,7},{4,8},{5,9},{6,10},{7,11},{8,12},{9,13},{1... | collective-permute-start | bytes 1572872 | tf_op jit(solution)/shard_map/ppermute | solution.py:33
  87.6 4.6 %collective-permute-start.11 = (f32[256,512]{1,0:T(8,128)}, f32[256,512]{1,0:T(8,128)}, u32[]{:S(2)}, u32[]{:S(2)}) collective-permute-start(f32[256,512]{1,0:T(8,128)} %get-tuple-element.50), channel_id=1, source_target_pairs={{0,8},{1,9},{2,10},{3,11},{4,12},{5,13},{6,14},{7,15},{8,0},{9,1},... | collective-permute-start | bytes 1572872 | tf_op jit(solution)/shard_map/ppermute | solution.py:33
  92.3 3.3 %collective-permute-start.12 = (f32[256,512]{1,0:T(8,128)}, f32[256,512]{1,0:T(8,128)}, u32[]{:S(2)}, u32[]{:S(2)}) collective-permute-start(f32[256,512]{1,0:T(8,128)} %get-tuple-element.49), channel_id=1, source_target_pairs={{0,12},{1,13},{2,14},{3,15},{4,0},{5,1},{6,2},{7,3},{8,4},{9,5},{1... | collective-permute-start | bytes 1572872 | tf_op jit(solution)/shard_map/ppermute | solution.py:33
  95.7 2.1 collective-permute-start.8
  100.6 7.8 %collective-permute-done.8 = f32[128,512]{1,0:T(8,128)S(1)} collective-permute-done((f32[128,512]{1,0:T(8,128)S(1)}, f32[128,512]{1,0:T(8,128)S(1)}, u32[]{:S(2)}, u32[]{:S(2)}) %collective-permute-start.8) | collective-permute-done | bytes 262176 | tf_op jit(solution)/shard_map/ppermute | solution.py:33
  108.4 1.3 fusion.18
  109.7 6.5 %collective-permute-start.9 = (f32[128,512]{1,0:T(8,128)S(1)}, f32[128,512]{1,0:T(8,128)}, u32[]{:S(2)}, u32[]{:S(2)}) collective-permute-start(f32[128,512]{1,0:T(8,128)S(1)} %fusion.18), channel_id=1, source_target_pairs={{0,1},{1,0},{2,3},{3,2},{4,5},{5,4},{6,7},{7,6},{8,9},{9,8},{10,11... | collective-permute-start | bytes 786440 | tf_op jit(solution)/shard_map/ppermute | solution.py:33
  116.2 1.7 add_add_fusion
  118.7 2.7 %collective-permute-start.16 = (f32[128,512]{1,0:T(8,128)}, f32[128,512]{1,0:T(8,128)}, u32[]{:S(2)}, u32[]{:S(2)}) collective-permute-start(f32[128,512]{1,0:T(8,128)} %constant_dynamic-slice_fusion), channel_id=1, source_target_pairs={{0,1},{1,0},{2,3},{3,2},{4,5},{5,4},{6,7},{7,6},{8,9},{9,8},{10,11... | collective-permute-start | bytes 786440 | tf_op jit(solution)/shard_map/ppermute | solution.py:33
  121.4 1.5 collective-permute-done.9
  122.8 1.9 maximum_select_fusion.2
  124.7 4.2 %collective-permute-done.16 = f32[128,512]{1,0:T(8,128)} collective-permute-done((f32[128,512]{1,0:T(8,128)}, f32[128,512]{1,0:T(8,128)}, u32[]{:S(2)}, u32[]{:S(2)}) %collective-permute-start.16) | collective-permute-done | bytes 262176 | tf_op jit(solution)/shard_map/ppermute | solution.py:33
  129.9 1.9 collective-permute-start.17
  133.1 3.5 %collective-permute-start.13 = (f32[256,512]{1,0:T(8,128)}, f32[256,512]{1,0:T(8,128)S(1)}, u32[]{:S(2)}, u32[]{:S(2)}) collective-permute-start(f32[256,512]{1,0:T(8,128)} %maximum_select_fusion.2), channel_id=1, source_target_pairs={{0,4},{1,5},{2,6},{3,7},{4,8},{5,9},{6,10},{7,11},{8,12},{9,13},{1... | collective-permute-start | bytes 1572872 | tf_op jit(solution)/shard_map/ppermute | solution.py:33
  136.6 3.6 %collective-permute-start.14 = (f32[256,512]{1,0:T(8,128)}, f32[256,512]{1,0:T(8,128)}, u32[]{:S(2)}, u32[]{:S(2)}) collective-permute-start(f32[256,512]{1,0:T(8,128)} %maximum_select_fusion.2), channel_id=1, source_target_pairs={{0,8},{1,9},{2,10},{3,11},{4,12},{5,13},{6,14},{7,15},{8,0},{9,1},... | collective-permute-start | bytes 1572872 | tf_op jit(solution)/shard_map/ppermute | solution.py:33
  140.3 2.9 %collective-permute-start.15 = (f32[256,512]{1,0:T(8,128)}, f32[256,512]{1,0:T(8,128)}, u32[]{:S(2)}, u32[]{:S(2)}) collective-permute-start(f32[256,512]{1,0:T(8,128)} %maximum_select_fusion.2), channel_id=1, source_target_pairs={{0,12},{1,13},{2,14},{3,15},{4,0},{5,1},{6,2},{7,3},{8,4},{9,5},{1... | collective-permute-start | bytes 1572872 | tf_op jit(solution)/shard_map/ppermute | solution.py:33
  143.1 1.4 fusion.20
  144.5 5.7 %collective-permute-start.18 = (f32[128,512]{1,0:T(8,128)S(1)}, f32[128,512]{1,0:T(8,128)}, u32[]{:S(2)}, u32[]{:S(2)}) collective-permute-start(f32[128,512]{1,0:T(8,128)S(1)} %fusion.20), channel_id=1, source_target_pairs={{0,1},{1,0},{2,3},{3,2},{4,5},{5,4},{6,7},{7,6},{8,9},{9,8},{10,11... | collective-permute-start | bytes 786440 | tf_op jit(solution)/shard_map/ppermute | solution.py:33
  150.4 6.5 %collective-permute-done.18 = f32[128,512]{1,0:T(8,128)} collective-permute-done((f32[128,512]{1,0:T(8,128)S(1)}, f32[128,512]{1,0:T(8,128)}, u32[]{:S(2)}, u32[]{:S(2)}) %collective-permute-start.18) | collective-permute-done | bytes 262176 | tf_op jit(solution)/shard_map/ppermute | solution.py:33
  156.9 1.1 maximum_select_fusion.3
  158.0 3.8 %collective-permute-start.19 = (f32[256,512]{1,0:T(8,128)S(1)}, f32[256,512]{1,0:T(8,128)S(1)}, u32[]{:S(2)}, u32[]{:S(2)}) collective-permute-start(f32[256,512]{1,0:T(8,128)S(1)} %maximum_select_fusion.3), channel_id=1, source_target_pairs={{0,4},{1,5},{2,6},{3,7},{4,8},{5,9},{6,10},{7,11},{8,12},{9,13},{1... | collective-permute-start | bytes 1572872 | tf_op jit(solution)/shard_map/ppermute | solution.py:33
  161.7 3.6 %collective-permute-start.20 = (f32[256,512]{1,0:T(8,128)S(1)}, f32[256,512]{1,0:T(8,128)S(1)}, u32[]{:S(2)}, u32[]{:S(2)}) collective-permute-start(f32[256,512]{1,0:T(8,128)S(1)} %maximum_select_fusion.3), channel_id=1, source_target_pairs={{0,8},{1,9},{2,10},{3,11},{4,12},{5,13},{6,14},{7,15},{8,0},{9,1},... | collective-permute-start | bytes 1572872 | tf_op jit(solution)/shard_map/ppermute | solution.py:33
  165.4 2.9 %collective-permute-start.21 = (f32[256,512]{1,0:T(8,128)S(1)}, f32[256,512]{1,0:T(8,128)S(1)}, u32[]{:S(2)}, u32[]{:S(2)}) collective-permute-start(f32[256,512]{1,0:T(8,128)S(1)} %maximum_select_fusion.3), channel_id=1, source_target_pairs={{0,12},{1,13},{2,14},{3,15},{4,0},{5,1},{6,2},{7,3},{8,4},{9,5},{1... | collective-permute-start | bytes 1572872 | tf_op jit(solution)/shard_map/ppermute | solution.py:33
  169.7 1.1 constant_dynamic-update-slice_fusion.5
  170.8 1.1 constant_dynamic-update-slice_fusion.4
  171.9 2.0 fusion.12
  173.8 1.9 fusion.34
  175.8 10.2 %collective-permute-done.20 = f32[256,512]{1,0:T(8,128)S(1)} collective-permute-done((f32[256,512]{1,0:T(8,128)S(1)}, f32[256,512]{1,0:T(8,128)S(1)}, u32[]{:S(2)}, u32[]{:S(2)}) %collective-permute-start.20) | collective-permute-done | bytes 524320 | tf_op jit(solution)/shard_map/ppermute | solution.py:33
  186.0 2.1 collective-permute-done.21
  188.6 1.9 fusion.35
  190.5 2.1 fusion.1
  192.6 1.9 collective-permute-start.22
  194.5 2.0 collective-permute-start.23
  196.5 1.3 collective-permute-start.24
  199.6 48.4 %collective-permute-done.23 = f32[512,512]{1,0:T(8,128)S(1)} collective-permute-done((f32[512,512]{1,0:T(8,128)S(1)}, f32[512,512]{1,0:T(8,128)S(1)}, u32[]{:S(2)}, u32[]{:S(2)}) %collective-permute-start.23) | collective-permute-done | bytes 1048608 | tf_op jit(solution)/shard_map/ppermute | solution.py:33
  248.0 1.2 collective-permute-done.24
  249.2 1.7 fusion
  (63 shorter events, 12.1 us)
Async XLA Ops:
  0.0 16.4 %collective-permute-start = (f32[512,1024]{1,0:T(8,128)}, f32[512,1024]{1,0:T(8,128)}, u32[]{:S(2)}, u32[]{:S(2)}) collective-permute-start(f32[512,1024]{1,0:T(8,128)} %bitcast.31), channel_id=1, source_target_pairs={{0,16},{1,17},{2,18},{3,19},{4,20},{5,21},{6,22},{7,23},{8,24},{9,... | collective-permute-start | bytes 6291464 | tf_op jit(solution)/shard_map/ppermute | solution.py:33
  5.1 46.5 %collective-permute-start.5 = (f32[256,1024]{1,0:T(8,128)}, f32[256,1024]{1,0:T(8,128)S(1)}, u32[]{:S(2)}, u32[]{:S(2)}) collective-permute-start(f32[256,1024]{1,0:T(8,128)} %get-tuple-element.58), channel_id=1, source_target_pairs={{0,480},{1,481},{2,482},{3,483},{4,484},{5,485},{6,486},{7,487},{8... | collective-permute-start | bytes 3145736 | tf_op jit(solution)/shard_map/ppermute | solution.py:33
  14.1 46.2 %collective-permute-start.6 = (f32[256,1024]{1,0:T(8,128)}, f32[256,1024]{1,0:T(8,128)}, u32[]{:S(2)}, u32[]{:S(2)}) collective-permute-start(f32[256,1024]{1,0:T(8,128)} %get-tuple-element.57), channel_id=1, source_target_pairs={{0,496},{1,497},{2,498},{3,499},{4,500},{5,501},{6,502},{7,503},{8... | collective-permute-start | bytes 3145736 | tf_op jit(solution)/shard_map/ppermute | solution.py:33
  19.2 1.9 copy-start
  23.0 1.3 copy-start.2
  25.5 15.2 %collective-permute-start.1 = (f32[256,512]{1,0:T(8,128)}, f32[256,512]{1,0:T(8,128)}, u32[]{:S(2)}, u32[]{:S(2)}) collective-permute-start(f32[256,512]{1,0:T(8,128)} %get-tuple-element.59), channel_id=1, source_target_pairs={{0,4},{1,5},{2,6},{3,7},{4,8},{5,9},{6,10},{7,11},{8,12},{9,13},{1... | collective-permute-start | bytes 1572872 | tf_op jit(solution)/shard_map/ppermute | solution.py:33
  29.0 17.4 %collective-permute-start.2 = (f32[256,512]{1,0:T(8,128)}, f32[256,512]{1,0:T(8,128)}, u32[]{:S(2)}, u32[]{:S(2)}) collective-permute-start(f32[256,512]{1,0:T(8,128)} %get-tuple-element.61), channel_id=1, source_target_pairs={{0,8},{1,9},{2,10},{3,11},{4,12},{5,13},{6,14},{7,15},{8,0},{9,1},... | collective-permute-start | bytes 1572872 | tf_op jit(solution)/shard_map/ppermute | solution.py:33
  33.6 14.3 %collective-permute-start.3 = (f32[256,512]{1,0:T(8,128)}, f32[256,512]{1,0:T(8,128)}, u32[]{:S(2)}, u32[]{:S(2)}) collective-permute-start(f32[256,512]{1,0:T(8,128)} %get-tuple-element.60), channel_id=1, source_target_pairs={{0,12},{1,13},{2,14},{3,15},{4,0},{5,1},{6,2},{7,3},{8,4},{9,5},{1... | collective-permute-start | bytes 1572872 | tf_op jit(solution)/shard_map/ppermute | solution.py:33
  49.7 10.6 %copy-start.6 = (f32[256,512]{1,0:T(8,128)}, f32[256,512]{1,0:T(8,128)S(1)}, u32[]{:S(2)}) copy-start(f32[256,512]{1,0:T(8,128)S(1)} %add_add_fusion.1) | copy-start | bytes 1572868
  51.6 8.7 %copy-start.10 = (f32[256,1024]{1,0:T(8,128)}, f32[256,1024]{1,0:T(8,128)S(1)}, u32[]{:S(2)}) copy-start(f32[256,1024]{1,0:T(8,128)S(1)} %collective-permute-done.5) | copy-start | bytes 3145732
  61.7 16.4 %collective-permute-start.7 = (f32[256,1024]{1,0:T(8,128)S(1)}, f32[256,1024]{1,0:T(8,128)}, u32[]{:S(2)}, u32[]{:S(2)}) collective-permute-start(f32[256,1024]{1,0:T(8,128)S(1)} %broadcast_select_fusion.2), channel_id=1, source_target_pairs={{0,16},{1,17},{2,18},{3,19},{4,20},{5,21},{6,22},{7,23},{8,24},{9,... | collective-permute-start | bytes 3145736 | tf_op jit(solution)/shard_map/ppermute | solution.py:33
  71.9 23.7 %collective-permute-start.4 = (f32[128,512]{1,0:T(8,128)S(1)}, f32[128,512]{1,0:T(8,128)S(1)}, u32[]{:S(2)}, u32[]{:S(2)}) collective-permute-start(f32[128,512]{1,0:T(8,128)S(1)} %constant_dynamic-slice_fusion.9), channel_id=1, source_target_pairs={{0,1},{1,0},{2,3},{3,2},{4,5},{5,4},{6,7},{7,6},{8,9},{9,8},{10,11... | collective-permute-start | bytes 786440 | tf_op jit(solution)/shard_map/ppermute | solution.py:33
  73.9 0.8 copy-start.3
  74.6 2.3 copy-start.8
  77.0 2.2 copy-start.5
  79.2 1.0 copy-start.9
  82.8 12.8 %copy-start.7 = (f32[256,512]{1,0:T(8,128)S(1)}, f32[256,512]{1,0:T(8,128)}, u32[]{:S(2)}) copy-start(f32[256,512]{1,0:T(8,128)} %copy-done.6) | copy-start | bytes 1572868
  82.8 15.0 %copy-start.13 = (f32[1024]{0:T(1024)S(1)}, f32[1024]{0:T(1024)}, u32[]{:S(2)}) copy-start(f32[1024]{0:T(1024)} %param.6) | copy-start | bytes 12292
  82.8 15.2 %copy-start.11 = (s32[32]{0:T(128)S(1)}, s32[32]{0:T(128)}, u32[]{:S(2)}) copy-start(s32[32]{0:T(128)} %param.7) | copy-start | bytes 388
  82.8 15.8 %copy-start.12 = (f32[32]{0:T(128)S(1)}, f32[32]{0:T(128)}, u32[]{:S(2)}) copy-start(f32[32]{0:T(128)} %param.5) | copy-start | bytes 388
  84.2 32.0 %collective-permute-start.10 = (f32[256,512]{1,0:T(8,128)}, f32[256,512]{1,0:T(8,128)}, u32[]{:S(2)}, u32[]{:S(2)}) collective-permute-start(f32[256,512]{1,0:T(8,128)} %get-tuple-element.51), channel_id=1, source_target_pairs={{0,4},{1,5},{2,6},{3,7},{4,8},{5,9},{6,10},{7,11},{8,12},{9,13},{1... | collective-permute-start | bytes 1572872 | tf_op jit(solution)/shard_map/ppermute | solution.py:33
  87.6 28.6 %collective-permute-start.11 = (f32[256,512]{1,0:T(8,128)}, f32[256,512]{1,0:T(8,128)}, u32[]{:S(2)}, u32[]{:S(2)}) collective-permute-start(f32[256,512]{1,0:T(8,128)} %get-tuple-element.50), channel_id=1, source_target_pairs={{0,8},{1,9},{2,10},{3,11},{4,12},{5,13},{6,14},{7,15},{8,0},{9,1},... | collective-permute-start | bytes 1572872 | tf_op jit(solution)/shard_map/ppermute | solution.py:33
  92.3 23.9 %collective-permute-start.12 = (f32[256,512]{1,0:T(8,128)}, f32[256,512]{1,0:T(8,128)}, u32[]{:S(2)}, u32[]{:S(2)}) collective-permute-start(f32[256,512]{1,0:T(8,128)} %get-tuple-element.49), channel_id=1, source_target_pairs={{0,12},{1,13},{2,14},{3,15},{4,0},{5,1},{6,2},{7,3},{8,4},{9,5},{1... | collective-permute-start | bytes 1572872 | tf_op jit(solution)/shard_map/ppermute | solution.py:33
  95.7 12.7 %collective-permute-start.8 = (f32[128,512]{1,0:T(8,128)S(1)}, f32[128,512]{1,0:T(8,128)S(1)}, u32[]{:S(2)}, u32[]{:S(2)}) collective-permute-start(f32[128,512]{1,0:T(8,128)S(1)} %dynamic-slice_add_fusion.1), channel_id=1, source_target_pairs={{0,2},{1,3},{2,0},{3,1},{4,6},{5,7},{6,4},{7,5},{8,10},{9,11},{10,... | collective-permute-start | bytes 786440 | tf_op jit(solution)/shard_map/ppermute | solution.py:33
  109.7 13.2 %collective-permute-start.9 = (f32[128,512]{1,0:T(8,128)S(1)}, f32[128,512]{1,0:T(8,128)}, u32[]{:S(2)}, u32[]{:S(2)}) collective-permute-start(f32[128,512]{1,0:T(8,128)S(1)} %fusion.18), channel_id=1, source_target_pairs={{0,1},{1,0},{2,3},{3,2},{4,5},{5,4},{6,7},{7,6},{8,9},{9,8},{10,11... | collective-permute-start | bytes 786440 | tf_op jit(solution)/shard_map/ppermute | solution.py:33
  118.7 10.2 %collective-permute-start.16 = (f32[128,512]{1,0:T(8,128)}, f32[128,512]{1,0:T(8,128)}, u32[]{:S(2)}, u32[]{:S(2)}) collective-permute-start(f32[128,512]{1,0:T(8,128)} %constant_dynamic-slice_fusion), channel_id=1, source_target_pairs={{0,1},{1,0},{2,3},{3,2},{4,5},{5,4},{6,7},{7,6},{8,9},{9,8},{10,11... | collective-permute-start | bytes 786440 | tf_op jit(solution)/shard_map/ppermute | solution.py:33
  129.9 13.2 %collective-permute-start.17 = (f32[128,512]{1,0:T(8,128)S(1)}, f32[128,512]{1,0:T(8,128)S(1)}, u32[]{:S(2)}, u32[]{:S(2)}) collective-permute-start(f32[128,512]{1,0:T(8,128)S(1)} %dynamic-slice_add_fusion), channel_id=1, source_target_pairs={{0,2},{1,3},{2,0},{3,1},{4,6},{5,7},{6,4},{7,5},{8,10},{9,11},{10,... | collective-permute-start | bytes 786440 | tf_op jit(solution)/shard_map/ppermute | solution.py:33
  133.1 32.3 %collective-permute-start.13 = (f32[256,512]{1,0:T(8,128)}, f32[256,512]{1,0:T(8,128)S(1)}, u32[]{:S(2)}, u32[]{:S(2)}) collective-permute-start(f32[256,512]{1,0:T(8,128)} %maximum_select_fusion.2), channel_id=1, source_target_pairs={{0,4},{1,5},{2,6},{3,7},{4,8},{5,9},{6,10},{7,11},{8,12},{9,13},{1... | collective-permute-start | bytes 1572872 | tf_op jit(solution)/shard_map/ppermute | solution.py:33
  136.6 31.7 %collective-permute-start.14 = (f32[256,512]{1,0:T(8,128)}, f32[256,512]{1,0:T(8,128)}, u32[]{:S(2)}, u32[]{:S(2)}) collective-permute-start(f32[256,512]{1,0:T(8,128)} %maximum_select_fusion.2), channel_id=1, source_target_pairs={{0,8},{1,9},{2,10},{3,11},{4,12},{5,13},{6,14},{7,15},{8,0},{9,1},... | collective-permute-start | bytes 1572872 | tf_op jit(solution)/shard_map/ppermute | solution.py:33
  140.3 28.0 %collective-permute-start.15 = (f32[256,512]{1,0:T(8,128)}, f32[256,512]{1,0:T(8,128)}, u32[]{:S(2)}, u32[]{:S(2)}) collective-permute-start(f32[256,512]{1,0:T(8,128)} %maximum_select_fusion.2), channel_id=1, source_target_pairs={{0,12},{1,13},{2,14},{3,15},{4,0},{5,1},{6,2},{7,3},{8,4},{9,5},{1... | collective-permute-start | bytes 1572872 | tf_op jit(solution)/shard_map/ppermute | solution.py:33
  144.5 12.3 %collective-permute-start.18 = (f32[128,512]{1,0:T(8,128)S(1)}, f32[128,512]{1,0:T(8,128)}, u32[]{:S(2)}, u32[]{:S(2)}) collective-permute-start(f32[128,512]{1,0:T(8,128)S(1)} %fusion.20), channel_id=1, source_target_pairs={{0,1},{1,0},{2,3},{3,2},{4,5},{5,4},{6,7},{7,6},{8,9},{9,8},{10,11... | collective-permute-start | bytes 786440 | tf_op jit(solution)/shard_map/ppermute | solution.py:33
  158.0 17.8 %collective-permute-start.19 = (f32[256,512]{1,0:T(8,128)S(1)}, f32[256,512]{1,0:T(8,128)S(1)}, u32[]{:S(2)}, u32[]{:S(2)}) collective-permute-start(f32[256,512]{1,0:T(8,128)S(1)} %maximum_select_fusion.3), channel_id=1, source_target_pairs={{0,4},{1,5},{2,6},{3,7},{4,8},{5,9},{6,10},{7,11},{8,12},{9,13},{1... | collective-permute-start | bytes 1572872 | tf_op jit(solution)/shard_map/ppermute | solution.py:33
  161.7 24.3 %collective-permute-start.20 = (f32[256,512]{1,0:T(8,128)S(1)}, f32[256,512]{1,0:T(8,128)S(1)}, u32[]{:S(2)}, u32[]{:S(2)}) collective-permute-start(f32[256,512]{1,0:T(8,128)S(1)} %maximum_select_fusion.3), channel_id=1, source_target_pairs={{0,8},{1,9},{2,10},{3,11},{4,12},{5,13},{6,14},{7,15},{8,0},{9,1},... | collective-permute-start | bytes 1572872 | tf_op jit(solution)/shard_map/ppermute | solution.py:33
  165.4 22.7 %collective-permute-start.21 = (f32[256,512]{1,0:T(8,128)S(1)}, f32[256,512]{1,0:T(8,128)S(1)}, u32[]{:S(2)}, u32[]{:S(2)}) collective-permute-start(f32[256,512]{1,0:T(8,128)S(1)} %maximum_select_fusion.3), channel_id=1, source_target_pairs={{0,12},{1,13},{2,14},{3,15},{4,0},{5,1},{6,2},{7,3},{8,4},{9,5},{1... | collective-permute-start | bytes 1572872 | tf_op jit(solution)/shard_map/ppermute | solution.py:33
  171.9 2.0 copy-start.1
  188.6 1.9 copy-start.4
  192.6 6.1 %collective-permute-start.22 = (f32[512,1024]{1,0:T(8,128)S(1)}, f32[512,1024]{1,0:T(8,128)S(1)}, u32[]{:S(2)}, u32[]{:S(2)}) collective-permute-start(f32[512,1024]{1,0:T(8,128)S(1)} %get-tuple-element.68), channel_id=1, source_target_pairs={{0,16},{1,17},{2,18},{3,19},{4,20},{5,21},{6,22},{7,23},{8,24},{9,... | collective-permute-start | bytes 6291464 | tf_op jit(solution)/shard_map/ppermute | solution.py:33
  194.5 53.5 %collective-permute-start.23 = (f32[512,512]{1,0:T(8,128)S(1)}, f32[512,512]{1,0:T(8,128)S(1)}, u32[]{:S(2)}, u32[]{:S(2)}) collective-permute-start(f32[512,512]{1,0:T(8,128)S(1)} %fusion.35), channel_id=1, source_target_pairs={{0,32},{1,33},{2,34},{3,35},{4,36},{5,37},{6,38},{7,39},{8,40},{9,... | collective-permute-start | bytes 3145736 | tf_op jit(solution)/shard_map/ppermute | solution.py:33
  196.5 52.7 %collective-permute-start.24 = (f32[512,512]{1,0:T(8,128)S(1)}, f32[512,512]{1,0:T(8,128)S(1)}, u32[]{:S(2)}, u32[]{:S(2)}) collective-permute-start(f32[512,512]{1,0:T(8,128)S(1)} %fusion.35), channel_id=1, source_target_pairs={{16,32},{17,33},{18,34},{19,35},{20,36},{21,37},{22,38},{23,39},{2... | collective-permute-start | bytes 3145736 | tf_op jit(solution)/shard_map/ppermute | solution.py:33

commit v2 on v1

--- a/solution.py
+++ b/solution.py
@@ -8,7 +8,7 @@
 AXES = ("orb", "aux")
 X, ZL = 4, 4
 QUARTER, HALF_Q, COLS = 256, 128, 512
-ROWS = 256
+ROWS, CHUNK = 256, 256
 
 
 def route(step):
@@ -116,8 +116,8 @@
 
     one, two, three = base, base + 1, (base + 2) % ORB
 
+    other = move(own, SWAP)
     arrived = [move(own[c * ROWS : (c + 1) * ROWS], DOWN[c]) for c in (0, 1)]
-    other = move(own, SWAP)
     slab_one = jnp.where(first, own, other)
     slab_two = jnp.where(first, other, own)
     one_cols = cols_at(slab_one, at, COLS)
@@ -125,13 +125,11 @@
 
     inner_sends = send_x(pair_term(slab_one, slab_two, two_cols, one_cols))
     inner_parts = around(inner_sends)
-    inner_kept, inner_sent = halves(add_x(inner_parts))
-    inner_kept_next = inner_kept + move(inner_sent, ALONG[1])
 
     near_two = rows_at(slab_two, core * ROWS, ROWS)
     far_two = rows_at(slab_two, (1 - core) * ROWS, ROWS)
     near_two_cols, far_two_cols = cols_at(near_two, at, COLS), cols_at(far_two, at, COLS)
-    arrived = after(arrived, inner_sent, near_two, far_two, near_two_cols, far_two_cols)
+    arrived = after(arrived, inner_parts, near_two, far_two, near_two_cols, far_two_cols)
     near = jnp.where(first, arrived[0], arrived[1])
     far = move(near, SWAP)
     near_cols = cols_at(near, at, COLS)
@@ -142,35 +140,42 @@
     outer_sends = send_x(outer)
     outer_parts = around(outer_sends)
 
-    inner_kept = after(inner_kept_next, outer_sends)
-    inner_kept = inner_kept + move(inner_kept, ALONG[2])
-    inner_t = amplitude(inner_kept, one, two, at)
+    inner_kept, inner_sent = halves(add_x(after(inner_parts, outer_sends)))
+    inner_kept = inner_kept + move(inner_sent, ALONG[1])
+    inner_far = move(inner_kept, ALONG[2])
+
+    outer_kept, outer_sent = halves(add_x(after(outer_parts, inner_kept)))
+    outer_next = move(outer_sent, ALONG[1])
+    inner_t = amplitude(inner_kept + after(inner_far, outer_sent), one, two, at)
     inner_other = move(inner_t, ALONG[1])
+    outer_kept = outer_kept + after(outer_next, inner_t)
+    outer_far = move(outer_kept, ALONG[2])
+    inner_quarter = join(inner_t, after(inner_other, outer_kept))
+    inner_pieces = around([inner_quarter] * X)
+    outer_t = amplitude(outer_kept + after(outer_far, inner_quarter), two, three, at)
+    outer_other = move(outer_t, ALONG[1])
 
-    outer_kept, outer_sent = halves(add_x(after(outer_parts, inner_t)))
-    outer_other = move(outer_sent, ALONG[1])
-    inner_quarter = join(inner_t, after(inner_other, outer_sent))
-    inner_pieces = around([inner_quarter] * X)
-    outer_kept = outer_kept + after(outer_other, inner_quarter)
-    outer_kept = outer_kept + move(outer_kept, ALONG[2])
-    outer_t = amplitude(outer_kept, two, three, at)
-    outer_quarter = join(outer_t, move(outer_t, ALONG[1]))
-    outer_pieces = around([outer_quarter] * X)
+    spans = [slice(w * CHUNK, (w + 1) * CHUNK) for w in range(COLS // CHUNK)]
+    quarters = [join(outer_t[:, w], outer_other[:, w]) for w in spans]
+    pieces = [around([q] * X) for q in quarters]
+    outer_all, incoming, earlier = [], [[], []], quarters
+    for n in range(len(spans)):
+        outer_all.append(in_order(after(pieces[n], earlier)))
+        outgoing = dot(slab_two, outer_all[n], 1, 0)
+        for c in (0, 1):
+            incoming[c].append(move(outgoing, UP[c]))
+        earlier = outgoing
 
-    inner_all = in_order(after(inner_pieces, outer_quarter))
+    inner_all = in_order(after(inner_pieces, outgoing))
     to_one = dot(two_cols, inner_all, 1, 1)
     to_two = dot(slab_one, inner_all, 1, 0)
-
-    outer_all = in_order(after(outer_pieces, to_one, to_two))
-    outgoing = dot(slab_two, outer_all, 1, 0)
-    incoming = [move(outgoing, UP[c]) for c in (0, 1)]
-
     three_cols = jnp.where(
         first,
         jnp.concatenate([near_cols, far_cols], 0),
         jnp.concatenate([far_cols, near_cols], 0),
     )
-    beyond = dot(three_cols, after(outer_all, outgoing), 1, 1)
+    three_cols, outer_all = after((three_cols, outer_all), outgoing)
+    beyond = sum(dot(three_cols[:, w], t, 1, 1) for w, t in zip(spans, outer_all))
     blank = jnp.zeros_like(to_two)
     to_two = beyond + jnp.where(
         first,
@@ -179,7 +184,8 @@
     )
     crossed = move(jnp.where(first, to_two, to_one), SWAP)
     density = jnp.where(first, to_one, to_two) + crossed
-    density = density + jnp.concatenate(after(incoming, density), 1)
+    incoming = after(incoming, density)
+    density = density + jnp.concatenate(incoming[0] + incoming[1], 1)
     return density[None]
 
 

time: 252 us -> 286 us (1.13)
  the two profiles are of different devices: /device:TPU:152 before, /device:TPU:56 now
where the time goes in v2:
time: 286 us; the launch traced here: 284 us
  waiting for transfers between devices  116 us (41%)
  starting transfers between devices  107 us (37%)
  other arithmetic  20.9 us (7%)
  local copies, waits for them, and re-layouts  20.4 us (7%)
  matrix products  19.2 us (7%)
    ppermute x30, waiting for transfers between devices, move(): return lax.ppermute(block, AXES, pairs)  116 us
    ppermute x30, starting transfers between devices, move(): return lax.ppermute(block, AXES, pairs)  107 us
    dot_general x12, matrix products, dot(): lax.dot_general(a, b, (((da,), (db,)), ((), ())), precision=lax.Precision...  19.2 us
  transfers between devices with their start and end apart: 30, of which 13 were waited for; matrix products, arithmetic and copies ran while one was open for 13% of the time, Pallas kernels for 0%

profile of v2, /device:TPU:56, one launch (start us, length us, event | category | flops | bytes accessed | tf_op | source)
XLA Modules:
  0.0 284.3 jit_solution(687453873382215292)
XLA Ops:
  0.0 1.9 collective-permute-start
  1.9 3.1 %slice_bitcast_fusion = (f32[256,1024]{1,0:T(8,128)}, f32[256,1024]{1,0:T(8,128)}) fusion(f32[1,512,1024]{2,1,0:T(8,128)} %param.4), kind=kLoop, calls=%fused_computation.8 | loop fusion | bytes 4194304 | tf_op jit(solution)/shard_map/slice | solution.py:120
  5.1 11.7 %collective-permute-start.4 = (f32[256,1024]{1,0:T(8,128)}, f32[256,1024]{1,0:T(8,128)S(1)}, u32[]{:S(2)}, u32[]{:S(2)}) collective-permute-start(f32[256,1024]{1,0:T(8,128)} %get-tuple-element.84), channel_id=1, source_target_pairs={{0,480},{1,481},{2,482},{3,483},{4,484},{5,485},{6,486},{7,487},{8... | collective-permute-start | bytes 3145736 | tf_op jit(solution)/shard_map/ppermute | solution.py:33
  16.8 2.3 collective-permute-start.5
  19.0 2.9 %broadcast_select_fusion.2 = (f32[512,1024]{1,0:T(8,128)S(1)}, f32[512,1024]{1,0:T(8,128)S(1)}) fusion(f32[512,1024]{1,0:T(8,128)} %collective-permute-done, pred[]{:T(512)S(6)} %eq.34, f32[1,512,1024]{2,1,0:T(8,128)} %param.4), kind=kLoop, calls=%fused_computation.14 | loop fusion | flops 1048576 | bytes 8388609 | tf_op jit(solution)/shard_map/jit(_where)/select_n | solution.py:122
  21.9 1.8 fusion.7
  23.8 1.9 multiply_subtract_fusion.1
  25.7 1.4 constant_dynamic-slice_fusion.10
  27.1 3.4 %collective-permute-start.1 = (f32[256,512]{1,0:T(8,128)}, f32[256,512]{1,0:T(8,128)}, u32[]{:S(2)}, u32[]{:S(2)}) collective-permute-start(f32[256,512]{1,0:T(8,128)} %get-tuple-element.87), channel_id=1, source_target_pairs={{0,4},{1,5},{2,6},{3,7},{4,8},{5,9},{6,10},{7,11},{8,12},{9,13},{1... | collective-permute-start | bytes 1572872 | tf_op jit(solution)/shard_map/ppermute | solution.py:33
  30.5 4.6 %collective-permute-start.2 = (f32[256,512]{1,0:T(8,128)}, f32[256,512]{1,0:T(8,128)}, u32[]{:S(2)}, u32[]{:S(2)}) collective-permute-start(f32[256,512]{1,0:T(8,128)} %get-tuple-element.86), channel_id=1, source_target_pairs={{0,8},{1,9},{2,10},{3,11},{4,12},{5,13},{6,14},{7,15},{8,0},{9,1},... | collective-permute-start | bytes 1572872 | tf_op jit(solution)/shard_map/ppermute | solution.py:33
  35.2 3.3 %collective-permute-start.3 = (f32[256,512]{1,0:T(8,128)}, f32[256,512]{1,0:T(8,128)}, u32[]{:S(2)}, u32[]{:S(2)}) collective-permute-start(f32[256,512]{1,0:T(8,128)} %get-tuple-element.85), channel_id=1, source_target_pairs={{0,12},{1,13},{2,14},{3,15},{4,0},{5,1},{6,2},{7,3},{8,4},{9,5},{1... | collective-permute-start | bytes 1572872 | tf_op jit(solution)/shard_map/ppermute | solution.py:33
  38.6 1.4 fusion.23
  39.9 1.6 constant_dynamic-slice_fusion.8
  41.5 18.0 %collective-permute-done.5 = f32[256,1024]{1,0:T(8,128)} collective-permute-done((f32[256,1024]{1,0:T(8,128)}, f32[256,1024]{1,0:T(8,128)}, u32[]{:S(2)}, u32[]{:S(2)}) %collective-permute-start.5) | collective-permute-done | bytes 1048608 | tf_op jit(solution)/shard_map/ppermute | solution.py:33
  59.6 1.4 broadcast_select_fusion.3
  61.0 1.9 collective-permute-start.6
  63.8 2.3 fusion.28
  69.4 2.5 subtract_add_fusion
  72.0 1.3 constant_dynamic-slice_fusion.2
  73.3 5.1 %collective-permute-start.10 = (f32[256,512]{1,0:T(8,128)}, f32[256,512]{1,0:T(8,128)}, u32[]{:S(2)}, u32[]{:S(2)}) collective-permute-start(f32[256,512]{1,0:T(8,128)} %get-tuple-element.76), channel_id=1, source_target_pairs={{0,8},{1,9},{2,10},{3,11},{4,12},{5,13},{6,14},{7,15},{8,0},{9,1},... | collective-permute-start | bytes 1572872 | tf_op jit(solution)/shard_map/ppermute | solution.py:33
  78.4 3.1 %collective-permute-start.11 = (f32[256,512]{1,0:T(8,128)}, f32[256,512]{1,0:T(8,128)}, u32[]{:S(2)}, u32[]{:S(2)}) collective-permute-start(f32[256,512]{1,0:T(8,128)} %get-tuple-element.75), channel_id=1, source_target_pairs={{0,12},{1,13},{2,14},{3,15},{4,0},{5,1},{6,2},{7,3},{8,4},{9,5},{1... | collective-permute-start | bytes 1572872 | tf_op jit(solution)/shard_map/ppermute | solution.py:33
  81.4 2.8 collective-permute-start.9
  84.2 1.6 add_add_fusion.1
  85.9 10.1 %collective-permute-start.7 = (f32[128,512]{1,0:T(8,128)S(1)}, f32[128,512]{1,0:T(8,128)}, u32[]{:S(2)}, u32[]{:S(2)}) collective-permute-start(f32[128,512]{1,0:T(8,128)S(1)} %constant_dynamic-slice_fusion.1), channel_id=1, source_target_pairs={{0,1},{1,0},{2,3},{3,2},{4,5},{5,4},{6,7},{7,6},{8,9},{9,8},{10,11... | collective-permute-start | bytes 786440 | tf_op jit(solution)/shard_map/ppermute | solution.py:33
  97.4 4.4 %collective-permute-done.7 = f32[128,512]{1,0:T(8,128)} collective-permute-done((f32[128,512]{1,0:T(8,128)S(1)}, f32[128,512]{1,0:T(8,128)}, u32[]{:S(2)}, u32[]{:S(2)}) %collective-permute-start.7) | collective-permute-done | bytes 262176 | tf_op jit(solution)/shard_map/ppermute | solution.py:33
  102.7 8.8 %collective-permute-start.8 = (f32[128,512]{1,0:T(8,128)S(1)}, f32[128,512]{1,0:T(8,128)S(1)}, u32[]{:S(2)}, u32[]{:S(2)}) collective-permute-start(f32[128,512]{1,0:T(8,128)S(1)} %dynamic-slice_add_fusion.1), channel_id=1, source_target_pairs={{0,2},{1,3},{2,0},{3,1},{4,6},{5,7},{6,4},{7,5},{8,10},{9,11},{10,... | collective-permute-start | bytes 786440 | tf_op jit(solution)/shard_map/ppermute | solution.py:33
  111.5 1.7 add_add_fusion
  114.8 2.2 collective-permute-start.13
  118.4 3.4 %collective-permute-done.8 = f32[128,512]{1,0:T(8,128)S(1)} collective-permute-done((f32[128,512]{1,0:T(8,128)S(1)}, f32[128,512]{1,0:T(8,128)S(1)}, u32[]{:S(2)}, u32[]{:S(2)}) %collective-permute-start.8) | collective-permute-done | bytes 262176 | tf_op jit(solution)/shard_map/ppermute | solution.py:33
  121.8 2.0 fusion.13
  123.8 2.0 collective-permute-start.12
  125.9 1.6 collective-permute-done.13
  128.5 3.6 %collective-permute-start.17 = (f32[128,512]{1,0:T(8,128)S(1)}, f32[128,512]{1,0:T(8,128)}, u32[]{:S(2)}, u32[]{:S(2)}) collective-permute-start(f32[128,512]{1,0:T(8,128)S(1)} %dynamic-slice_add_fusion), channel_id=1, source_target_pairs={{0,2},{1,3},{2,0},{3,1},{4,6},{5,7},{6,4},{7,5},{8,10},{9,11},{10,... | collective-permute-start | bytes 786440 | tf_op jit(solution)/shard_map/ppermute | solution.py:33
  133.3 1.4 collective-permute-done.12
  134.7 2.1 maximum_select_fusion.1
  136.8 8.5 %collective-permute-done.17 = f32[128,512]{1,0:T(8,128)} collective-permute-done((f32[128,512]{1,0:T(8,128)S(1)}, f32[128,512]{1,0:T(8,128)}, u32[]{:S(2)}, u32[]{:S(2)}) %collective-permute-start.17) | collective-permute-done | bytes 262176 | tf_op jit(solution)/shard_map/ppermute | solution.py:33
  145.3 2.3 fusion.15
  147.5 1.9 collective-permute-start.18
  149.5 7.9 %collective-permute-done.18 = f32[128,512]{1,0:T(8,128)S(1)} collective-permute-done((f32[128,512]{1,0:T(8,128)S(1)}, f32[128,512]{1,0:T(8,128)S(1)}, u32[]{:S(2)}, u32[]{:S(2)}) %collective-permute-start.18) | collective-permute-done | bytes 262176 | tf_op jit(solution)/shard_map/ppermute | solution.py:33
  158.0 2.4 collective-permute-start.22
  160.4 5.1 %collective-permute-start.23 = (f32[256,256]{1,0:T(8,128)S(1)}, f32[256,256]{1,0:T(8,128)}, u32[]{:S(2)}, u32[]{:S(2)}) collective-permute-start(f32[256,256]{1,0:T(8,128)S(1)} %maximum_select_fusion.3), channel_id=1, source_target_pairs={{0,8},{1,9},{2,10},{3,11},{4,12},{5,13},{6,14},{7,15},{8,0},{9,1},... | collective-permute-start | bytes 786440 | tf_op jit(solution)/shard_map/ppermute | solution.py:33
  165.6 1.9 collective-permute-start.24
  168.6 3.9 %collective-permute-start.14 = (f32[256,512]{1,0:T(8,128)S(1)}, f32[256,512]{1,0:T(8,128)S(1)}, u32[]{:S(2)}, u32[]{:S(2)}) collective-permute-start(f32[256,512]{1,0:T(8,128)S(1)} %copy-done.6), channel_id=1, source_target_pairs={{0,4},{1,5},{2,6},{3,7},{4,8},{5,9},{6,10},{7,11},{8,12},{9,13},{1... | collective-permute-start | bytes 1572872 | tf_op jit(solution)/shard_map/ppermute | solution.py:33
  172.5 2.4 collective-permute-start.15
  175.0 3.5 %collective-permute-start.19 = (f32[256,256]{1,0:T(8,128)S(1)}, f32[256,256]{1,0:T(8,128)S(1)}, u32[]{:S(2)}, u32[]{:S(2)}) collective-permute-start(f32[256,256]{1,0:T(8,128)S(1)} %maximum_select_fusion.2), channel_id=1, source_target_pairs={{0,4},{1,5},{2,6},{3,7},{4,8},{5,9},{6,10},{7,11},{8,12},{9,13},{1... | collective-permute-start | bytes 786440 | tf_op jit(solution)/shard_map/ppermute | solution.py:33
  178.5 4.4 %collective-permute-start.20 = (f32[256,256]{1,0:T(8,128)S(1)}, f32[256,256]{1,0:T(8,128)S(1)}, u32[]{:S(2)}, u32[]{:S(2)}) collective-permute-start(f32[256,256]{1,0:T(8,128)S(1)} %maximum_select_fusion.2), channel_id=1, source_target_pairs={{0,8},{1,9},{2,10},{3,11},{4,12},{5,13},{6,14},{7,15},{8,0},{9,1},... | collective-permute-start | bytes 786440 | tf_op jit(solution)/shard_map/ppermute | solution.py:33
  182.9 3.5 %collective-permute-start.21 = (f32[256,256]{1,0:T(8,128)S(1)}, f32[256,256]{1,0:T(8,128)S(1)}, u32[]{:S(2)}, u32[]{:S(2)}) collective-permute-start(f32[256,256]{1,0:T(8,128)S(1)} %maximum_select_fusion.2), channel_id=1, source_target_pairs={{0,12},{1,13},{2,14},{3,15},{4,0},{5,1},{6,2},{7,3},{8,4},{9,5},{1... | collective-permute-start | bytes 786440 | tf_op jit(solution)/shard_map/ppermute | solution.py:33
  190.5 17.6 %collective-permute-done.19 = f32[256,256]{1,0:T(8,128)S(1)} collective-permute-done((f32[256,256]{1,0:T(8,128)S(1)}, f32[256,256]{1,0:T(8,128)S(1)}, u32[]{:S(2)}, u32[]{:S(2)}) %collective-permute-start.19) | collective-permute-done | bytes 262176 | tf_op jit(solution)/shard_map/ppermute | solution.py:33
  208.2 1.9 collective-permute-start.16
  211.4 7.9 %collective-permute-done.16 = f32[256,512]{1,0:T(8,128)S(1)} collective-permute-done((f32[256,512]{1,0:T(8,128)S(1)}, f32[256,512]{1,0:T(8,128)S(1)}, u32[]{:S(2)}, u32[]{:S(2)}) %collective-permute-start.16) | collective-permute-done | bytes 524320 | tf_op jit(solution)/shard_map/ppermute | solution.py:33
  219.7 1.4 copy-done.1
  221.1 1.9 fusion.32
  223.0 2.0 fusion.5
  226.1 1.5 broadcast_select_fusion
  227.5 1.9 collective-permute-start.25
  229.5 2.4 collective-permute-start.27
  231.9 1.3 collective-permute-start.29
  233.2 2.5 collective-permute-start.26
  235.7 1.3 collective-permute-start.28
  237.8 19.6 %collective-permute-done.27 = f32[512,256]{1,0:T(8,128)S(1)} collective-permute-done((f32[512,256]{1,0:T(8,128)S(1)}, f32[512,256]{1,0:T(8,128)S(1)}, u32[]{:S(2)}, u32[]{:S(2)}) %collective-permute-start.27) | collective-permute-done | bytes 524320 | tf_op jit(solution)/shard_map/ppermute | solution.py:33
  257.4 7.1 %collective-permute-done.29 = f32[512,256]{1,0:T(8,128)S(1)} collective-permute-done((f32[512,256]{1,0:T(8,128)S(1)}, f32[512,256]{1,0:T(8,128)S(1)}, u32[]{:S(2)}, u32[]{:S(2)}) %collective-permute-start.29) | collective-permute-done | bytes 524320 | tf_op jit(solution)/shard_map/ppermute | solution.py:33
  264.4 14.5 %collective-permute-done.26 = f32[512,256]{1,0:T(8,128)S(1)} collective-permute-done((f32[512,256]{1,0:T(8,128)S(1)}, f32[512,256]{1,0:T(8,128)S(1)}, u32[]{:S(2)}, u32[]{:S(2)}) %collective-permute-start.26) | collective-permute-done | bytes 524320 | tf_op jit(solution)/shard_map/ppermute | solution.py:33
  278.9 3.7 %collective-permute-done.28 = f32[512,256]{1,0:T(8,128)S(1)} collective-permute-done((f32[512,256]{1,0:T(8,128)S(1)}, f32[512,256]{1,0:T(8,128)S(1)}, u32[]{:S(2)}, u32[]{:S(2)}) %collective-permute-start.28) | collective-permute-done | bytes 524320 | tf_op jit(solution)/shard_map/ppermute | solution.py:33
  282.6 1.6 fusion
  (86 shorter events, 20.8 us)
Async XLA Ops:
  0.0 19.0 %collective-permute-start = (f32[512,1024]{1,0:T(8,128)}, f32[512,1024]{1,0:T(8,128)}, u32[]{:S(2)}, u32[]{:S(2)}) collective-permute-start(f32[512,1024]{1,0:T(8,128)} %bitcast.34), channel_id=1, source_target_pairs={{0,16},{1,17},{2,18},{3,19},{4,20},{5,21},{6,22},{7,23},{8,24},{9,... | collective-permute-start | bytes 6291464 | tf_op jit(solution)/shard_map/ppermute | solution.py:33
  5.1 36.5 %collective-permute-start.4 = (f32[256,1024]{1,0:T(8,128)}, f32[256,1024]{1,0:T(8,128)S(1)}, u32[]{:S(2)}, u32[]{:S(2)}) collective-permute-start(f32[256,1024]{1,0:T(8,128)} %get-tuple-element.84), channel_id=1, source_target_pairs={{0,480},{1,481},{2,482},{3,483},{4,484},{5,485},{6,486},{7,487},{8... | collective-permute-start | bytes 3145736 | tf_op jit(solution)/shard_map/ppermute | solution.py:33
  16.8 42.8 %collective-permute-start.5 = (f32[256,1024]{1,0:T(8,128)}, f32[256,1024]{1,0:T(8,128)}, u32[]{:S(2)}, u32[]{:S(2)}) collective-permute-start(f32[256,1024]{1,0:T(8,128)} %get-tuple-element.83), channel_id=1, source_target_pairs={{0,496},{1,497},{2,498},{3,499},{4,500},{5,501},{6,502},{7,503},{8... | collective-permute-start | bytes 3145736 | tf_op jit(solution)/shard_map/ppermute | solution.py:33
  21.9 1.9 copy-start
  27.1 32.4 %collective-permute-start.1 = (f32[256,512]{1,0:T(8,128)}, f32[256,512]{1,0:T(8,128)}, u32[]{:S(2)}, u32[]{:S(2)}) collective-permute-start(f32[256,512]{1,0:T(8,128)} %get-tuple-element.87), channel_id=1, source_target_pairs={{0,4},{1,5},{2,6},{3,7},{4,8},{5,9},{6,10},{7,11},{8,12},{9,13},{1... | collective-permute-start | bytes 1572872 | tf_op jit(solution)/shard_map/ppermute | solution.py:33
  30.5 29.1 %collective-permute-start.2 = (f32[256,512]{1,0:T(8,128)}, f32[256,512]{1,0:T(8,128)}, u32[]{:S(2)}, u32[]{:S(2)}) collective-permute-start(f32[256,512]{1,0:T(8,128)} %get-tuple-element.86), channel_id=1, source_target_pairs={{0,8},{1,9},{2,10},{3,11},{4,12},{5,13},{6,14},{7,15},{8,0},{9,1},... | collective-permute-start | bytes 1572872 | tf_op jit(solution)/shard_map/ppermute | solution.py:33
  35.2 24.4 %collective-permute-start.3 = (f32[256,512]{1,0:T(8,128)}, f32[256,512]{1,0:T(8,128)}, u32[]{:S(2)}, u32[]{:S(2)}) collective-permute-start(f32[256,512]{1,0:T(8,128)} %get-tuple-element.85), channel_id=1, source_target_pairs={{0,12},{1,13},{2,14},{3,15},{4,0},{5,1},{6,2},{7,3},{8,4},{9,5},{1... | collective-permute-start | bytes 1572872 | tf_op jit(solution)/shard_map/ppermute | solution.py:33
  41.5 18.1 %copy-start.10 = (f32[256,1024]{1,0:T(8,128)}, f32[256,1024]{1,0:T(8,128)S(1)}, u32[]{:S(2)}) copy-start(f32[256,1024]{1,0:T(8,128)S(1)} %collective-permute-done.4) | copy-start | bytes 3145732
  61.0 6.3 %collective-permute-start.6 = (f32[256,1024]{1,0:T(8,128)S(1)}, f32[256,1024]{1,0:T(8,128)}, u32[]{:S(2)}, u32[]{:S(2)}) collective-permute-start(f32[256,1024]{1,0:T(8,128)S(1)} %broadcast_select_fusion.3), channel_id=1, source_target_pairs={{0,16},{1,17},{2,18},{3,19},{4,20},{5,21},{6,22},{7,23},{8,24},{9,... | collective-permute-start | bytes 3145736 | tf_op jit(solution)/shard_map/ppermute | solution.py:33
  63.0 0.8 copy-start.2
  63.8 2.3 copy-start.8
  66.1 2.2 copy-start.4
  68.4 1.0 copy-start.9
  72.0 12.3 %copy-start.7 = (f32[256,512]{1,0:T(8,128)S(1)}, f32[256,512]{1,0:T(8,128)}, u32[]{:S(2)}) copy-start(f32[256,512]{1,0:T(8,128)} %get-tuple-element.42) | copy-start | bytes 1572868
  73.3 22.7 %copy-start.12 = (s32[32]{0:T(128)S(1)}, s32[32]{0:T(128)}, u32[]{:S(2)}) copy-start(s32[32]{0:T(128)} %param.7) | copy-start | bytes 388
  73.3 38.2 %collective-permute-start.10 = (f32[256,512]{1,0:T(8,128)}, f32[256,512]{1,0:T(8,128)}, u32[]{:S(2)}, u32[]{:S(2)}) collective-permute-start(f32[256,512]{1,0:T(8,128)} %get-tuple-element.76), channel_id=1, source_target_pairs={{0,8},{1,9},{2,10},{3,11},{4,12},{5,13},{6,14},{7,15},{8,0},{9,1},... | collective-permute-start | bytes 1572872 | tf_op jit(solution)/shard_map/ppermute | solution.py:33
  78.4 33.2 %collective-permute-start.11 = (f32[256,512]{1,0:T(8,128)}, f32[256,512]{1,0:T(8,128)}, u32[]{:S(2)}, u32[]{:S(2)}) collective-permute-start(f32[256,512]{1,0:T(8,128)} %get-tuple-element.75), channel_id=1, source_target_pairs={{0,12},{1,13},{2,14},{3,15},{4,0},{5,1},{6,2},{7,3},{8,4},{9,5},{1... | collective-permute-start | bytes 1572872 | tf_op jit(solution)/shard_map/ppermute | solution.py:33
  81.4 30.1 %collective-permute-start.9 = (f32[256,512]{1,0:T(8,128)}, f32[256,512]{1,0:T(8,128)}, u32[]{:S(2)}, u32[]{:S(2)}) collective-permute-start(f32[256,512]{1,0:T(8,128)} %get-tuple-element.77), channel_id=1, source_target_pairs={{0,4},{1,5},{2,6},{3,7},{4,8},{5,9},{6,10},{7,11},{8,12},{9,13},{1... | collective-permute-start | bytes 1572872 | tf_op jit(solution)/shard_map/ppermute | solution.py:33
  85.9 31.8 %copy-start.14 = (f32[1024]{0:T(1024)S(1)}, f32[1024]{0:T(1024)}, u32[]{:S(2)}) copy-start(f32[1024]{0:T(1024)} %param.6) | copy-start | bytes 12292
  85.9 31.9 %copy-start.13 = (f32[32]{0:T(128)S(1)}, f32[32]{0:T(128)}, u32[]{:S(2)}) copy-start(f32[32]{0:T(128)} %param.5) | copy-start | bytes 388
  85.9 15.8 %collective-permute-start.7 = (f32[128,512]{1,0:T(8,128)S(1)}, f32[128,512]{1,0:T(8,128)}, u32[]{:S(2)}, u32[]{:S(2)}) collective-permute-start(f32[128,512]{1,0:T(8,128)S(1)} %constant_dynamic-slice_fusion.1), channel_id=1, source_target_pairs={{0,1},{1,0},{2,3},{3,2},{4,5},{5,4},{6,7},{7,6},{8,9},{9,8},{10,11... | collective-permute-start | bytes 786440 | tf_op jit(solution)/shard_map/ppermute | solution.py:33
  102.7 19.1 %collective-permute-start.8 = (f32[128,512]{1,0:T(8,128)S(1)}, f32[128,512]{1,0:T(8,128)S(1)}, u32[]{:S(2)}, u32[]{:S(2)}) collective-permute-start(f32[128,512]{1,0:T(8,128)S(1)} %dynamic-slice_add_fusion.1), channel_id=1, source_target_pairs={{0,2},{1,3},{2,0},{3,1},{4,6},{5,7},{6,4},{7,5},{8,10},{9,11},{10,... | collective-permute-start | bytes 786440 | tf_op jit(solution)/shard_map/ppermute | solution.py:33
  113.3 0.8 copy-start.5
  114.8 12.7 %collective-permute-start.13 = (f32[128,512]{1,0:T(8,128)}, f32[128,512]{1,0:T(8,128)}, u32[]{:S(2)}, u32[]{:S(2)}) collective-permute-start(f32[128,512]{1,0:T(8,128)} %constant_dynamic-slice_fusion), channel_id=1, source_target_pairs={{0,1},{1,0},{2,3},{3,2},{4,5},{5,4},{6,7},{7,6},{8,9},{9,8},{10,11... | collective-permute-start | bytes 786440 | tf_op jit(solution)/shard_map/ppermute | solution.py:33
  123.8 43.7 %copy-start.3 = (f32[256,512]{1,0:T(8,128)S(1)}, f32[256,512]{1,0:T(8,128)}, u32[]{:S(2)}) copy-start(f32[256,512]{1,0:T(8,128)} %copy-done.2) | copy-start | bytes 1572868
  123.8 10.9 %collective-permute-start.12 = (f32[128,512]{1,0:T(8,128)}, f32[128,512]{1,0:T(8,128)}, u32[]{:S(2)}, u32[]{:S(2)}) collective-permute-start(f32[128,512]{1,0:T(8,128)} %fusion.13), channel_id=1, source_target_pairs={{0,1},{1,0},{2,3},{3,2},{4,5},{5,4},{6,7},{7,6},{8,9},{9,8},{10,11... | collective-permute-start | bytes 786440 | tf_op jit(solution)/shard_map/ppermute | solution.py:33
  128.5 16.7 %collective-permute-start.17 = (f32[128,512]{1,0:T(8,128)S(1)}, f32[128,512]{1,0:T(8,128)}, u32[]{:S(2)}, u32[]{:S(2)}) collective-permute-start(f32[128,512]{1,0:T(8,128)S(1)} %dynamic-slice_add_fusion), channel_id=1, source_target_pairs={{0,2},{1,3},{2,0},{3,1},{4,6},{5,7},{6,4},{7,5},{8,10},{9,11},{10,... | collective-permute-start | bytes 786440 | tf_op jit(solution)/shard_map/ppermute | solution.py:33
  147.5 9.8 %collective-permute-start.18 = (f32[128,512]{1,0:T(8,128)S(1)}, f32[128,512]{1,0:T(8,128)S(1)}, u32[]{:S(2)}, u32[]{:S(2)}) collective-permute-start(f32[128,512]{1,0:T(8,128)S(1)} %fusion.15), channel_id=1, source_target_pairs={{0,1},{1,0},{2,3},{3,2},{4,5},{5,4},{6,7},{7,6},{8,9},{9,8},{10,11... | collective-permute-start | bytes 786440 | tf_op jit(solution)/shard_map/ppermute | solution.py:33
  158.0 16.9 %collective-permute-start.22 = (f32[256,256]{1,0:T(8,128)S(1)}, f32[256,256]{1,0:T(8,128)}, u32[]{:S(2)}, u32[]{:S(2)}) collective-permute-start(f32[256,256]{1,0:T(8,128)S(1)} %maximum_select_fusion.3), channel_id=1, source_target_pairs={{0,4},{1,5},{2,6},{3,7},{4,8},{5,9},{6,10},{7,11},{8,12},{9,13},{1... | collective-permute-start | bytes 786440 | tf_op jit(solution)/shard_map/ppermute | solution.py:33
  160.4 18.1 %collective-permute-start.23 = (f32[256,256]{1,0:T(8,128)S(1)}, f32[256,256]{1,0:T(8,128)}, u32[]{:S(2)}, u32[]{:S(2)}) collective-permute-start(f32[256,256]{1,0:T(8,128)S(1)} %maximum_select_fusion.3), channel_id=1, source_target_pairs={{0,8},{1,9},{2,10},{3,11},{4,12},{5,13},{6,14},{7,15},{8,0},{9,1},... | collective-permute-start | bytes 786440 | tf_op jit(solution)/shard_map/ppermute | solution.py:33
  165.6 17.3 %collective-permute-start.24 = (f32[256,256]{1,0:T(8,128)S(1)}, f32[256,256]{1,0:T(8,128)}, u32[]{:S(2)}, u32[]{:S(2)}) collective-permute-start(f32[256,256]{1,0:T(8,128)S(1)} %maximum_select_fusion.3), channel_id=1, source_target_pairs={{0,12},{1,13},{2,14},{3,15},{4,0},{5,1},{6,2},{7,3},{8,4},{9,5},{1... | collective-permute-start | bytes 786440 | tf_op jit(solution)/shard_map/ppermute | solution.py:33
  167.6 1.0 copy-start.6
  167.6 7.3 %copy-start.11 = (f32[128,256]{1,0:T(8,128)S(1)}, f32[128,256]{1,0:T(8,128)}, u32[]{:S(2)}) copy-start(f32[128,256]{1,0:T(8,128)} %get-tuple-element.92) | copy-start | bytes 393220
  168.6 42.7 %collective-permute-start.14 = (f32[256,512]{1,0:T(8,128)S(1)}, f32[256,512]{1,0:T(8,128)S(1)}, u32[]{:S(2)}, u32[]{:S(2)}) collective-permute-start(f32[256,512]{1,0:T(8,128)S(1)} %copy-done.6), channel_id=1, source_target_pairs={{0,4},{1,5},{2,6},{3,7},{4,8},{5,9},{6,10},{7,11},{8,12},{9,13},{1... | collective-permute-start | bytes 1572872 | tf_op jit(solution)/shard_map/ppermute | solution.py:33
  172.5 38.8 %collective-permute-start.15 = (f32[256,512]{1,0:T(8,128)S(1)}, f32[256,512]{1,0:T(8,128)S(1)}, u32[]{:S(2)}, u32[]{:S(2)}) collective-permute-start(f32[256,512]{1,0:T(8,128)S(1)} %copy-done.6), channel_id=1, source_target_pairs={{0,8},{1,9},{2,10},{3,11},{4,12},{5,13},{6,14},{7,15},{8,0},{9,1},... | collective-permute-start | bytes 1572872 | tf_op jit(solution)/shard_map/ppermute | solution.py:33
  175.0 33.2 %collective-permute-start.19 = (f32[256,256]{1,0:T(8,128)S(1)}, f32[256,256]{1,0:T(8,128)S(1)}, u32[]{:S(2)}, u32[]{:S(2)}) collective-permute-start(f32[256,256]{1,0:T(8,128)S(1)} %maximum_select_fusion.2), channel_id=1, source_target_pairs={{0,4},{1,5},{2,6},{3,7},{4,8},{5,9},{6,10},{7,11},{8,12},{9,13},{1... | collective-permute-start | bytes 786440 | tf_op jit(solution)/shard_map/ppermute | solution.py:33
  178.5 31.6 %collective-permute-start.20 = (f32[256,256]{1,0:T(8,128)S(1)}, f32[256,256]{1,0:T(8,128)S(1)}, u32[]{:S(2)}, u32[]{:S(2)}) collective-permute-start(f32[256,256]{1,0:T(8,128)S(1)} %maximum_select_fusion.2), channel_id=1, source_target_pairs={{0,8},{1,9},{2,10},{3,11},{4,12},{5,13},{6,14},{7,15},{8,0},{9,1},... | collective-permute-start | bytes 786440 | tf_op jit(solution)/shard_map/ppermute | solution.py:33
  182.9 27.2 %collective-permute-start.21 = (f32[256,256]{1,0:T(8,128)S(1)}, f32[256,256]{1,0:T(8,128)S(1)}, u32[]{:S(2)}, u32[]{:S(2)}) collective-permute-start(f32[256,256]{1,0:T(8,128)S(1)} %maximum_select_fusion.2), channel_id=1, source_target_pairs={{0,12},{1,13},{2,14},{3,15},{4,0},{5,1},{6,2},{7,3},{8,4},{9,5},{1... | collective-permute-start | bytes 786440 | tf_op jit(solution)/shard_map/ppermute | solution.py:33
  208.2 11.1 %collective-permute-start.16 = (f32[256,512]{1,0:T(8,128)S(1)}, f32[256,512]{1,0:T(8,128)S(1)}, u32[]{:S(2)}, u32[]{:S(2)}) collective-permute-start(f32[256,512]{1,0:T(8,128)S(1)} %copy-done.6), channel_id=1, source_target_pairs={{0,12},{1,13},{2,14},{3,15},{4,0},{5,1},{6,2},{7,3},{8,4},{9,5},{1... | collective-permute-start | bytes 1572872 | tf_op jit(solution)/shard_map/ppermute | solution.py:33
  219.5 1.6 copy-start.1
  227.5 9.5 %collective-permute-start.25 = (f32[512,1024]{1,0:T(8,128)S(1)}, f32[512,1024]{1,0:T(8,128)S(1)}, u32[]{:S(2)}, u32[]{:S(2)}) collective-permute-start(f32[512,1024]{1,0:T(8,128)S(1)} %get-tuple-element.99), channel_id=1, source_target_pairs={{0,16},{1,17},{2,18},{3,19},{4,20},{5,21},{6,22},{7,23},{8,24},{9,... | collective-permute-start | bytes 6291464 | tf_op jit(solution)/shard_map/ppermute | solution.py:33
  229.5 27.9 %collective-permute-start.27 = (f32[512,256]{1,0:T(8,128)S(1)}, f32[512,256]{1,0:T(8,128)S(1)}, u32[]{:S(2)}, u32[]{:S(2)}) collective-permute-start(f32[512,256]{1,0:T(8,128)S(1)} %fusion.31), channel_id=1, source_target_pairs={{0,32},{1,33},{2,34},{3,35},{4,36},{5,37},{6,38},{7,39},{8,40},{9,... | collective-permute-start | bytes 1572872 | tf_op jit(solution)/shard_map/ppermute | solution.py:33
  231.9 32.6 %collective-permute-start.29 = (f32[512,256]{1,0:T(8,128)S(1)}, f32[512,256]{1,0:T(8,128)S(1)}, u32[]{:S(2)}, u32[]{:S(2)}) collective-permute-start(f32[512,256]{1,0:T(8,128)S(1)} %fusion.31), channel_id=1, source_target_pairs={{16,32},{17,33},{18,34},{19,35},{20,36},{21,37},{22,38},{23,39},{2... | collective-permute-start | bytes 1572872 | tf_op jit(solution)/shard_map/ppermute | solution.py:33
  233.2 45.8 %collective-permute-start.26 = (f32[512,256]{1,0:T(8,128)S(1)}, f32[512,256]{1,0:T(8,128)S(1)}, u32[]{:S(2)}, u32[]{:S(2)}) collective-permute-start(f32[512,256]{1,0:T(8,128)S(1)} %fusion.30), channel_id=1, source_target_pairs={{0,32},{1,33},{2,34},{3,35},{4,36},{5,37},{6,38},{7,39},{8,40},{9,... | collective-permute-start | bytes 1572872 | tf_op jit(solution)/shard_map/ppermute | solution.py:33
  235.7 46.9 %collective-permute-start.28 = (f32[512,256]{1,0:T(8,128)S(1)}, f32[512,256]{1,0:T(8,128)S(1)}, u32[]{:S(2)}, u32[]{:S(2)}) collective-permute-start(f32[512,256]{1,0:T(8,128)S(1)} %fusion.30), channel_id=1, source_target_pairs={{16,32},{17,33},{18,34},{19,35},{20,36},{21,37},{22,38},{23,39},{2... | collective-permute-start | bytes 1572872 | tf_op jit(solution)/shard_map/ppermute | solution.py:33

commit v3 on v2

--- a/solution.py
+++ b/solution.py
@@ -83,12 +83,12 @@
             total, (1 - bit) * HALF_Q, HALF_Q
         )
 
-    def amplitude(term, left, right, col):
+    def weight(left, right, col):
         row = px * QUARTER + bit * HALF_Q
-        rows = row + jnp.arange(term.shape[0], dtype=jnp.int32)
-        cols = col + jnp.arange(term.shape[1], dtype=jnp.int32)
-        energy_rows = lax.dynamic_slice_in_dim(virtual_energy, row, term.shape[0])
-        energy_cols = lax.dynamic_slice_in_dim(virtual_energy, col, term.shape[1])
+        rows = row + jnp.arange(HALF_Q, dtype=jnp.int32)
+        cols = col + jnp.arange(COLS, dtype=jnp.int32)
+        energy_rows = lax.dynamic_slice_in_dim(virtual_energy, row, HALF_Q)
+        energy_cols = lax.dynamic_slice_in_dim(virtual_energy, col, COLS)
         keep_rows = (rows < virtual_count[left]).astype(jnp.float32)
         keep_cols = (cols < virtual_count[right]).astype(jnp.float32)
         denominator = (
@@ -97,7 +97,7 @@
             - occupied_energy[left]
             - occupied_energy[right]
         )
-        return term * keep_rows[:, None] * keep_cols[None, :] / denominator
+        return keep_rows[:, None] * keep_cols[None, :] / denominator
 
     def join(part, other):
         return jnp.where(
@@ -129,7 +129,10 @@
     near_two = rows_at(slab_two, core * ROWS, ROWS)
     far_two = rows_at(slab_two, (1 - core) * ROWS, ROWS)
     near_two_cols, far_two_cols = cols_at(near_two, at, COLS), cols_at(far_two, at, COLS)
-    arrived = after(arrived, inner_parts, near_two, far_two, near_two_cols, far_two_cols)
+    inner_weight, outer_weight = weight(one, two, at), weight(two, three, at)
+    ready = (arrived, inner_weight, outer_weight)
+    ready = after(ready, inner_parts, near_two, far_two, near_two_cols, far_two_cols)
+    arrived, inner_weight, outer_weight = ready
     near = jnp.where(first, arrived[0], arrived[1])
     far = move(near, SWAP)
     near_cols = cols_at(near, at, COLS)
@@ -145,15 +148,15 @@
     inner_far = move(inner_kept, ALONG[2])
 
     outer_kept, outer_sent = halves(add_x(after(outer_parts, inner_kept)))
-    outer_next = move(outer_sent, ALONG[1])
-    inner_t = amplitude(inner_kept + after(inner_far, outer_sent), one, two, at)
+    outer_kept = outer_kept + move(outer_sent, ALONG[1])
+    outer_far = move(outer_kept, ALONG[2])
+    inner_t = (inner_kept + after(inner_far, outer_kept)) * inner_weight
     inner_other = move(inner_t, ALONG[1])
-    outer_kept = outer_kept + after(outer_next, inner_t)
-    outer_far = move(outer_kept, ALONG[2])
-    inner_quarter = join(inner_t, after(inner_other, outer_kept))
+    outer_t = (outer_kept + after(outer_far, inner_t)) * outer_weight
+    outer_other = move(outer_t, ALONG[1])
+    inner_quarter = join(inner_t, after(inner_other, outer_t))
     inner_pieces = around([inner_quarter] * X)
-    outer_t = amplitude(outer_kept + after(outer_far, inner_quarter), two, three, at)
-    outer_other = move(outer_t, ALONG[1])
+    outer_other = after(outer_other, inner_quarter)
 
     spans = [slice(w * CHUNK, (w + 1) * CHUNK) for w in range(COLS // CHUNK)]
     quarters = [join(outer_t[:, w], outer_other[:, w]) for w in spans]

time: 286 us -> 286 us (level)
  the two profiles are of different devices: /device:TPU:56 before, /device:TPU:184 now
where the time goes in v3:
time: 286 us; the launch traced here: 285 us
  waiting for transfers between devices  123 us (43%)
  starting transfers between devices  102 us (36%)
  local copies, waits for them, and re-layouts  19.9 us (7%)
  other arithmetic  19.6 us (7%)
  matrix products  19.2 us (7%)
    ppermute x30, waiting for transfers between devices, move(): return lax.ppermute(block, AXES, pairs)  123 us
    ppermute x30, starting transfers between devices, move(): return lax.ppermute(block, AXES, pairs)  102 us
    dot_general x12, matrix products, dot(): lax.dot_general(a, b, (((da,), (db,)), ((), ())), precision=lax.Precision...  19.2 us
  transfers between devices with their start and end apart: 30, of which 14 were waited for; matrix products, arithmetic and copies ran while one was open for 13% of the time, Pallas kernels for 0%

profile of v3, /device:TPU:184, one launch (start us, length us, event | category | flops | bytes accessed | tf_op | source)
XLA Modules:
  0.0 284.7 jit_solution(6349813196261243343)
XLA Ops:
  0.0 2.1 collective-permute-start
  2.1 3.1 %slice_bitcast_fusion = (f32[256,1024]{1,0:T(8,128)}, f32[256,1024]{1,0:T(8,128)}) fusion(f32[1,512,1024]{2,1,0:T(8,128)} %param.4), kind=kLoop, calls=%fused_computation.8 | loop fusion | bytes 4194304 | tf_op jit(solution)/shard_map/slice | solution.py:120
  5.2 9.9 %collective-permute-start.4 = (f32[256,1024]{1,0:T(8,128)}, f32[256,1024]{1,0:T(8,128)S(1)}, u32[]{:S(2)}, u32[]{:S(2)}) collective-permute-start(f32[256,1024]{1,0:T(8,128)} %get-tuple-element.92), channel_id=1, source_target_pairs={{0,480},{1,481},{2,482},{3,483},{4,484},{5,485},{6,486},{7,487},{8... | collective-permute-start | bytes 3145736 | tf_op jit(solution)/shard_map/ppermute | solution.py:33
  15.1 2.3 collective-permute-start.5
  18.8 1.3 compare_convert_fusion
  20.1 1.3 fusion.21
  21.4 2.7 broadcast_select_fusion.2
  24.1 1.8 fusion.7
  25.9 1.9 multiply_subtract_fusion.1
  28.9 3.4 %collective-permute-start.1 = (f32[256,512]{1,0:T(8,128)S(1)}, f32[256,512]{1,0:T(8,128)S(1)}, u32[]{:S(2)}, u32[]{:S(2)}) collective-permute-start(f32[256,512]{1,0:T(8,128)S(1)} %get-tuple-element.89), channel_id=1, source_target_pairs={{0,4},{1,5},{2,6},{3,7},{4,8},{5,9},{6,10},{7,11},{8,12},{9,13},{1... | collective-permute-start | bytes 1572872 | tf_op jit(solution)/shard_map/ppermute | solution.py:33
  32.3 4.6 %collective-permute-start.2 = (f32[256,512]{1,0:T(8,128)S(1)}, f32[256,512]{1,0:T(8,128)S(1)}, u32[]{:S(2)}, u32[]{:S(2)}) collective-permute-start(f32[256,512]{1,0:T(8,128)S(1)} %get-tuple-element.88), channel_id=1, source_target_pairs={{0,8},{1,9},{2,10},{3,11},{4,12},{5,13},{6,14},{7,15},{8,0},{9,1},... | collective-permute-start | bytes 1572872 | tf_op jit(solution)/shard_map/ppermute | solution.py:33
  36.9 3.3 %collective-permute-start.3 = (f32[256,512]{1,0:T(8,128)S(1)}, f32[256,512]{1,0:T(8,128)S(1)}, u32[]{:S(2)}, u32[]{:S(2)}) collective-permute-start(f32[256,512]{1,0:T(8,128)S(1)} %get-tuple-element.87), channel_id=1, source_target_pairs={{0,12},{1,13},{2,14},{3,15},{4,0},{5,1},{6,2},{7,3},{8,4},{9,5},{1... | collective-permute-start | bytes 1572872 | tf_op jit(solution)/shard_map/ppermute | solution.py:33
  40.3 2.7 fusion.15
  43.0 1.4 fusion.23
  44.4 1.5 constant_dynamic-slice_fusion.8
  45.9 5.8 %collective-permute-done.4 = f32[256,1024]{1,0:T(8,128)S(1)} collective-permute-done((f32[256,1024]{1,0:T(8,128)}, f32[256,1024]{1,0:T(8,128)S(1)}, u32[]{:S(2)}, u32[]{:S(2)}) %collective-permute-start.4) | collective-permute-done | bytes 1048608 | tf_op jit(solution)/shard_map/ppermute | solution.py:33
  51.7 9.6 %collective-permute-done.5 = f32[256,1024]{1,0:T(8,128)} collective-permute-done((f32[256,1024]{1,0:T(8,128)}, f32[256,1024]{1,0:T(8,128)}, u32[]{:S(2)}, u32[]{:S(2)}) %collective-permute-start.5) | collective-permute-done | bytes 1048608 | tf_op jit(solution)/shard_map/ppermute | solution.py:33
  62.1 1.4 broadcast_select_fusion.3
  63.5 9.3 %collective-permute-start.6 = (f32[256,1024]{1,0:T(8,128)S(1)}, f32[256,1024]{1,0:T(8,128)}, u32[]{:S(2)}, u32[]{:S(2)}) collective-permute-start(f32[256,1024]{1,0:T(8,128)S(1)} %broadcast_select_fusion.3), channel_id=1, source_target_pairs={{0,16},{1,17},{2,18},{3,19},{4,20},{5,21},{6,22},{7,23},{8,24},{9,... | collective-permute-start | bytes 3145736 | tf_op jit(solution)/shard_map/ppermute | solution.py:33
  73.7 2.3 fusion.28
  76.0 1.1 multiply_subtract_fusion
  79.3 2.5 subtract_add_fusion
  81.8 1.4 constant_dynamic-slice_fusion.2
  83.2 4.9 %collective-permute-start.10 = (f32[256,512]{1,0:T(8,128)}, f32[256,512]{1,0:T(8,128)}, u32[]{:S(2)}, u32[]{:S(2)}) collective-permute-start(f32[256,512]{1,0:T(8,128)} %get-tuple-element.80), channel_id=1, source_target_pairs={{0,8},{1,9},{2,10},{3,11},{4,12},{5,13},{6,14},{7,15},{8,0},{9,1},... | collective-permute-start | bytes 1572872 | tf_op jit(solution)/shard_map/ppermute | solution.py:33
  88.2 3.1 %collective-permute-start.11 = (f32[256,512]{1,0:T(8,128)}, f32[256,512]{1,0:T(8,128)}, u32[]{:S(2)}, u32[]{:S(2)}) collective-permute-start(f32[256,512]{1,0:T(8,128)} %get-tuple-element.79), channel_id=1, source_target_pairs={{0,12},{1,13},{2,14},{3,15},{4,0},{5,1},{6,2},{7,3},{8,4},{9,5},{1... | collective-permute-start | bytes 1572872 | tf_op jit(solution)/shard_map/ppermute | solution.py:33
  91.2 3.0 %collective-permute-start.9 = (f32[256,512]{1,0:T(8,128)}, f32[256,512]{1,0:T(8,128)}, u32[]{:S(2)}, u32[]{:S(2)}) collective-permute-start(f32[256,512]{1,0:T(8,128)} %get-tuple-element.81), channel_id=1, source_target_pairs={{0,4},{1,5},{2,6},{3,7},{4,8},{5,9},{6,10},{7,11},{8,12},{9,13},{1... | collective-permute-start | bytes 1572872 | tf_op jit(solution)/shard_map/ppermute | solution.py:33
  95.2 1.9 collective-permute-start.7
  97.1 7.7 %collective-permute-done.7 = f32[128,512]{1,0:T(8,128)} collective-permute-done((f32[128,512]{1,0:T(8,128)}, f32[128,512]{1,0:T(8,128)}, u32[]{:S(2)}, u32[]{:S(2)}) %collective-permute-start.7) | collective-permute-done | bytes 262176 | tf_op jit(solution)/shard_map/ppermute | solution.py:33
  105.8 6.4 %collective-permute-done.11 = f32[256,512]{1,0:T(8,128)} collective-permute-done((f32[256,512]{1,0:T(8,128)}, f32[256,512]{1,0:T(8,128)}, u32[]{:S(2)}, u32[]{:S(2)}) %collective-permute-start.11) | collective-permute-done | bytes 524320 | tf_op jit(solution)/shard_map/ppermute | solution.py:33
  112.2 1.7 add_add_fusion
  113.9 1.9 collective-permute-start.12
  115.9 1.9 collective-permute-start.8
  117.8 7.2 %collective-permute-done.12 = f32[128,512]{1,0:T(8,128)S(1)} collective-permute-done((f32[128,512]{1,0:T(8,128)S(1)}, f32[128,512]{1,0:T(8,128)S(1)}, u32[]{:S(2)}, u32[]{:S(2)}) %collective-permute-start.12) | collective-permute-done | bytes 262176 | tf_op jit(solution)/shard_map/ppermute | solution.py:33
  125.8 1.9 collective-permute-start.14
  127.7 7.9 %collective-permute-done.8 = f32[128,512]{1,0:T(8,128)S(1)} collective-permute-done((f32[128,512]{1,0:T(8,128)S(1)}, f32[128,512]{1,0:T(8,128)S(1)}, u32[]{:S(2)}, u32[]{:S(2)}) %collective-permute-start.8) | collective-permute-done | bytes 262176 | tf_op jit(solution)/shard_map/ppermute | solution.py:33
  136.3 6.0 %collective-permute-start.13 = (f32[128,512]{1,0:T(8,128)}, f32[128,512]{1,0:T(8,128)}, u32[]{:S(2)}, u32[]{:S(2)}) collective-permute-start(f32[128,512]{1,0:T(8,128)} %add_multiply_fusion.1), channel_id=1, source_target_pairs={{0,1},{1,0},{2,3},{3,2},{4,5},{5,4},{6,7},{7,6},{8,9},{9,8},{10,11... | collective-permute-start | bytes 786440 | tf_op jit(solution)/shard_map/ppermute | solution.py:33
  143.5 4.7 %collective-permute-start.18 = (f32[128,512]{1,0:T(8,128)S(1)}, f32[128,512]{1,0:T(8,128)S(1)}, u32[]{:S(2)}, u32[]{:S(2)}) collective-permute-start(f32[128,512]{1,0:T(8,128)S(1)} %add_multiply_fusion), channel_id=1, source_target_pairs={{0,1},{1,0},{2,3},{3,2},{4,5},{5,4},{6,7},{7,6},{8,9},{9,8},{10,11... | collective-permute-start | bytes 786440 | tf_op jit(solution)/shard_map/ppermute | solution.py:33
  149.0 2.1 maximum_select_fusion.1
  151.2 3.5 %collective-permute-done.18 = f32[128,512]{1,0:T(8,128)S(1)} collective-permute-done((f32[128,512]{1,0:T(8,128)S(1)}, f32[128,512]{1,0:T(8,128)S(1)}, u32[]{:S(2)}, u32[]{:S(2)}) %collective-permute-start.18) | collective-permute-done | bytes 262176 | tf_op jit(solution)/shard_map/ppermute | solution.py:33
  155.3 3.4 %collective-permute-start.22 = (f32[256,256]{1,0:T(8,128)S(1)}, f32[256,256]{1,0:T(8,128)}, u32[]{:S(2)}, u32[]{:S(2)}) collective-permute-start(f32[256,256]{1,0:T(8,128)S(1)} %maximum_select_fusion.3), channel_id=1, source_target_pairs={{0,4},{1,5},{2,6},{3,7},{4,8},{5,9},{6,10},{7,11},{8,12},{9,13},{1... | collective-permute-start | bytes 786440 | tf_op jit(solution)/shard_map/ppermute | solution.py:33
  158.8 4.6 %collective-permute-start.23 = (f32[256,256]{1,0:T(8,128)S(1)}, f32[256,256]{1,0:T(8,128)}, u32[]{:S(2)}, u32[]{:S(2)}) collective-permute-start(f32[256,256]{1,0:T(8,128)S(1)} %maximum_select_fusion.3), channel_id=1, source_target_pairs={{0,8},{1,9},{2,10},{3,11},{4,12},{5,13},{6,14},{7,15},{8,0},{9,1},... | collective-permute-start | bytes 786440 | tf_op jit(solution)/shard_map/ppermute | solution.py:33
  163.4 3.3 %collective-permute-start.24 = (f32[256,256]{1,0:T(8,128)S(1)}, f32[256,256]{1,0:T(8,128)}, u32[]{:S(2)}, u32[]{:S(2)}) collective-permute-start(f32[256,256]{1,0:T(8,128)S(1)} %maximum_select_fusion.3), channel_id=1, source_target_pairs={{0,12},{1,13},{2,14},{3,15},{4,0},{5,1},{6,2},{7,3},{8,4},{9,5},{1... | collective-permute-start | bytes 786440 | tf_op jit(solution)/shard_map/ppermute | solution.py:33
  167.9 2.5 collective-permute-start.15
  170.4 2.8 collective-permute-start.16
  173.2 4.5 %collective-permute-start.19 = (f32[256,256]{1,0:T(8,128)S(1)}, f32[256,256]{1,0:T(8,128)S(1)}, u32[]{:S(2)}, u32[]{:S(2)}) collective-permute-start(f32[256,256]{1,0:T(8,128)S(1)} %maximum_select_fusion.2), channel_id=1, source_target_pairs={{0,4},{1,5},{2,6},{3,7},{4,8},{5,9},{6,10},{7,11},{8,12},{9,13},{1... | collective-permute-start | bytes 786440 | tf_op jit(solution)/shard_map/ppermute | solution.py:33
  177.8 2.6 collective-permute-start.20
  180.3 3.9 %collective-permute-start.21 = (f32[256,256]{1,0:T(8,128)S(1)}, f32[256,256]{1,0:T(8,128)S(1)}, u32[]{:S(2)}, u32[]{:S(2)}) collective-permute-start(f32[256,256]{1,0:T(8,128)S(1)} %maximum_select_fusion.2), channel_id=1, source_target_pairs={{0,12},{1,13},{2,14},{3,15},{4,0},{5,1},{6,2},{7,3},{8,4},{9,5},{1... | collective-permute-start | bytes 786440 | tf_op jit(solution)/shard_map/ppermute | solution.py:33
  188.4 18.5 %collective-permute-done.19 = f32[256,256]{1,0:T(8,128)S(1)} collective-permute-done((f32[256,256]{1,0:T(8,128)S(1)}, f32[256,256]{1,0:T(8,128)S(1)}, u32[]{:S(2)}, u32[]{:S(2)}) %collective-permute-start.19) | collective-permute-done | bytes 262176 | tf_op jit(solution)/shard_map/ppermute | solution.py:33
  206.9 1.9 collective-permute-start.17
  210.1 7.9 %collective-permute-done.17 = f32[256,512]{1,0:T(8,128)S(1)} collective-permute-done((f32[256,512]{1,0:T(8,128)S(1)}, f32[256,512]{1,0:T(8,128)S(1)}, u32[]{:S(2)}, u32[]{:S(2)}) %collective-permute-start.17) | collective-permute-done | bytes 524320 | tf_op jit(solution)/shard_map/ppermute | solution.py:33
  218.4 1.4 copy-done.1
  219.8 1.9 fusion.32
  221.8 2.0 fusion.5
  224.8 1.5 broadcast_select_fusion
  226.3 1.9 collective-permute-start.25
  228.2 1.9 collective-permute-start.27
  230.1 1.3 collective-permute-start.29
  231.4 2.2 collective-permute-start.26
  233.6 1.3 collective-permute-start.28
  235.8 26.8 %collective-permute-done.27 = f32[512,256]{1,0:T(8,128)S(1)} collective-permute-done((f32[512,256]{1,0:T(8,128)S(1)}, f32[512,256]{1,0:T(8,128)S(1)}, u32[]{:S(2)}, u32[]{:S(2)}) %collective-permute-start.27) | collective-permute-done | bytes 524320 | tf_op jit(solution)/shard_map/ppermute | solution.py:33
  262.6 5.7 %collective-permute-done.29 = f32[512,256]{1,0:T(8,128)S(1)} collective-permute-done((f32[512,256]{1,0:T(8,128)S(1)}, f32[512,256]{1,0:T(8,128)S(1)}, u32[]{:S(2)}, u32[]{:S(2)}) %collective-permute-start.29) | collective-permute-done | bytes 524320 | tf_op jit(solution)/shard_map/ppermute | solution.py:33
  268.3 13.6 %collective-permute-done.26 = f32[512,256]{1,0:T(8,128)S(1)} collective-permute-done((f32[512,256]{1,0:T(8,128)S(1)}, f32[512,256]{1,0:T(8,128)S(1)}, u32[]{:S(2)}, u32[]{:S(2)}) %collective-permute-start.26) | collective-permute-done | bytes 524320 | tf_op jit(solution)/shard_map/ppermute | solution.py:33
  281.9 1.2 collective-permute-done.28
  283.1 1.6 fusion
  (97 shorter events, 21.0 us)
Async XLA Ops:
  0.0 17.4 %copy-start.20 = (f32[1024]{0:T(1024)S(1)}, f32[1024]{0:T(1024)}, u32[]{:S(2)}) copy-start(f32[1024]{0:T(1024)} %param.6) | copy-start | bytes 12292
  0.0 17.5 %copy-start.18 = (s32[32]{0:T(128)S(1)}, s32[32]{0:T(128)}, u32[]{:S(2)}) copy-start(s32[32]{0:T(128)} %param.7) | copy-start | bytes 388
  0.0 18.2 %copy-start.19 = (f32[32]{0:T(128)S(1)}, f32[32]{0:T(128)}, u32[]{:S(2)}) copy-start(f32[32]{0:T(128)} %param.5) | copy-start | bytes 388
  0.0 21.4 %collective-permute-start = (f32[512,1024]{1,0:T(8,128)}, f32[512,1024]{1,0:T(8,128)}, u32[]{:S(2)}, u32[]{:S(2)}) collective-permute-start(f32[512,1024]{1,0:T(8,128)} %bitcast.34), channel_id=1, source_target_pairs={{0,16},{1,17},{2,18},{3,19},{4,20},{5,21},{6,22},{7,23},{8,24},{9,... | collective-permute-start | bytes 6291464 | tf_op jit(solution)/shard_map/ppermute | solution.py:33
  5.2 46.5 %collective-permute-start.4 = (f32[256,1024]{1,0:T(8,128)}, f32[256,1024]{1,0:T(8,128)S(1)}, u32[]{:S(2)}, u32[]{:S(2)}) collective-permute-start(f32[256,1024]{1,0:T(8,128)} %get-tuple-element.92), channel_id=1, source_target_pairs={{0,480},{1,481},{2,482},{3,483},{4,484},{5,485},{6,486},{7,487},{8... | collective-permute-start | bytes 3145736 | tf_op jit(solution)/shard_map/ppermute | solution.py:33
  15.1 46.2 %collective-permute-start.5 = (f32[256,1024]{1,0:T(8,128)}, f32[256,1024]{1,0:T(8,128)}, u32[]{:S(2)}, u32[]{:S(2)}) collective-permute-start(f32[256,1024]{1,0:T(8,128)} %get-tuple-element.91), channel_id=1, source_target_pairs={{0,496},{1,497},{2,498},{3,499},{4,500},{5,501},{6,502},{7,503},{8... | collective-permute-start | bytes 3145736 | tf_op jit(solution)/shard_map/ppermute | solution.py:33
  24.1 1.9 copy-start
  28.9 32.4 %collective-permute-start.1 = (f32[256,512]{1,0:T(8,128)S(1)}, f32[256,512]{1,0:T(8,128)S(1)}, u32[]{:S(2)}, u32[]{:S(2)}) collective-permute-start(f32[256,512]{1,0:T(8,128)S(1)} %get-tuple-element.89), channel_id=1, source_target_pairs={{0,4},{1,5},{2,6},{3,7},{4,8},{5,9},{6,10},{7,11},{8,12},{9,13},{1... | collective-permute-start | bytes 1572872 | tf_op jit(solution)/shard_map/ppermute | solution.py:33
  32.3 29.0 %collective-permute-start.2 = (f32[256,512]{1,0:T(8,128)S(1)}, f32[256,512]{1,0:T(8,128)S(1)}, u32[]{:S(2)}, u32[]{:S(2)}) collective-permute-start(f32[256,512]{1,0:T(8,128)S(1)} %get-tuple-element.88), channel_id=1, source_target_pairs={{0,8},{1,9},{2,10},{3,11},{4,12},{5,13},{6,14},{7,15},{8,0},{9,1},... | collective-permute-start | bytes 1572872 | tf_op jit(solution)/shard_map/ppermute | solution.py:33
  36.9 24.4 %collective-permute-start.3 = (f32[256,512]{1,0:T(8,128)S(1)}, f32[256,512]{1,0:T(8,128)S(1)}, u32[]{:S(2)}, u32[]{:S(2)}) collective-permute-start(f32[256,512]{1,0:T(8,128)S(1)} %get-tuple-element.87), channel_id=1, source_target_pairs={{0,12},{1,13},{2,14},{3,15},{4,0},{5,1},{6,2},{7,3},{8,4},{9,5},{1... | collective-permute-start | bytes 1572872 | tf_op jit(solution)/shard_map/ppermute | solution.py:33
  51.7 9.7 %copy-start.9 = (f32[256,1024]{1,0:T(8,128)}, f32[256,1024]{1,0:T(8,128)S(1)}, u32[]{:S(2)}) copy-start(f32[256,1024]{1,0:T(8,128)S(1)} %collective-permute-done.4) | copy-start | bytes 3145732
  61.3 0.8 copy-start.11
  61.3 2.2 copy-start.13
  61.4 2.1 copy-start.15
  63.5 13.6 %collective-permute-start.6 = (f32[256,1024]{1,0:T(8,128)S(1)}, f32[256,1024]{1,0:T(8,128)}, u32[]{:S(2)}, u32[]{:S(2)}) collective-permute-start(f32[256,1024]{1,0:T(8,128)S(1)} %broadcast_select_fusion.3), channel_id=1, source_target_pairs={{0,16},{1,17},{2,18},{3,19},{4,20},{5,21},{6,22},{7,23},{8,24},{9,... | collective-permute-start | bytes 3145736 | tf_op jit(solution)/shard_map/ppermute | solution.py:33
  72.9 0.8 copy-start.2
  73.6 2.3 copy-start.7
  76.0 2.2 copy-start.4
  78.2 1.0 copy-start.8
  81.8 12.4 %copy-start.6 = (f32[256,512]{1,0:T(8,128)S(1)}, f32[256,512]{1,0:T(8,128)}, u32[]{:S(2)}) copy-start(f32[256,512]{1,0:T(8,128)} %get-tuple-element.44) | copy-start | bytes 1572868
  81.8 12.4 %copy-start.12 = (f32[256,512]{1,0:T(8,128)S(1)}, f32[256,512]{1,0:T(8,128)}, u32[]{:S(2)}) copy-start(f32[256,512]{1,0:T(8,128)} %copy-done.11) | copy-start | bytes 1572868
  81.8 12.4 %copy-start.14 = (f32[256,512]{1,0:T(8,128)S(1)}, f32[256,512]{1,0:T(8,128)}, u32[]{:S(2)}) copy-start(f32[256,512]{1,0:T(8,128)} %copy-done.13) | copy-start | bytes 1572868
  81.8 12.4 %copy-start.16 = (f32[256,512]{1,0:T(8,128)S(1)}, f32[256,512]{1,0:T(8,128)}, u32[]{:S(2)}) copy-start(f32[256,512]{1,0:T(8,128)} %copy-done.15) | copy-start | bytes 1572868
  83.2 22.5 %collective-permute-start.10 = (f32[256,512]{1,0:T(8,128)}, f32[256,512]{1,0:T(8,128)}, u32[]{:S(2)}, u32[]{:S(2)}) collective-permute-start(f32[256,512]{1,0:T(8,128)} %get-tuple-element.80), channel_id=1, source_target_pairs={{0,8},{1,9},{2,10},{3,11},{4,12},{5,13},{6,14},{7,15},{8,0},{9,1},... | collective-permute-start | bytes 1572872 | tf_op jit(solution)/shard_map/ppermute | solution.py:33
  88.2 24.0 %collective-permute-start.11 = (f32[256,512]{1,0:T(8,128)}, f32[256,512]{1,0:T(8,128)}, u32[]{:S(2)}, u32[]{:S(2)}) collective-permute-start(f32[256,512]{1,0:T(8,128)} %get-tuple-element.79), channel_id=1, source_target_pairs={{0,12},{1,13},{2,14},{3,15},{4,0},{5,1},{6,2},{7,3},{8,4},{9,5},{1... | collective-permute-start | bytes 1572872 | tf_op jit(solution)/shard_map/ppermute | solution.py:33
  91.2 20.9 %collective-permute-start.9 = (f32[256,512]{1,0:T(8,128)}, f32[256,512]{1,0:T(8,128)}, u32[]{:S(2)}, u32[]{:S(2)}) collective-permute-start(f32[256,512]{1,0:T(8,128)} %get-tuple-element.81), channel_id=1, source_target_pairs={{0,4},{1,5},{2,6},{3,7},{4,8},{5,9},{6,10},{7,11},{8,12},{9,13},{1... | collective-permute-start | bytes 1572872 | tf_op jit(solution)/shard_map/ppermute | solution.py:33
  95.2 9.6 %collective-permute-start.7 = (f32[128,512]{1,0:T(8,128)}, f32[128,512]{1,0:T(8,128)}, u32[]{:S(2)}, u32[]{:S(2)}) collective-permute-start(f32[128,512]{1,0:T(8,128)} %constant_dynamic-slice_fusion.1), channel_id=1, source_target_pairs={{0,1},{1,0},{2,3},{3,2},{4,5},{5,4},{6,7},{7,6},{8,9},{9,8},{10,11... | collective-permute-start | bytes 786440 | tf_op jit(solution)/shard_map/ppermute | solution.py:33
  105.8 36.6 %copy-start.10 = (f32[128,512]{1,0:T(8,128)S(1)}, f32[128,512]{1,0:T(8,128)}, u32[]{:S(2)}) copy-start(f32[128,512]{1,0:T(8,128)} %get-tuple-element.55) | copy-start | bytes 786436
  113.9 11.1 %collective-permute-start.12 = (f32[128,512]{1,0:T(8,128)S(1)}, f32[128,512]{1,0:T(8,128)S(1)}, u32[]{:S(2)}, u32[]{:S(2)}) collective-permute-start(f32[128,512]{1,0:T(8,128)S(1)} %constant_dynamic-slice_fusion), channel_id=1, source_target_pairs={{0,1},{1,0},{2,3},{3,2},{4,5},{5,4},{6,7},{7,6},{8,9},{9,8},{10,11... | collective-permute-start | bytes 786440 | tf_op jit(solution)/shard_map/ppermute | solution.py:33
  115.9 19.7 %collective-permute-start.8 = (f32[128,512]{1,0:T(8,128)S(1)}, f32[128,512]{1,0:T(8,128)S(1)}, u32[]{:S(2)}, u32[]{:S(2)}) collective-permute-start(f32[128,512]{1,0:T(8,128)S(1)} %dynamic-slice_add_fusion.1), channel_id=1, source_target_pairs={{0,2},{1,3},{2,0},{3,1},{4,6},{5,7},{6,4},{7,5},{8,10},{9,11},{10,... | collective-permute-start | bytes 786440 | tf_op jit(solution)/shard_map/ppermute | solution.py:33
  125.8 16.6 %collective-permute-start.14 = (f32[128,512]{1,0:T(8,128)}, f32[128,512]{1,0:T(8,128)}, u32[]{:S(2)}, u32[]{:S(2)}) collective-permute-start(f32[128,512]{1,0:T(8,128)} %dynamic-slice_add_fusion), channel_id=1, source_target_pairs={{0,2},{1,3},{2,0},{3,1},{4,6},{5,7},{6,4},{7,5},{8,10},{9,11},{10,... | collective-permute-start | bytes 786440 | tf_op jit(solution)/shard_map/ppermute | solution.py:33
  136.3 30.5 %copy-start.3 = (f32[256,512]{1,0:T(8,128)S(1)}, f32[256,512]{1,0:T(8,128)}, u32[]{:S(2)}) copy-start(f32[256,512]{1,0:T(8,128)} %copy-done.2) | copy-start | bytes 1572868
  136.3 12.7 %collective-permute-start.13 = (f32[128,512]{1,0:T(8,128)}, f32[128,512]{1,0:T(8,128)}, u32[]{:S(2)}, u32[]{:S(2)}) collective-permute-start(f32[128,512]{1,0:T(8,128)} %add_multiply_fusion.1), channel_id=1, source_target_pairs={{0,1},{1,0},{2,3},{3,2},{4,5},{5,4},{6,7},{7,6},{8,9},{9,8},{10,11... | collective-permute-start | bytes 786440 | tf_op jit(solution)/shard_map/ppermute | solution.py:33
  143.5 11.2 %collective-permute-start.18 = (f32[128,512]{1,0:T(8,128)S(1)}, f32[128,512]{1,0:T(8,128)S(1)}, u32[]{:S(2)}, u32[]{:S(2)}) collective-permute-start(f32[128,512]{1,0:T(8,128)S(1)} %add_multiply_fusion), channel_id=1, source_target_pairs={{0,1},{1,0},{2,3},{3,2},{4,5},{5,4},{6,7},{7,6},{8,9},{9,8},{10,11... | collective-permute-start | bytes 786440 | tf_op jit(solution)/shard_map/ppermute | solution.py:33
  155.3 17.9 %collective-permute-start.22 = (f32[256,256]{1,0:T(8,128)S(1)}, f32[256,256]{1,0:T(8,128)}, u32[]{:S(2)}, u32[]{:S(2)}) collective-permute-start(f32[256,256]{1,0:T(8,128)S(1)} %maximum_select_fusion.3), channel_id=1, source_target_pairs={{0,4},{1,5},{2,6},{3,7},{4,8},{5,9},{6,10},{7,11},{8,12},{9,13},{1... | collective-permute-start | bytes 786440 | tf_op jit(solution)/shard_map/ppermute | solution.py:33
  158.8 19.0 %collective-permute-start.23 = (f32[256,256]{1,0:T(8,128)S(1)}, f32[256,256]{1,0:T(8,128)}, u32[]{:S(2)}, u32[]{:S(2)}) collective-permute-start(f32[256,256]{1,0:T(8,128)S(1)} %maximum_select_fusion.3), channel_id=1, source_target_pairs={{0,8},{1,9},{2,10},{3,11},{4,12},{5,13},{6,14},{7,15},{8,0},{9,1},... | collective-permute-start | bytes 786440 | tf_op jit(solution)/shard_map/ppermute | solution.py:33
  163.4 16.9 %collective-permute-start.24 = (f32[256,256]{1,0:T(8,128)S(1)}, f32[256,256]{1,0:T(8,128)}, u32[]{:S(2)}, u32[]{:S(2)}) collective-permute-start(f32[256,256]{1,0:T(8,128)S(1)} %maximum_select_fusion.3), channel_id=1, source_target_pairs={{0,12},{1,13},{2,14},{3,15},{4,0},{5,1},{6,2},{7,3},{8,4},{9,5},{1... | collective-permute-start | bytes 786440 | tf_op jit(solution)/shard_map/ppermute | solution.py:33
  166.8 1.0 copy-start.5
  166.8 6.3 %copy-start.17 = (f32[128,256]{1,0:T(8,128)S(1)}, f32[128,256]{1,0:T(8,128)}, u32[]{:S(2)}) copy-start(f32[128,256]{1,0:T(8,128)} %get-tuple-element.96) | copy-start | bytes 393220
  167.9 42.2 %collective-permute-start.15 = (f32[256,512]{1,0:T(8,128)S(1)}, f32[256,512]{1,0:T(8,128)S(1)}, u32[]{:S(2)}, u32[]{:S(2)}) collective-permute-start(f32[256,512]{1,0:T(8,128)S(1)} %copy-done.5), channel_id=1, source_target_pairs={{0,4},{1,5},{2,6},{3,7},{4,8},{5,9},{6,10},{7,11},{8,12},{9,13},{1... | collective-permute-start | bytes 1572872 | tf_op jit(solution)/shard_map/ppermute | solution.py:33
  170.4 39.7 %collective-permute-start.16 = (f32[256,512]{1,0:T(8,128)S(1)}, f32[256,512]{1,0:T(8,128)S(1)}, u32[]{:S(2)}, u32[]{:S(2)}) collective-permute-start(f32[256,512]{1,0:T(8,128)S(1)} %copy-done.5), channel_id=1, source_target_pairs={{0,8},{1,9},{2,10},{3,11},{4,12},{5,13},{6,14},{7,15},{8,0},{9,1},... | collective-permute-start | bytes 1572872 | tf_op jit(solution)/shard_map/ppermute | solution.py:33
  173.2 33.7 %collective-permute-start.19 = (f32[256,256]{1,0:T(8,128)S(1)}, f32[256,256]{1,0:T(8,128)S(1)}, u32[]{:S(2)}, u32[]{:S(2)}) collective-permute-start(f32[256,256]{1,0:T(8,128)S(1)} %maximum_select_fusion.2), channel_id=1, source_target_pairs={{0,4},{1,5},{2,6},{3,7},{4,8},{5,9},{6,10},{7,11},{8,12},{9,13},{1... | collective-permute-start | bytes 786440 | tf_op jit(solution)/shard_map/ppermute | solution.py:33
  177.8 31.1 %collective-permute-start.20 = (f32[256,256]{1,0:T(8,128)S(1)}, f32[256,256]{1,0:T(8,128)S(1)}, u32[]{:S(2)}, u32[]{:S(2)}) collective-permute-start(f32[256,256]{1,0:T(8,128)S(1)} %maximum_select_fusion.2), channel_id=1, source_target_pairs={{0,8},{1,9},{2,10},{3,11},{4,12},{5,13},{6,14},{7,15},{8,0},{9,1},... | collective-permute-start | bytes 786440 | tf_op jit(solution)/shard_map/ppermute | solution.py:33
  180.3 28.5 %collective-permute-start.21 = (f32[256,256]{1,0:T(8,128)S(1)}, f32[256,256]{1,0:T(8,128)S(1)}, u32[]{:S(2)}, u32[]{:S(2)}) collective-permute-start(f32[256,256]{1,0:T(8,128)S(1)} %maximum_select_fusion.2), channel_id=1, source_target_pairs={{0,12},{1,13},{2,14},{3,15},{4,0},{5,1},{6,2},{7,3},{8,4},{9,5},{1... | collective-permute-start | bytes 786440 | tf_op jit(solution)/shard_map/ppermute | solution.py:33
  206.9 11.1 %collective-permute-start.17 = (f32[256,512]{1,0:T(8,128)S(1)}, f32[256,512]{1,0:T(8,128)S(1)}, u32[]{:S(2)}, u32[]{:S(2)}) collective-permute-start(f32[256,512]{1,0:T(8,128)S(1)} %copy-done.5), channel_id=1, source_target_pairs={{0,12},{1,13},{2,14},{3,15},{4,0},{5,1},{6,2},{7,3},{8,4},{9,5},{1... | collective-permute-start | bytes 1572872 | tf_op jit(solution)/shard_map/ppermute | solution.py:33
  218.2 1.6 copy-start.1
  226.3 8.7 %collective-permute-start.25 = (f32[512,1024]{1,0:T(8,128)S(1)}, f32[512,1024]{1,0:T(8,128)S(1)}, u32[]{:S(2)}, u32[]{:S(2)}) collective-permute-start(f32[512,1024]{1,0:T(8,128)S(1)} %get-tuple-element.105), channel_id=1, source_target_pairs={{0,16},{1,17},{2,18},{3,19},{4,20},{5,21},{6,22},{7,23},{8,24},{9,... | collective-permute-start | bytes 6291464 | tf_op jit(solution)/shard_map/ppermute | solution.py:33
  228.2 34.4 %collective-permute-start.27 = (f32[512,256]{1,0:T(8,128)S(1)}, f32[512,256]{1,0:T(8,128)S(1)}, u32[]{:S(2)}, u32[]{:S(2)}) collective-permute-start(f32[512,256]{1,0:T(8,128)S(1)} %fusion.31), channel_id=1, source_target_pairs={{0,32},{1,33},{2,34},{3,35},{4,36},{5,37},{6,38},{7,39},{8,40},{9,... | collective-permute-start | bytes 1572872 | tf_op jit(solution)/shard_map/ppermute | solution.py:33
  230.1 38.2 %collective-permute-start.29 = (f32[512,256]{1,0:T(8,128)S(1)}, f32[512,256]{1,0:T(8,128)S(1)}, u32[]{:S(2)}, u32[]{:S(2)}) collective-permute-start(f32[512,256]{1,0:T(8,128)S(1)} %fusion.31), channel_id=1, source_target_pairs={{16,32},{17,33},{18,34},{19,35},{20,36},{21,37},{22,38},{23,39},{2... | collective-permute-start | bytes 1572872 | tf_op jit(solution)/shard_map/ppermute | solution.py:33
  231.4 50.5 %collective-permute-start.26 = (f32[512,256]{1,0:T(8,128)S(1)}, f32[512,256]{1,0:T(8,128)S(1)}, u32[]{:S(2)}, u32[]{:S(2)}) collective-permute-start(f32[512,256]{1,0:T(8,128)S(1)} %fusion.30), channel_id=1, source_target_pairs={{0,32},{1,33},{2,34},{3,35},{4,36},{5,37},{6,38},{7,39},{8,40},{9,... | collective-permute-start | bytes 1572872 | tf_op jit(solution)/shard_map/ppermute | solution.py:33
  233.6 49.5 %collective-permute-start.28 = (f32[512,256]{1,0:T(8,128)S(1)}, f32[512,256]{1,0:T(8,128)S(1)}, u32[]{:S(2)}, u32[]{:S(2)}) collective-permute-start(f32[512,256]{1,0:T(8,128)S(1)} %fusion.30), channel_id=1, source_target_pairs={{16,32},{17,33},{18,34},{19,35},{20,36},{21,37},{22,38},{23,39},{2... | collective-permute-start | bytes 1572872 | tf_op jit(solution)/shard_map/ppermute | solution.py:33

commit v4 on v3

--- a/solution.py
+++ b/solution.py
@@ -83,7 +83,7 @@
             total, (1 - bit) * HALF_Q, HALF_Q
         )
 
-    def weight(left, right, col):
+    def weight(left, right, col, occupied_energy, virtual_energy, virtual_count):
         row = px * QUARTER + bit * HALF_Q
         rows = row + jnp.arange(HALF_Q, dtype=jnp.int32)
         cols = col + jnp.arange(COLS, dtype=jnp.int32)
@@ -125,49 +125,62 @@
 
     inner_sends = send_x(pair_term(slab_one, slab_two, two_cols, one_cols))
     inner_parts = around(inner_sends)
-
+    energies = after((occupied_energy, virtual_energy, virtual_count), inner_sends)
+    inner_weight = weight(one, two, at, *energies)
+    outer_weight = weight(two, three, at, *energies)
     near_two = rows_at(slab_two, core * ROWS, ROWS)
     far_two = rows_at(slab_two, (1 - core) * ROWS, ROWS)
     near_two_cols, far_two_cols = cols_at(near_two, at, COLS), cols_at(far_two, at, COLS)
-    inner_weight, outer_weight = weight(one, two, at), weight(two, three, at)
-    ready = (arrived, inner_weight, outer_weight)
-    ready = after(ready, inner_parts, near_two, far_two, near_two_cols, far_two_cols)
-    arrived, inner_weight, outer_weight = ready
-    near = jnp.where(first, arrived[0], arrived[1])
+    prepared = (near_two, far_two, near_two_cols, far_two_cols)
+    ready = after((inner_parts, inner_weight, outer_weight), prepared)
+    inner_parts, inner_weight, outer_weight = ready
+    inner_kept, inner_sent = halves(add_x(inner_parts))
+    inner_next = move(inner_sent, ALONG[1])
+
+    arrived = after(arrived, inner_sent)
+    near = arrived[0] + arrived[1]
     far = move(near, SWAP)
     near_cols = cols_at(near, at, COLS)
     outer_near = pair_term(near_two, near, near_cols, near_two_cols)
     far = after(far, outer_near)
     far_cols = cols_at(far, at, COLS)
     outer = outer_near + pair_term(far_two, far, far_cols, far_two_cols)
-    outer_sends = send_x(outer)
-    outer_parts = around(outer_sends)
-
-    inner_kept, inner_sent = halves(add_x(after(inner_parts, outer_sends)))
-    inner_kept = inner_kept + move(inner_sent, ALONG[1])
+
+    left, right = slice(0, CHUNK), slice(CHUNK, COLS)
+    sends = [send_x(outer[:, w]) for w in (left, right)]
+    parts = [around(sends[n]) for n in (0, 1)]
+    inner_kept = inner_kept + after(inner_next, sends)
     inner_far = move(inner_kept, ALONG[2])
 
-    outer_kept, outer_sent = halves(add_x(after(outer_parts, inner_kept)))
-    outer_kept = outer_kept + move(outer_sent, ALONG[1])
-    outer_far = move(outer_kept, ALONG[2])
-    inner_t = (inner_kept + after(inner_far, outer_kept)) * inner_weight
+    kept_a, sent_a = halves(add_x(after(parts[0], inner_kept)))
+    kept_a = kept_a + move(sent_a, ALONG[1])
+    far_a = move(kept_a, ALONG[2])
+    kept_b, sent_b = halves(add_x(after(parts[1], kept_a)))
+    next_b = move(sent_b, ALONG[1])
+
+    inner_t = (inner_kept + after(inner_far, sent_b)) * inner_weight
     inner_other = move(inner_t, ALONG[1])
-    outer_t = (outer_kept + after(outer_far, inner_t)) * outer_weight
-    outer_other = move(outer_t, ALONG[1])
-    inner_quarter = join(inner_t, after(inner_other, outer_t))
+    t_a = (kept_a + after(far_a, inner_t)) * outer_weight[:, left]
+    other_a = move(t_a, ALONG[1])
+    kept_b = kept_b + after(next_b, t_a)
+    far_b = move(kept_b, ALONG[2])
+
+    quarter_a = join(t_a, after(other_a, kept_b))
+    pieces_a = around([quarter_a] * X)
+    inner_quarter = join(inner_t, after(inner_other, quarter_a))
     inner_pieces = around([inner_quarter] * X)
-    outer_other = after(outer_other, inner_quarter)
-
-    spans = [slice(w * CHUNK, (w + 1) * CHUNK) for w in range(COLS // CHUNK)]
-    quarters = [join(outer_t[:, w], outer_other[:, w]) for w in spans]
-    pieces = [around([q] * X) for q in quarters]
-    outer_all, incoming, earlier = [], [[], []], quarters
-    for n in range(len(spans)):
-        outer_all.append(in_order(after(pieces[n], earlier)))
-        outgoing = dot(slab_two, outer_all[n], 1, 0)
-        for c in (0, 1):
-            incoming[c].append(move(outgoing, UP[c]))
-        earlier = outgoing
+    t_b = (kept_b + after(far_b, inner_quarter)) * outer_weight[:, right]
+    other_b = move(t_b, ALONG[1])
+
+    all_a = in_order(after(pieces_a, t_b))
+    leaving_a = dot(slab_two, all_a, 1, 0)
+    incoming_a = [move(leaving_a, UP[c]) for c in (0, 1)]
+    quarter_b = join(t_b, after(other_b, leaving_a))
+    pieces_b = around([quarter_b] * X)
+    all_b = in_order(pieces_b)
+    outgoing = dot(slab_two, all_b, 1, 0)
+    incoming_b = [move(outgoing, UP[c]) for c in (0, 1)]
+    incoming = [incoming_a[0], incoming_b[0], incoming_a[1], incoming_b[1]]
 
     inner_all = in_order(after(inner_pieces, outgoing))
     to_one = dot(two_cols, inner_all, 1, 1)
@@ -177,8 +190,8 @@
         jnp.concatenate([near_cols, far_cols], 0),
         jnp.concatenate([far_cols, near_cols], 0),
     )
-    three_cols, outer_all = after((three_cols, outer_all), outgoing)
-    beyond = sum(dot(three_cols[:, w], t, 1, 1) for w, t in zip(spans, outer_all))
+    three_cols, all_a, all_b = after((three_cols, all_a, all_b), outgoing)
+    beyond = dot(three_cols[:, left], all_a, 1, 1) + dot(three_cols[:, right], all_b, 1, 1)
     blank = jnp.zeros_like(to_two)
     to_two = beyond + jnp.where(
         first,
@@ -188,7 +201,7 @@
     crossed = move(jnp.where(first, to_two, to_one), SWAP)
     density = jnp.where(first, to_one, to_two) + crossed
     incoming = after(incoming, density)
-    density = density + jnp.concatenate(incoming[0] + incoming[1], 1)
+    density = density + jnp.concatenate(incoming, 1)
     return density[None]
 
 

time: 286 us -> 279 us (0.976)
  the two profiles are of different devices: /device:TPU:184 before, /device:TPU:24 now
where the time goes in v4:
time: 279 us; the launch traced here: 278 us
  starting transfers between devices  132 us (47%)
  waiting for transfers between devices  96.4 us (35%)
  matrix products  19.3 us (7%)
  other arithmetic  14.7 us (5%)
  local copies, waits for them, and re-layouts  14 us (5%)
    ppermute x36, starting transfers between devices, move(): return lax.ppermute(block, AXES, pairs)  132 us
    ppermute x36, waiting for transfers between devices, move(): return lax.ppermute(block, AXES, pairs)  96.4 us
    dot_general x12, matrix products, dot(): lax.dot_general(a, b, (((da,), (db,)), ((), ())), precision=lax.Precision...  19.3 us
  transfers between devices with their start and end apart: 36, of which 14 were waited for; matrix products, arithmetic and copies ran while one was open for 13% of the time, Pallas kernels for 0%

profile of v4, /device:TPU:24, one launch (start us, length us, event | category | flops | bytes accessed | tf_op | source)
XLA Modules:
  0.0 277.6 jit_solution(17417174492434864984)
XLA Ops:
  0.0 1.9 collective-permute-start
  1.9 3.1 %slice_bitcast_fusion = (f32[256,1024]{1,0:T(8,128)}, f32[256,1024]{1,0:T(8,128)}) fusion(f32[1,512,1024]{2,1,0:T(8,128)} %param.4), kind=kLoop, calls=%fused_computation.8 | loop fusion | bytes 4194304 | tf_op jit(solution)/shard_map/slice | solution.py:120
  5.0 10.8 %collective-permute-start.5 = (f32[256,1024]{1,0:T(8,128)}, f32[256,1024]{1,0:T(8,128)S(1)}, u32[]{:S(2)}, u32[]{:S(2)}) collective-permute-start(f32[256,1024]{1,0:T(8,128)} %get-tuple-element.98), channel_id=1, source_target_pairs={{0,480},{1,481},{2,482},{3,483},{4,484},{5,485},{6,486},{7,487},{8... | collective-permute-start | bytes 3145736 | tf_op jit(solution)/shard_map/ppermute | solution.py:33
  15.8 2.3 collective-permute-start.6
  18.1 2.7 broadcast_select_fusion.2
  20.8 1.8 fusion.7
  22.6 1.9 multiply_subtract_fusion.1
  24.8 3.5 %collective-permute-start.1 = (f32[256,512]{1,0:T(8,128)S(1)}, f32[256,512]{1,0:T(8,128)S(1)}, u32[]{:S(2)}, u32[]{:S(2)}) collective-permute-start(f32[256,512]{1,0:T(8,128)S(1)} %get-tuple-element.105), channel_id=1, source_target_pairs={{0,4},{1,5},{2,6},{3,7},{4,8},{5,9},{6,10},{7,11},{8,12},{9,13},{1... | collective-permute-start | bytes 1572872 | tf_op jit(solution)/shard_map/ppermute | solution.py:33
  28.4 4.6 %collective-permute-start.2 = (f32[256,512]{1,0:T(8,128)S(1)}, f32[256,512]{1,0:T(8,128)S(1)}, u32[]{:S(2)}, u32[]{:S(2)}) collective-permute-start(f32[256,512]{1,0:T(8,128)S(1)} %get-tuple-element.104), channel_id=1, source_target_pairs={{0,8},{1,9},{2,10},{3,11},{4,12},{5,13},{6,14},{7,15},{8,0},{9,1},... | collective-permute-start | bytes 1572872 | tf_op jit(solution)/shard_map/ppermute | solution.py:33
  33.0 3.3 %collective-permute-start.3 = (f32[256,512]{1,0:T(8,128)S(1)}, f32[256,512]{1,0:T(8,128)S(1)}, u32[]{:S(2)}, u32[]{:S(2)}) collective-permute-start(f32[256,512]{1,0:T(8,128)S(1)} %get-tuple-element.103), channel_id=1, source_target_pairs={{0,12},{1,13},{2,14},{3,15},{4,0},{5,1},{6,2},{7,3},{8,4},{9,5},{1... | collective-permute-start | bytes 1572872 | tf_op jit(solution)/shard_map/ppermute | solution.py:33
  36.4 1.3 fusion.24
  41.6 1.5 constant_dynamic-slice_fusion.13
  43.1 2.8 fusion.15
  48.0 10.7 %collective-permute-done.6 = f32[256,1024]{1,0:T(8,128)} collective-permute-done((f32[256,1024]{1,0:T(8,128)}, f32[256,1024]{1,0:T(8,128)}, u32[]{:S(2)}, u32[]{:S(2)}) %collective-permute-start.6) | collective-permute-done | bytes 1048608 | tf_op jit(solution)/shard_map/ppermute | solution.py:33
  58.7 1.7 add.323
  60.4 1.9 collective-permute-start.7
  62.3 11.0 %collective-permute-start.4 = (f32[128,512]{1,0:T(8,128)}, f32[128,512]{1,0:T(8,128)S(1)}, u32[]{:S(2)}, u32[]{:S(2)}) collective-permute-start(f32[128,512]{1,0:T(8,128)} %constant_dynamic-slice_fusion.12), channel_id=1, source_target_pairs={{0,1},{1,0},{2,3},{3,2},{4,5},{5,4},{6,7},{7,6},{8,9},{9,8},{10,11... | collective-permute-start | bytes 786440 | tf_op jit(solution)/shard_map/ppermute | solution.py:33
  74.2 2.3 fusion.27
  79.8 2.5 subtract_add_fusion
  82.6 3.5 %collective-permute-start.12 = (f32[256,256]{1,0:T(8,128)S(1)}, f32[256,256]{1,0:T(8,128)S(1)}, u32[]{:S(2)}, u32[]{:S(2)}) collective-permute-start(f32[256,256]{1,0:T(8,128)S(1)} %get-tuple-element.113), channel_id=1, source_target_pairs={{0,4},{1,5},{2,6},{3,7},{4,8},{5,9},{6,10},{7,11},{8,12},{9,13},{1... | collective-permute-start | bytes 786440 | tf_op jit(solution)/shard_map/ppermute | solution.py:33
  86.1 4.6 %collective-permute-start.13 = (f32[256,256]{1,0:T(8,128)S(1)}, f32[256,256]{1,0:T(8,128)S(1)}, u32[]{:S(2)}, u32[]{:S(2)}) collective-permute-start(f32[256,256]{1,0:T(8,128)S(1)} %get-tuple-element.112), channel_id=1, source_target_pairs={{0,8},{1,9},{2,10},{3,11},{4,12},{5,13},{6,14},{7,15},{8,0},{9,1},... | collective-permute-start | bytes 786440 | tf_op jit(solution)/shard_map/ppermute | solution.py:33
  90.8 3.5 %collective-permute-start.14 = (f32[256,256]{1,0:T(8,128)S(1)}, f32[256,256]{1,0:T(8,128)S(1)}, u32[]{:S(2)}, u32[]{:S(2)}) collective-permute-start(f32[256,256]{1,0:T(8,128)S(1)} %get-tuple-element.111), channel_id=1, source_target_pairs={{0,12},{1,13},{2,14},{3,15},{4,0},{5,1},{6,2},{7,3},{8,4},{9,5},{1... | collective-permute-start | bytes 786440 | tf_op jit(solution)/shard_map/ppermute | solution.py:33
  96.0 4.4 %collective-permute-done.13 = f32[256,256]{1,0:T(8,128)S(1)} collective-permute-done((f32[256,256]{1,0:T(8,128)S(1)}, f32[256,256]{1,0:T(8,128)S(1)}, u32[]{:S(2)}, u32[]{:S(2)}) %collective-permute-start.13) | collective-permute-done | bytes 262176 | tf_op jit(solution)/shard_map/ppermute | solution.py:33
  100.4 1.5 collective-permute-done.14
  102.6 2.2 collective-permute-start.15
  104.8 4.3 %collective-permute-start.9 = (f32[256,256]{1,0:T(8,128)}, f32[256,256]{1,0:T(8,128)}, u32[]{:S(2)}, u32[]{:S(2)}) collective-permute-start(f32[256,256]{1,0:T(8,128)} %get-tuple-element.109), channel_id=1, source_target_pairs={{0,4},{1,5},{2,6},{3,7},{4,8},{5,9},{6,10},{7,11},{8,12},{9,13},{1... | collective-permute-start | bytes 786440 | tf_op jit(solution)/shard_map/ppermute | solution.py:33
  109.1 3.6 %collective-permute-start.10 = (f32[256,256]{1,0:T(8,128)}, f32[256,256]{1,0:T(8,128)}, u32[]{:S(2)}, u32[]{:S(2)}) collective-permute-start(f32[256,256]{1,0:T(8,128)} %get-tuple-element.108), channel_id=1, source_target_pairs={{0,8},{1,9},{2,10},{3,11},{4,12},{5,13},{6,14},{7,15},{8,0},{9,1},... | collective-permute-start | bytes 786440 | tf_op jit(solution)/shard_map/ppermute | solution.py:33
  112.8 3.5 %collective-permute-start.11 = (f32[256,256]{1,0:T(8,128)}, f32[256,256]{1,0:T(8,128)}, u32[]{:S(2)}, u32[]{:S(2)}) collective-permute-start(f32[256,256]{1,0:T(8,128)} %get-tuple-element.107), channel_id=1, source_target_pairs={{0,12},{1,13},{2,14},{3,15},{4,0},{5,1},{6,2},{7,3},{8,4},{9,5},{1... | collective-permute-start | bytes 786440 | tf_op jit(solution)/shard_map/ppermute | solution.py:33
  116.3 8.7 %collective-permute-start.8 = (f32[128,512]{1,0:T(8,128)}, f32[128,512]{1,0:T(8,128)S(1)}, u32[]{:S(2)}, u32[]{:S(2)}) collective-permute-start(f32[128,512]{1,0:T(8,128)} %dynamic-slice_add_fusion), channel_id=1, source_target_pairs={{0,2},{1,3},{2,0},{3,1},{4,6},{5,7},{6,4},{7,5},{8,10},{9,11},{10,... | collective-permute-start | bytes 786440 | tf_op jit(solution)/shard_map/ppermute | solution.py:33
  125.1 1.9 collective-permute-start.17
  128.3 2.2 collective-permute-start.19
  130.5 8.2 %collective-permute-done.8 = f32[128,512]{1,0:T(8,128)S(1)} collective-permute-done((f32[128,512]{1,0:T(8,128)}, f32[128,512]{1,0:T(8,128)S(1)}, u32[]{:S(2)}, u32[]{:S(2)}) %collective-permute-start.8) | collective-permute-done | bytes 262176 | tf_op jit(solution)/shard_map/ppermute | solution.py:33
  138.7 2.9 %collective-permute-start.16 = (f32[128,512]{1,0:T(8,128)S(1)}, f32[128,512]{1,0:T(8,128)S(1)}, u32[]{:S(2)}, u32[]{:S(2)}) collective-permute-start(f32[128,512]{1,0:T(8,128)S(1)} %add_multiply_fusion), channel_id=1, source_target_pairs={{0,1},{1,0},{2,3},{3,2},{4,5},{5,4},{6,7},{7,6},{8,9},{9,8},{10,11... | collective-permute-start | bytes 786440 | tf_op jit(solution)/shard_map/ppermute | solution.py:33
  141.7 2.9 %collective-permute-start.18 = (f32[128,256]{1,0:T(8,128)S(1)}, f32[128,256]{1,0:T(8,128)S(1)}, u32[]{:S(2)}, u32[]{:S(2)}) collective-permute-start(f32[128,256]{1,0:T(8,128)S(1)} %slice_multiply_fusion.1), channel_id=1, source_target_pairs={{0,1},{1,0},{2,3},{3,2},{4,5},{5,4},{6,7},{7,6},{8,9},{9,8},{10,11... | collective-permute-start | bytes 393224 | tf_op jit(solution)/shard_map/ppermute | solution.py:33
  144.7 4.3 %collective-permute-start.23 = (f32[128,256]{1,0:T(8,128)S(1)}, f32[128,256]{1,0:T(8,128)S(1)}, u32[]{:S(2)}, u32[]{:S(2)}) collective-permute-start(f32[128,256]{1,0:T(8,128)S(1)} %dynamic-slice_add_fusion.1), channel_id=1, source_target_pairs={{0,2},{1,3},{2,0},{3,1},{4,6},{5,7},{6,4},{7,5},{8,10},{9,11},{10,... | collective-permute-start | bytes 393224 | tf_op jit(solution)/shard_map/ppermute | solution.py:33
  149.0 4.9 %collective-permute-done.18 = f32[128,256]{1,0:T(8,128)S(1)} collective-permute-done((f32[128,256]{1,0:T(8,128)S(1)}, f32[128,256]{1,0:T(8,128)S(1)}, u32[]{:S(2)}, u32[]{:S(2)}) %collective-permute-start.18) | collective-permute-done | bytes 131104 | tf_op jit(solution)/shard_map/ppermute | solution.py:33
  153.9 2.2 collective-permute-start.25
  156.1 4.2 %collective-permute-start.26 = (f32[256,256]{1,0:T(8,128)S(1)}, f32[256,256]{1,0:T(8,128)S(1)}, u32[]{:S(2)}, u32[]{:S(2)}) collective-permute-start(f32[256,256]{1,0:T(8,128)S(1)} %maximum_select_fusion.2), channel_id=1, source_target_pairs={{0,8},{1,9},{2,10},{3,11},{4,12},{5,13},{6,14},{7,15},{8,0},{9,1},... | collective-permute-start | bytes 786440 | tf_op jit(solution)/shard_map/ppermute | solution.py:33
  160.3 2.8 %collective-permute-start.27 = (f32[256,256]{1,0:T(8,128)S(1)}, f32[256,256]{1,0:T(8,128)S(1)}, u32[]{:S(2)}, u32[]{:S(2)}) collective-permute-start(f32[256,256]{1,0:T(8,128)S(1)} %maximum_select_fusion.2), channel_id=1, source_target_pairs={{0,12},{1,13},{2,14},{3,15},{4,0},{5,1},{6,2},{7,3},{8,4},{9,5},{1... | collective-permute-start | bytes 786440 | tf_op jit(solution)/shard_map/ppermute | solution.py:33
  163.2 1.9 collective-permute-start.24
  165.2 3.9 %collective-permute-done.25 = f32[256,256]{1,0:T(8,128)S(1)} collective-permute-done((f32[256,256]{1,0:T(8,128)S(1)}, f32[256,256]{1,0:T(8,128)S(1)}, u32[]{:S(2)}, u32[]{:S(2)}) %collective-permute-start.25) | collective-permute-done | bytes 262176 | tf_op jit(solution)/shard_map/ppermute | solution.py:33
  169.1 2.5 collective-permute-done.27
  173.0 2.5 collective-permute-start.28
  175.5 5.4 %collective-permute-start.29 = (f32[256,256]{1,0:T(8,128)S(1)}, f32[256,256]{1,0:T(8,128)S(1)}, u32[]{:S(2)}, u32[]{:S(2)}) collective-permute-start(f32[256,256]{1,0:T(8,128)S(1)} %get-tuple-element.92), channel_id=1, source_target_pairs={{0,8},{1,9},{2,10},{3,11},{4,12},{5,13},{6,14},{7,15},{8,0},{9,1},... | collective-permute-start | bytes 786440 | tf_op jit(solution)/shard_map/ppermute | solution.py:33
  180.9 1.9 collective-permute-start.30
  183.0 3.9 %collective-permute-start.20 = (f32[256,512]{1,0:T(8,128)S(1)}, f32[256,512]{1,0:T(8,128)S(1)}, u32[]{:S(2)}, u32[]{:S(2)}) collective-permute-start(f32[256,512]{1,0:T(8,128)S(1)} %maximum_select_fusion.1), channel_id=1, source_target_pairs={{0,4},{1,5},{2,6},{3,7},{4,8},{5,9},{6,10},{7,11},{8,12},{9,13},{1... | collective-permute-start | bytes 1572872 | tf_op jit(solution)/shard_map/ppermute | solution.py:33
  186.9 1.9 collective-permute-start.21
  188.9 4.6 %collective-permute-start.22 = (f32[256,512]{1,0:T(8,128)S(1)}, f32[256,512]{1,0:T(8,128)S(1)}, u32[]{:S(2)}, u32[]{:S(2)}) collective-permute-start(f32[256,512]{1,0:T(8,128)S(1)} %maximum_select_fusion.1), channel_id=1, source_target_pairs={{0,12},{1,13},{2,14},{3,15},{4,0},{5,1},{6,2},{7,3},{8,4},{9,5},{1... | collective-permute-start | bytes 1572872 | tf_op jit(solution)/shard_map/ppermute | solution.py:33
  194.6 8.4 %collective-permute-done.20 = f32[256,512]{1,0:T(8,128)S(1)} collective-permute-done((f32[256,512]{1,0:T(8,128)S(1)}, f32[256,512]{1,0:T(8,128)S(1)}, u32[]{:S(2)}, u32[]{:S(2)}) %collective-permute-start.20) | collective-permute-done | bytes 524320 | tf_op jit(solution)/shard_map/ppermute | solution.py:33
  203.0 9.3 %collective-permute-done.21 = f32[256,512]{1,0:T(8,128)S(1)} collective-permute-done((f32[256,512]{1,0:T(8,128)S(1)}, f32[256,512]{1,0:T(8,128)S(1)}, u32[]{:S(2)}, u32[]{:S(2)}) %collective-permute-start.21) | collective-permute-done | bytes 524320 | tf_op jit(solution)/shard_map/ppermute | solution.py:33
  212.2 1.4 collective-permute-done.22
  214.1 2.0 fusion.5
  216.1 1.9 fusion.31
  219.1 1.5 broadcast_select_fusion
  220.6 1.9 collective-permute-start.31
  222.5 2.1 collective-permute-start.32
  224.6 1.3 collective-permute-start.34
  225.9 6.5 %collective-permute-start.33 = (f32[512,256]{1,0:T(8,128)S(1)}, f32[512,256]{1,0:T(8,128)S(1)}, u32[]{:S(2)}, u32[]{:S(2)}) collective-permute-start(f32[512,256]{1,0:T(8,128)S(1)} %fusion.30), channel_id=1, source_target_pairs={{0,32},{1,33},{2,34},{3,35},{4,36},{5,37},{6,38},{7,39},{8,40},{9,... | collective-permute-start | bytes 1572872 | tf_op jit(solution)/shard_map/ppermute | solution.py:33
  232.5 1.3 collective-permute-start.35
  234.7 16.6 %collective-permute-done.32 = f32[512,256]{1,0:T(8,128)S(1)} collective-permute-done((f32[512,256]{1,0:T(8,128)S(1)}, f32[512,256]{1,0:T(8,128)S(1)}, u32[]{:S(2)}, u32[]{:S(2)}) %collective-permute-start.32) | collective-permute-done | bytes 524320 | tf_op jit(solution)/shard_map/ppermute | solution.py:33
  251.3 6.2 %collective-permute-done.34 = f32[512,256]{1,0:T(8,128)S(1)} collective-permute-done((f32[512,256]{1,0:T(8,128)S(1)}, f32[512,256]{1,0:T(8,128)S(1)}, u32[]{:S(2)}, u32[]{:S(2)}) %collective-permute-start.34) | collective-permute-done | bytes 524320 | tf_op jit(solution)/shard_map/ppermute | solution.py:33
  257.5 15.9 %collective-permute-done.33 = f32[512,256]{1,0:T(8,128)S(1)} collective-permute-done((f32[512,256]{1,0:T(8,128)S(1)}, f32[512,256]{1,0:T(8,128)S(1)}, u32[]{:S(2)}, u32[]{:S(2)}) %collective-permute-start.33) | collective-permute-done | bytes 524320 | tf_op jit(solution)/shard_map/ppermute | solution.py:33
  273.4 2.5 collective-permute-done.35
  276.0 1.6 fusion
  (100 shorter events, 19.3 us)
Async XLA Ops:
  0.0 18.1 %collective-permute-start = (f32[512,1024]{1,0:T(8,128)}, f32[512,1024]{1,0:T(8,128)}, u32[]{:S(2)}, u32[]{:S(2)}) collective-permute-start(f32[512,1024]{1,0:T(8,128)} %bitcast.34), channel_id=1, source_target_pairs={{0,16},{1,17},{2,18},{3,19},{4,20},{5,21},{6,22},{7,23},{8,24},{9,... | collective-permute-start | bytes 6291464 | tf_op jit(solution)/shard_map/ppermute | solution.py:33
  5.0 41.9 %collective-permute-start.5 = (f32[256,1024]{1,0:T(8,128)}, f32[256,1024]{1,0:T(8,128)S(1)}, u32[]{:S(2)}, u32[]{:S(2)}) collective-permute-start(f32[256,1024]{1,0:T(8,128)} %get-tuple-element.98), channel_id=1, source_target_pairs={{0,480},{1,481},{2,482},{3,483},{4,484},{5,485},{6,486},{7,487},{8... | collective-permute-start | bytes 3145736 | tf_op jit(solution)/shard_map/ppermute | solution.py:33
  15.8 42.8 %collective-permute-start.6 = (f32[256,1024]{1,0:T(8,128)}, f32[256,1024]{1,0:T(8,128)}, u32[]{:S(2)}, u32[]{:S(2)}) collective-permute-start(f32[256,1024]{1,0:T(8,128)} %get-tuple-element.97), channel_id=1, source_target_pairs={{0,496},{1,497},{2,498},{3,499},{4,500},{5,501},{6,502},{7,503},{8... | collective-permute-start | bytes 3145736 | tf_op jit(solution)/shard_map/ppermute | solution.py:33
  20.8 1.9 copy-start
  24.8 12.9 %copy-start.12 = (s32[32]{0:T(128)S(1)}, s32[32]{0:T(128)}, u32[]{:S(2)}) copy-start(s32[32]{0:T(128)} %param.7) | copy-start | bytes 388
  24.8 14.8 %copy-start.14 = (f32[1024]{0:T(1024)S(1)}, f32[1024]{0:T(1024)}, u32[]{:S(2)}) copy-start(f32[1024]{0:T(1024)} %param.6) | copy-start | bytes 12292
  24.8 14.9 %copy-start.13 = (f32[32]{0:T(128)S(1)}, f32[32]{0:T(128)}, u32[]{:S(2)}) copy-start(f32[32]{0:T(128)} %param.5) | copy-start | bytes 388
  24.8 21.1 %collective-permute-start.1 = (f32[256,512]{1,0:T(8,128)S(1)}, f32[256,512]{1,0:T(8,128)S(1)}, u32[]{:S(2)}, u32[]{:S(2)}) collective-permute-start(f32[256,512]{1,0:T(8,128)S(1)} %get-tuple-element.105), channel_id=1, source_target_pairs={{0,4},{1,5},{2,6},{3,7},{4,8},{5,9},{6,10},{7,11},{8,12},{9,13},{1... | collective-permute-start | bytes 1572872 | tf_op jit(solution)/shard_map/ppermute | solution.py:33
  28.4 17.6 %collective-permute-start.2 = (f32[256,512]{1,0:T(8,128)S(1)}, f32[256,512]{1,0:T(8,128)S(1)}, u32[]{:S(2)}, u32[]{:S(2)}) collective-permute-start(f32[256,512]{1,0:T(8,128)S(1)} %get-tuple-element.104), channel_id=1, source_target_pairs={{0,8},{1,9},{2,10},{3,11},{4,12},{5,13},{6,14},{7,15},{8,0},{9,1},... | collective-permute-start | bytes 1572872 | tf_op jit(solution)/shard_map/ppermute | solution.py:33
  33.0 12.9 %collective-permute-start.3 = (f32[256,512]{1,0:T(8,128)S(1)}, f32[256,512]{1,0:T(8,128)S(1)}, u32[]{:S(2)}, u32[]{:S(2)}) collective-permute-start(f32[256,512]{1,0:T(8,128)S(1)} %get-tuple-element.103), channel_id=1, source_target_pairs={{0,12},{1,13},{2,14},{3,15},{4,0},{5,1},{6,2},{7,3},{8,4},{9,5},{1... | collective-permute-start | bytes 1572872 | tf_op jit(solution)/shard_map/ppermute | solution.py:33
  46.1 12.5 %copy-start.5 = (f32[256,512]{1,0:T(8,128)}, f32[256,512]{1,0:T(8,128)S(1)}, u32[]{:S(2)}) copy-start(f32[256,512]{1,0:T(8,128)S(1)} %add_add_fusion) | copy-start | bytes 1572868
  47.0 1.0 copy-start.9
  60.4 17.3 %collective-permute-start.7 = (f32[256,1024]{1,0:T(8,128)S(1)}, f32[256,1024]{1,0:T(8,128)}, u32[]{:S(2)}, u32[]{:S(2)}) collective-permute-start(f32[256,1024]{1,0:T(8,128)S(1)} %add.323), channel_id=1, source_target_pairs={{0,16},{1,17},{2,18},{3,19},{4,20},{5,21},{6,22},{7,23},{8,24},{9,... | collective-permute-start | bytes 3145736 | tf_op jit(solution)/shard_map/ppermute | solution.py:33
  62.3 32.9 %collective-permute-start.4 = (f32[128,512]{1,0:T(8,128)}, f32[128,512]{1,0:T(8,128)S(1)}, u32[]{:S(2)}, u32[]{:S(2)}) collective-permute-start(f32[128,512]{1,0:T(8,128)} %constant_dynamic-slice_fusion.12), channel_id=1, source_target_pairs={{0,1},{1,0},{2,3},{3,2},{4,5},{5,4},{6,7},{7,6},{8,9},{9,8},{10,11... | collective-permute-start | bytes 786440 | tf_op jit(solution)/shard_map/ppermute | solution.py:33
  73.4 0.8 copy-start.2
  74.1 2.3 copy-start.7
  76.5 2.2 copy-start.4
  78.7 1.0 copy-start.8
  82.5 12.8 %copy-start.6 = (f32[256,512]{1,0:T(8,128)S(1)}, f32[256,512]{1,0:T(8,128)}, u32[]{:S(2)}) copy-start(f32[256,512]{1,0:T(8,128)} %copy-done.5) | copy-start | bytes 1572868
  82.6 13.4 %collective-permute-start.12 = (f32[256,256]{1,0:T(8,128)S(1)}, f32[256,256]{1,0:T(8,128)S(1)}, u32[]{:S(2)}, u32[]{:S(2)}) collective-permute-start(f32[256,256]{1,0:T(8,128)S(1)} %get-tuple-element.113), channel_id=1, source_target_pairs={{0,4},{1,5},{2,6},{3,7},{4,8},{5,9},{6,10},{7,11},{8,12},{9,13},{1... | collective-permute-start | bytes 786440 | tf_op jit(solution)/shard_map/ppermute | solution.py:33
  86.1 14.2 %collective-permute-start.13 = (f32[256,256]{1,0:T(8,128)S(1)}, f32[256,256]{1,0:T(8,128)S(1)}, u32[]{:S(2)}, u32[]{:S(2)}) collective-permute-start(f32[256,256]{1,0:T(8,128)S(1)} %get-tuple-element.112), channel_id=1, source_target_pairs={{0,8},{1,9},{2,10},{3,11},{4,12},{5,13},{6,14},{7,15},{8,0},{9,1},... | collective-permute-start | bytes 786440 | tf_op jit(solution)/shard_map/ppermute | solution.py:33
  90.8 11.1 %collective-permute-start.14 = (f32[256,256]{1,0:T(8,128)S(1)}, f32[256,256]{1,0:T(8,128)S(1)}, u32[]{:S(2)}, u32[]{:S(2)}) collective-permute-start(f32[256,256]{1,0:T(8,128)S(1)} %get-tuple-element.111), channel_id=1, source_target_pairs={{0,12},{1,13},{2,14},{3,15},{4,0},{5,1},{6,2},{7,3},{8,4},{9,5},{1... | collective-permute-start | bytes 786440 | tf_op jit(solution)/shard_map/ppermute | solution.py:33
  102.6 22.5 %collective-permute-start.15 = (f32[128,256]{1,0:T(8,128)}, f32[128,256]{1,0:T(8,128)S(1)}, u32[]{:S(2)}, u32[]{:S(2)}) collective-permute-start(f32[128,256]{1,0:T(8,128)} %constant_dynamic-slice_fusion.1), channel_id=1, source_target_pairs={{0,1},{1,0},{2,3},{3,2},{4,5},{5,4},{6,7},{7,6},{8,9},{9,8},{10,11... | collective-permute-start | bytes 393224 | tf_op jit(solution)/shard_map/ppermute | solution.py:33
  104.8 22.2 %collective-permute-start.9 = (f32[256,256]{1,0:T(8,128)}, f32[256,256]{1,0:T(8,128)}, u32[]{:S(2)}, u32[]{:S(2)}) collective-permute-start(f32[256,256]{1,0:T(8,128)} %get-tuple-element.109), channel_id=1, source_target_pairs={{0,4},{1,5},{2,6},{3,7},{4,8},{5,9},{6,10},{7,11},{8,12},{9,13},{1... | collective-permute-start | bytes 786440 | tf_op jit(solution)/shard_map/ppermute | solution.py:33
  109.1 17.9 %collective-permute-start.10 = (f32[256,256]{1,0:T(8,128)}, f32[256,256]{1,0:T(8,128)}, u32[]{:S(2)}, u32[]{:S(2)}) collective-permute-start(f32[256,256]{1,0:T(8,128)} %get-tuple-element.108), channel_id=1, source_target_pairs={{0,8},{1,9},{2,10},{3,11},{4,12},{5,13},{6,14},{7,15},{8,0},{9,1},... | collective-permute-start | bytes 786440 | tf_op jit(solution)/shard_map/ppermute | solution.py:33
  112.8 14.3 %collective-permute-start.11 = (f32[256,256]{1,0:T(8,128)}, f32[256,256]{1,0:T(8,128)}, u32[]{:S(2)}, u32[]{:S(2)}) collective-permute-start(f32[256,256]{1,0:T(8,128)} %get-tuple-element.107), channel_id=1, source_target_pairs={{0,12},{1,13},{2,14},{3,15},{4,0},{5,1},{6,2},{7,3},{8,4},{9,5},{1... | collective-permute-start | bytes 786440 | tf_op jit(solution)/shard_map/ppermute | solution.py:33
  116.3 22.4 %copy-start.10 = (f32[128,512]{1,0:T(8,128)S(1)}, f32[128,512]{1,0:T(8,128)}, u32[]{:S(2)}) copy-start(f32[128,512]{1,0:T(8,128)} %get-tuple-element.68) | copy-start | bytes 786436
  116.3 22.3 %copy-start.11 = (f32[128,512]{1,0:T(8,128)S(1)}, f32[128,512]{1,0:T(8,128)}, u32[]{:S(2)}) copy-start(f32[128,512]{1,0:T(8,128)} %dynamic-slice_add_fusion) | copy-start | bytes 786436
  116.3 22.3 %collective-permute-start.8 = (f32[128,512]{1,0:T(8,128)}, f32[128,512]{1,0:T(8,128)S(1)}, u32[]{:S(2)}, u32[]{:S(2)}) collective-permute-start(f32[128,512]{1,0:T(8,128)} %dynamic-slice_add_fusion), channel_id=1, source_target_pairs={{0,2},{1,3},{2,0},{3,1},{4,6},{5,7},{6,4},{7,5},{8,10},{9,11},{10,... | collective-permute-start | bytes 786440 | tf_op jit(solution)/shard_map/ppermute | solution.py:33
  125.1 16.6 %collective-permute-start.17 = (f32[128,256]{1,0:T(8,128)S(1)}, f32[128,256]{1,0:T(8,128)S(1)}, u32[]{:S(2)}, u32[]{:S(2)}) collective-permute-start(f32[128,256]{1,0:T(8,128)S(1)} %dynamic-slice_add_fusion.2), channel_id=1, source_target_pairs={{0,2},{1,3},{2,0},{3,1},{4,6},{5,7},{6,4},{7,5},{8,10},{9,11},{10,... | collective-permute-start | bytes 393224 | tf_op jit(solution)/shard_map/ppermute | solution.py:33
  128.3 16.4 %collective-permute-start.19 = (f32[128,256]{1,0:T(8,128)S(1)}, f32[128,256]{1,0:T(8,128)S(1)}, u32[]{:S(2)}, u32[]{:S(2)}) collective-permute-start(f32[128,256]{1,0:T(8,128)S(1)} %constant_dynamic-slice_fusion), channel_id=1, source_target_pairs={{0,1},{1,0},{2,3},{3,2},{4,5},{5,4},{6,7},{7,6},{8,9},{9,8},{10,11... | collective-permute-start | bytes 393224 | tf_op jit(solution)/shard_map/ppermute | solution.py:33
  138.7 24.4 %collective-permute-start.16 = (f32[128,512]{1,0:T(8,128)S(1)}, f32[128,512]{1,0:T(8,128)S(1)}, u32[]{:S(2)}, u32[]{:S(2)}) collective-permute-start(f32[128,512]{1,0:T(8,128)S(1)} %add_multiply_fusion), channel_id=1, source_target_pairs={{0,1},{1,0},{2,3},{3,2},{4,5},{5,4},{6,7},{7,6},{8,9},{9,8},{10,11... | collective-permute-start | bytes 786440 | tf_op jit(solution)/shard_map/ppermute | solution.py:33
  141.7 12.1 %collective-permute-start.18 = (f32[128,256]{1,0:T(8,128)S(1)}, f32[128,256]{1,0:T(8,128)S(1)}, u32[]{:S(2)}, u32[]{:S(2)}) collective-permute-start(f32[128,256]{1,0:T(8,128)S(1)} %slice_multiply_fusion.1), channel_id=1, source_target_pairs={{0,1},{1,0},{2,3},{3,2},{4,5},{5,4},{6,7},{7,6},{8,9},{9,8},{10,11... | collective-permute-start | bytes 393224 | tf_op jit(solution)/shard_map/ppermute | solution.py:33
  144.7 18.5 %collective-permute-start.23 = (f32[128,256]{1,0:T(8,128)S(1)}, f32[128,256]{1,0:T(8,128)S(1)}, u32[]{:S(2)}, u32[]{:S(2)}) collective-permute-start(f32[128,256]{1,0:T(8,128)S(1)} %dynamic-slice_add_fusion.1), channel_id=1, source_target_pairs={{0,2},{1,3},{2,0},{3,1},{4,6},{5,7},{6,4},{7,5},{8,10},{9,11},{10,... | collective-permute-start | bytes 393224 | tf_op jit(solution)/shard_map/ppermute | solution.py:33
  153.9 15.2 %collective-permute-start.25 = (f32[256,256]{1,0:T(8,128)S(1)}, f32[256,256]{1,0:T(8,128)S(1)}, u32[]{:S(2)}, u32[]{:S(2)}) collective-permute-start(f32[256,256]{1,0:T(8,128)S(1)} %maximum_select_fusion.2), channel_id=1, source_target_pairs={{0,4},{1,5},{2,6},{3,7},{4,8},{5,9},{6,10},{7,11},{8,12},{9,13},{1... | collective-permute-start | bytes 786440 | tf_op jit(solution)/shard_map/ppermute | solution.py:33
  156.1 13.0 %collective-permute-start.26 = (f32[256,256]{1,0:T(8,128)S(1)}, f32[256,256]{1,0:T(8,128)S(1)}, u32[]{:S(2)}, u32[]{:S(2)}) collective-permute-start(f32[256,256]{1,0:T(8,128)S(1)} %maximum_select_fusion.2), channel_id=1, source_target_pairs={{0,8},{1,9},{2,10},{3,11},{4,12},{5,13},{6,14},{7,15},{8,0},{9,1},... | collective-permute-start | bytes 786440 | tf_op jit(solution)/shard_map/ppermute | solution.py:33
  160.3 11.3 %collective-permute-start.27 = (f32[256,256]{1,0:T(8,128)S(1)}, f32[256,256]{1,0:T(8,128)S(1)}, u32[]{:S(2)}, u32[]{:S(2)}) collective-permute-start(f32[256,256]{1,0:T(8,128)S(1)} %maximum_select_fusion.2), channel_id=1, source_target_pairs={{0,12},{1,13},{2,14},{3,15},{4,0},{5,1},{6,2},{7,3},{8,4},{9,5},{1... | collective-permute-start | bytes 786440 | tf_op jit(solution)/shard_map/ppermute | solution.py:33
  163.2 9.6 %collective-permute-start.24 = (f32[128,256]{1,0:T(8,128)S(1)}, f32[128,256]{1,0:T(8,128)S(1)}, u32[]{:S(2)}, u32[]{:S(2)}) collective-permute-start(f32[128,256]{1,0:T(8,128)S(1)} %slice_multiply_fusion), channel_id=1, source_target_pairs={{0,1},{1,0},{2,3},{3,2},{4,5},{5,4},{6,7},{7,6},{8,9},{9,8},{10,11... | collective-permute-start | bytes 393224 | tf_op jit(solution)/shard_map/ppermute | solution.py:33
  171.8 11.1 %copy-start.3 = (f32[256,512]{1,0:T(8,128)S(1)}, f32[256,512]{1,0:T(8,128)}, u32[]{:S(2)}) copy-start(f32[256,512]{1,0:T(8,128)} %copy-done.2) | copy-start | bytes 1572868
  173.0 15.9 %collective-permute-start.28 = (f32[256,256]{1,0:T(8,128)S(1)}, f32[256,256]{1,0:T(8,128)S(1)}, u32[]{:S(2)}, u32[]{:S(2)}) collective-permute-start(f32[256,256]{1,0:T(8,128)S(1)} %get-tuple-element.92), channel_id=1, source_target_pairs={{0,4},{1,5},{2,6},{3,7},{4,8},{5,9},{6,10},{7,11},{8,12},{9,13},{1... | collective-permute-start | bytes 786440 | tf_op jit(solution)/shard_map/ppermute | solution.py:33
  175.5 18.0 %collective-permute-start.29 = (f32[256,256]{1,0:T(8,128)S(1)}, f32[256,256]{1,0:T(8,128)S(1)}, u32[]{:S(2)}, u32[]{:S(2)}) collective-permute-start(f32[256,256]{1,0:T(8,128)S(1)} %get-tuple-element.92), channel_id=1, source_target_pairs={{0,8},{1,9},{2,10},{3,11},{4,12},{5,13},{6,14},{7,15},{8,0},{9,1},... | collective-permute-start | bytes 786440 | tf_op jit(solution)/shard_map/ppermute | solution.py:33
  180.9 12.6 %collective-permute-start.30 = (f32[256,256]{1,0:T(8,128)S(1)}, f32[256,256]{1,0:T(8,128)S(1)}, u32[]{:S(2)}, u32[]{:S(2)}) collective-permute-start(f32[256,256]{1,0:T(8,128)S(1)} %get-tuple-element.92), channel_id=1, source_target_pairs={{0,12},{1,13},{2,14},{3,15},{4,0},{5,1},{6,2},{7,3},{8,4},{9,5},{1... | collective-permute-start | bytes 786440 | tf_op jit(solution)/shard_map/ppermute | solution.py:33
  183.0 20.0 %collective-permute-start.20 = (f32[256,512]{1,0:T(8,128)S(1)}, f32[256,512]{1,0:T(8,128)S(1)}, u32[]{:S(2)}, u32[]{:S(2)}) collective-permute-start(f32[256,512]{1,0:T(8,128)S(1)} %maximum_select_fusion.1), channel_id=1, source_target_pairs={{0,4},{1,5},{2,6},{3,7},{4,8},{5,9},{6,10},{7,11},{8,12},{9,13},{1... | collective-permute-start | bytes 1572872 | tf_op jit(solution)/shard_map/ppermute | solution.py:33
  186.9 25.3 %collective-permute-start.21 = (f32[256,512]{1,0:T(8,128)S(1)}, f32[256,512]{1,0:T(8,128)S(1)}, u32[]{:S(2)}, u32[]{:S(2)}) collective-permute-start(f32[256,512]{1,0:T(8,128)S(1)} %maximum_select_fusion.1), channel_id=1, source_target_pairs={{0,8},{1,9},{2,10},{3,11},{4,12},{5,13},{6,14},{7,15},{8,0},{9,1},... | collective-permute-start | bytes 1572872 | tf_op jit(solution)/shard_map/ppermute | solution.py:33
  188.9 24.7 %collective-permute-start.22 = (f32[256,512]{1,0:T(8,128)S(1)}, f32[256,512]{1,0:T(8,128)S(1)}, u32[]{:S(2)}, u32[]{:S(2)}) collective-permute-start(f32[256,512]{1,0:T(8,128)S(1)} %maximum_select_fusion.1), channel_id=1, source_target_pairs={{0,12},{1,13},{2,14},{3,15},{4,0},{5,1},{6,2},{7,3},{8,4},{9,5},{1... | collective-permute-start | bytes 1572872 | tf_op jit(solution)/shard_map/ppermute | solution.py:33
  214.1 2.0 copy-start.1
  220.6 13.2 %collective-permute-start.31 = (f32[512,1024]{1,0:T(8,128)S(1)}, f32[512,1024]{1,0:T(8,128)S(1)}, u32[]{:S(2)}, u32[]{:S(2)}) collective-permute-start(f32[512,1024]{1,0:T(8,128)S(1)} %get-tuple-element.123), channel_id=1, source_target_pairs={{0,16},{1,17},{2,18},{3,19},{4,20},{5,21},{6,22},{7,23},{8,24},{9,... | collective-permute-start | bytes 6291464 | tf_op jit(solution)/shard_map/ppermute | solution.py:33
  222.5 28.8 %collective-permute-start.32 = (f32[512,256]{1,0:T(8,128)S(1)}, f32[512,256]{1,0:T(8,128)S(1)}, u32[]{:S(2)}, u32[]{:S(2)}) collective-permute-start(f32[512,256]{1,0:T(8,128)S(1)} %fusion.29), channel_id=1, source_target_pairs={{0,32},{1,33},{2,34},{3,35},{4,36},{5,37},{6,38},{7,39},{8,40},{9,... | collective-permute-start | bytes 1572872 | tf_op jit(solution)/shard_map/ppermute | solution.py:33
  224.6 32.9 %collective-permute-start.34 = (f32[512,256]{1,0:T(8,128)S(1)}, f32[512,256]{1,0:T(8,128)S(1)}, u32[]{:S(2)}, u32[]{:S(2)}) collective-permute-start(f32[512,256]{1,0:T(8,128)S(1)} %fusion.29), channel_id=1, source_target_pairs={{16,32},{17,33},{18,34},{19,35},{20,36},{21,37},{22,38},{23,39},{2... | collective-permute-start | bytes 1572872 | tf_op jit(solution)/shard_map/ppermute | solution.py:33
  225.9 47.5 %collective-permute-start.33 = (f32[512,256]{1,0:T(8,128)S(1)}, f32[512,256]{1,0:T(8,128)S(1)}, u32[]{:S(2)}, u32[]{:S(2)}) collective-permute-start(f32[512,256]{1,0:T(8,128)S(1)} %fusion.30), channel_id=1, source_target_pairs={{0,32},{1,33},{2,34},{3,35},{4,36},{5,37},{6,38},{7,39},{8,40},{9,... | collective-permute-start | bytes 1572872 | tf_op jit(solution)/shard_map/ppermute | solution.py:33
  232.5 43.5 %collective-permute-start.35 = (f32[512,256]{1,0:T(8,128)S(1)}, f32[512,256]{1,0:T(8,128)S(1)}, u32[]{:S(2)}, u32[]{:S(2)}) collective-permute-start(f32[512,256]{1,0:T(8,128)S(1)} %fusion.30), channel_id=1, source_target_pairs={{16,32},{17,33},{18,34},{19,35},{20,36},{21,37},{22,38},{23,39},{2... | collective-permute-start | bytes 1572872 | tf_op jit(solution)/shard_map/ppermute | solution.py:33

commit v5 on v4

--- a/solution.py
+++ b/solution.py
@@ -23,9 +23,10 @@
 
 
 SWAP = route(lambda o, x, z: (o ^ 1, x, z))
-DOWN = [route(lambda o, x, z: (o - 2 + c, x, z) if o % 2 == 0 else None) for c in (0, 1)]
+DOWN = route(lambda o, x, z: (o - 2, x, z))
 UP = [route(lambda o, x, z: (o + 2 - c, x, z) if o % 2 == c else None) for c in (0, 1)]
 AROUND = [route(lambda o, x, z: (o, x + r, z)) for r in range(X)]
+ACROSS = [route(lambda o, x, z: (o, x ^ d, z)) for d in range(X)]
 ALONG = [route(lambda o, x, z: (o, x, z ^ d)) for d in range(ZL)]
 
 
@@ -106,24 +107,26 @@
             jnp.concatenate([other, part], 0),
         )
 
+    def place(whole, piece, quarter):
+        return lax.dynamic_update_slice_in_dim(whole, piece, quarter * QUARTER, 0)
+
     def in_order(pieces):
         whole = jnp.zeros((X * QUARTER, pieces[0].shape[1]), jnp.float32)
         for r, piece in enumerate(pieces):
-            whole = lax.dynamic_update_slice_in_dim(
-                whole, piece, (px - r) % X * QUARTER, 0
-            )
+            whole = place(whole, piece, (px - r) % X)
         return whole
 
     one, two, three = base, base + 1, (base + 2) % ORB
 
     other = move(own, SWAP)
-    arrived = [move(own[c * ROWS : (c + 1) * ROWS], DOWN[c]) for c in (0, 1)]
     slab_one = jnp.where(first, own, other)
     slab_two = jnp.where(first, other, own)
+    near = move(rows_at(slab_one, core * ROWS, ROWS), DOWN)
     one_cols = cols_at(slab_one, at, COLS)
     two_cols = cols_at(slab_two, at, COLS)
 
-    inner_sends = send_x(pair_term(slab_one, slab_two, two_cols, one_cols))
+    inner = pair_term(slab_one, slab_two, two_cols, one_cols)
+    inner_sends = send_x(inner)
     inner_parts = around(inner_sends)
     energies = after((occupied_energy, virtual_energy, virtual_count), inner_sends)
     inner_weight = weight(one, two, at, *energies)
@@ -137,8 +140,7 @@
     inner_kept, inner_sent = halves(add_x(inner_parts))
     inner_next = move(inner_sent, ALONG[1])
 
-    arrived = after(arrived, inner_sent)
-    near = arrived[0] + arrived[1]
+    near = after(near, inner_sent)
     far = move(near, SWAP)
     near_cols = cols_at(near, at, COLS)
     outer_near = pair_term(near_two, near, near_cols, near_two_cols)
@@ -149,30 +151,44 @@
     left, right = slice(0, CHUNK), slice(CHUNK, COLS)
     sends = [send_x(outer[:, w]) for w in (left, right)]
     parts = [around(sends[n]) for n in (0, 1)]
-    inner_kept = inner_kept + after(inner_next, sends)
+    inner_kept = inner_kept + after(inner_next, sends[0])
     inner_far = move(inner_kept, ALONG[2])
 
-    kept_a, sent_a = halves(add_x(after(parts[0], inner_kept)))
-    kept_a = kept_a + move(sent_a, ALONG[1])
+    kept_a, sent_a = halves(add_x(after(parts[0], sends, inner_kept)))
+    next_a = move(sent_a, ALONG[1])
+    held_near, held_far = after((near_cols, far_cols), sent_a)
+    three_cols = jnp.where(
+        first,
+        jnp.concatenate([held_near, held_far], 0),
+        jnp.concatenate([held_far, held_near], 0),
+    )
+    inner_far, three_cols = after((inner_far, three_cols), sent_a)
+    inner_t = (inner_kept + inner_far) * inner_weight
+    inner_other = move(inner_t, ALONG[1])
+    kept_a = kept_a + after(next_a, inner_t)
     far_a = move(kept_a, ALONG[2])
-    kept_b, sent_b = halves(add_x(after(parts[1], kept_a)))
+    parts_b = after(parts[1], kept_a)
+    sum_b = add_x(parts_b)
+    kept_b, sent_b = halves(sum_b)
     next_b = move(sent_b, ALONG[1])
-
-    inner_t = (inner_kept + after(inner_far, sent_b)) * inner_weight
-    inner_other = move(inner_t, ALONG[1])
-    t_a = (kept_a + after(far_a, inner_t)) * outer_weight[:, left]
+    inner_quarter = join(inner_t, after(inner_other, sent_b))
+    inner_next = move(inner_quarter, ACROSS[1])
+
+    t_a = (kept_a + after(far_a, inner_quarter)) * outer_weight[:, left]
     other_a = move(t_a, ALONG[1])
     kept_b = kept_b + after(next_b, t_a)
     far_b = move(kept_b, ALONG[2])
-
     quarter_a = join(t_a, after(other_a, kept_b))
     pieces_a = around([quarter_a] * X)
-    inner_quarter = join(inner_t, after(inner_other, quarter_a))
-    inner_pieces = around([inner_quarter] * X)
-    t_b = (kept_b + after(far_b, inner_quarter)) * outer_weight[:, right]
+    t_b = (kept_b + after(far_b, quarter_a)) * outer_weight[:, right]
     other_b = move(t_b, ALONG[1])
-
-    all_a = in_order(after(pieces_a, t_b))
+    inner_pair = jnp.concatenate([inner_quarter, after(inner_next, t_b)], 0)
+    inner_rest = move(inner_pair, ACROSS[3])
+
+    inner_all = jnp.zeros((X * QUARTER, COLS), jnp.float32)
+    inner_all = place(inner_all, inner_pair[:QUARTER], px)
+    inner_all = place(inner_all, inner_pair[QUARTER:], px ^ 1)
+    all_a = in_order(after(pieces_a, t_b, inner_all))
     leaving_a = dot(slab_two, all_a, 1, 0)
     incoming_a = [move(leaving_a, UP[c]) for c in (0, 1)]
     quarter_b = join(t_b, after(other_b, leaving_a))
@@ -182,14 +198,11 @@
     incoming_b = [move(outgoing, UP[c]) for c in (0, 1)]
     incoming = [incoming_a[0], incoming_b[0], incoming_a[1], incoming_b[1]]
 
-    inner_all = in_order(after(inner_pieces, outgoing))
+    inner_rest = after(inner_rest, outgoing)
+    inner_all = place(inner_all, inner_rest[:QUARTER], px ^ 3)
+    inner_all = place(inner_all, inner_rest[QUARTER:], px ^ 2)
     to_one = dot(two_cols, inner_all, 1, 1)
     to_two = dot(slab_one, inner_all, 1, 0)
-    three_cols = jnp.where(
-        first,
-        jnp.concatenate([near_cols, far_cols], 0),
-        jnp.concatenate([far_cols, near_cols], 0),
-    )
     three_cols, all_a, all_b = after((three_cols, all_a, all_b), outgoing)
     beyond = dot(three_cols[:, left], all_a, 1, 1) + dot(three_cols[:, right], all_b, 1, 1)
     blank = jnp.zeros_like(to_two)
@@ -199,9 +212,8 @@
         jnp.concatenate([blank, to_two], 1),
     )
     crossed = move(jnp.where(first, to_two, to_one), SWAP)
-    density = jnp.where(first, to_one, to_two) + crossed
-    incoming = after(incoming, density)
-    density = density + jnp.concatenate(incoming, 1)
+    crossed, incoming = after((crossed, incoming))
+    density = jnp.where(first, to_one, to_two) + crossed + jnp.concatenate(incoming, 1)
     return density[None]
 
 

time: 279 us -> 289 us (1.036)
  the two profiles are of different devices: /device:TPU:24 before, /device:TPU:222 now
where the time goes in v5:
time: 289 us; the launch traced here: 288 us
  waiting for transfers between devices  115 us (40%)
  starting transfers between devices  114 us (39%)
  matrix products  24.4 us (8%)
  other arithmetic  16.9 us (6%)
  local copies, waits for them, and re-layouts  16.8 us (6%)
    ppermute x34, waiting for transfers between devices, move(): return lax.ppermute(block, AXES, pairs)  115 us
    ppermute x34, starting transfers between devices, move(): return lax.ppermute(block, AXES, pairs)  114 us
    dot_general x12, matrix products, dot(): lax.dot_general(a, b, (((da,), (db,)), ((), ())), precision=lax.Precision...  24.4 us
    dynamic_update_slice x10, local copies, waits for them, and re-layouts, place(): return lax.dynamic_update_slice_in_dim(whole, piece, quarter * QUARTER, 0)  6.69 us
  transfers between devices with their start and end apart: 34, of which 14 were waited for; matrix products, arithmetic and copies ran while one was open for 12% of the time, Pallas kernels for 0%

profile of v5, /device:TPU:222, one launch (start us, length us, event | category | flops | bytes accessed | tf_op | source)
XLA Modules:
  0.0 287.8 jit_solution(3957973384751227276)
XLA Ops:
  0.0 1.9 collective-permute-start
  2.1 4.3 %collective-permute-done = f32[512,1024]{1,0:T(8,128)} collective-permute-done((f32[512,1024]{1,0:T(8,128)}, f32[512,1024]{1,0:T(8,128)}, u32[]{:S(2)}, u32[]{:S(2)}) %collective-permute-start) | collective-permute-done | bytes 2097184 | tf_op jit(solution)/shard_map/ppermute | solution.py:34
  6.4 2.7 broadcast_select_fusion.2
  9.1 1.8 fusion.7
  11.0 1.9 multiply_subtract_fusion.1
  13.2 2.5 collective-permute-start.1
  15.8 4.3 %collective-permute-start.2 = (f32[256,512]{1,0:T(8,128)S(1)}, f32[256,512]{1,0:T(8,128)S(1)}, u32[]{:S(2)}, u32[]{:S(2)}) collective-permute-start(f32[256,512]{1,0:T(8,128)S(1)} %get-tuple-element.108), channel_id=1, source_target_pairs={{0,8},{1,9},{2,10},{3,11},{4,12},{5,13},{6,14},{7,15},{8,0},{9,1},... | collective-permute-start | bytes 1572872 | tf_op jit(solution)/shard_map/ppermute | solution.py:34
  20.1 1.9 collective-permute-start.3
  22.0 8.1 %collective-permute-start.5 = (f32[256,1024]{1,0:T(8,128)S(1)}, f32[256,1024]{1,0:T(8,128)}, u32[]{:S(2)}, u32[]{:S(2)}) collective-permute-start(f32[256,1024]{1,0:T(8,128)S(1)} %constant_dynamic-slice_fusion.12), channel_id=1, source_target_pairs={{0,480},{1,481},{2,482},{3,483},{4,484},{5,485},{6,486},{7,487},{8... | collective-permute-start | bytes 3145736 | tf_op jit(solution)/shard_map/ppermute | solution.py:34
  30.1 1.3 fusion.24
  34.0 1.2 fusion.21
  35.3 1.2 constant_dynamic-slice_fusion.14
  36.4 2.8 fusion.15
  39.2 4.9 %collective-permute-done.3 = f32[256,512]{1,0:T(8,128)S(1)} collective-permute-done((f32[256,512]{1,0:T(8,128)S(1)}, f32[256,512]{1,0:T(8,128)S(1)}, u32[]{:S(2)}, u32[]{:S(2)}) %collective-permute-start.3) | collective-permute-done | bytes 524320 | tf_op jit(solution)/shard_map/ppermute | solution.py:34
  45.9 25.4 %collective-permute-done.5 = f32[256,1024]{1,0:T(8,128)} collective-permute-done((f32[256,1024]{1,0:T(8,128)S(1)}, f32[256,1024]{1,0:T(8,128)}, u32[]{:S(2)}, u32[]{:S(2)}) %collective-permute-start.5) | collective-permute-done | bytes 1048608 | tf_op jit(solution)/shard_map/ppermute | solution.py:34
  71.2 1.9 collective-permute-start.6
  73.2 14.4 %collective-permute-start.4 = (f32[128,512]{1,0:T(8,128)}, f32[128,512]{1,0:T(8,128)S(1)}, u32[]{:S(2)}, u32[]{:S(2)}) collective-permute-start(f32[128,512]{1,0:T(8,128)} %constant_dynamic-slice_fusion.13), channel_id=1, source_target_pairs={{0,1},{1,0},{2,3},{3,2},{4,5},{5,4},{6,7},{7,6},{8,9},{9,8},{10,11... | collective-permute-start | bytes 786440 | tf_op jit(solution)/shard_map/ppermute | solution.py:34
  88.7 2.3 fusion.27
  91.1 2.4 multiply_subtract_fusion
  95.6 2.5 subtract_add_fusion
  98.4 2.8 collective-permute-start.10
  101.2 4.4 %collective-permute-start.8 = (f32[256,256]{1,0:T(8,128)S(1)}, f32[256,256]{1,0:T(8,128)S(1)}, u32[]{:S(2)}, u32[]{:S(2)}) collective-permute-start(f32[256,256]{1,0:T(8,128)S(1)} %get-tuple-element.117), channel_id=1, source_target_pairs={{0,4},{1,5},{2,6},{3,7},{4,8},{5,9},{6,10},{7,11},{8,12},{9,13},{1... | collective-permute-start | bytes 786440 | tf_op jit(solution)/shard_map/ppermute | solution.py:34
  105.6 3.7 %collective-permute-start.9 = (f32[256,256]{1,0:T(8,128)S(1)}, f32[256,256]{1,0:T(8,128)S(1)}, u32[]{:S(2)}, u32[]{:S(2)}) collective-permute-start(f32[256,256]{1,0:T(8,128)S(1)} %get-tuple-element.116), channel_id=1, source_target_pairs={{0,8},{1,9},{2,10},{3,11},{4,12},{5,13},{6,14},{7,15},{8,0},{9,1},... | collective-permute-start | bytes 786440 | tf_op jit(solution)/shard_map/ppermute | solution.py:34
  109.4 1.9 collective-permute-start.7
  111.4 2.8 collective-permute-start.12
  114.3 4.2 %collective-permute-start.13 = (f32[256,256]{1,0:T(8,128)S(1)}, f32[256,256]{1,0:T(8,128)S(1)}, u32[]{:S(2)}, u32[]{:S(2)}) collective-permute-start(f32[256,256]{1,0:T(8,128)S(1)} %get-tuple-element.112), channel_id=1, source_target_pairs={{0,8},{1,9},{2,10},{3,11},{4,12},{5,13},{6,14},{7,15},{8,0},{9,1},... | collective-permute-start | bytes 786440 | tf_op jit(solution)/shard_map/ppermute | solution.py:34
  118.4 2.2 collective-permute-start.14
  120.8 1.9 collective-permute-start.15
  123.8 1.4 collective-permute-done.7
  125.2 2.5 collective-permute-start.11
  127.9 5.6 %collective-permute-start.18 = (f32[128,256]{1,0:T(8,128)S(1)}, f32[128,256]{1,0:T(8,128)S(1)}, u32[]{:S(2)}, u32[]{:S(2)}) collective-permute-start(f32[128,256]{1,0:T(8,128)S(1)} %dynamic-slice_add_fusion.2), channel_id=1, source_target_pairs={{0,2},{1,3},{2,0},{3,1},{4,6},{5,7},{6,4},{7,5},{8,10},{9,11},{10,... | collective-permute-start | bytes 393224 | tf_op jit(solution)/shard_map/ppermute | solution.py:34
  133.7 1.9 collective-permute-start.17
  135.6 3.5 %collective-permute-done.11 = f32[128,512]{1,0:T(8,128)S(1)} collective-permute-done((f32[128,512]{1,0:T(8,128)S(1)}, f32[128,512]{1,0:T(8,128)S(1)}, u32[]{:S(2)}, u32[]{:S(2)}) %collective-permute-start.11) | collective-permute-done | bytes 262176 | tf_op jit(solution)/shard_map/ppermute | solution.py:34
  139.1 1.6 broadcast_in_dim.4
  141.6 2.7 collective-permute-start.16
  144.4 1.9 collective-permute-start.20
  147.0 3.8 %collective-permute-start.19 = (f32[128,256]{1,0:T(8,128)}, f32[128,256]{1,0:T(8,128)}, u32[]{:S(2)}, u32[]{:S(2)}) collective-permute-start(f32[128,256]{1,0:T(8,128)} %dynamic-slice_add_fusion.1), channel_id=1, source_target_pairs={{0,2},{1,3},{2,0},{3,1},{4,6},{5,7},{6,4},{7,5},{8,10},{9,11},{10,... | collective-permute-start | bytes 393224 | tf_op jit(solution)/shard_map/ppermute | solution.py:34
  150.8 1.6 collective-permute-done.20
  153.4 2.7 collective-permute-start.23
  156.2 4.2 %collective-permute-start.24 = (f32[256,256]{1,0:T(8,128)S(1)}, f32[256,256]{1,0:T(8,128)S(1)}, u32[]{:S(2)}, u32[]{:S(2)}) collective-permute-start(f32[256,256]{1,0:T(8,128)S(1)} %maximum_select_fusion.2), channel_id=1, source_target_pairs={{0,8},{1,9},{2,10},{3,11},{4,12},{5,13},{6,14},{7,15},{8,0},{9,1},... | collective-permute-start | bytes 786440 | tf_op jit(solution)/shard_map/ppermute | solution.py:34
  160.4 2.4 collective-permute-start.25
  163.8 1.9 collective-permute-start.22
  166.6 3.3 %collective-permute-done.25 = f32[256,256]{1,0:T(8,128)S(1)} collective-permute-done((f32[256,256]{1,0:T(8,128)S(1)}, f32[256,256]{1,0:T(8,128)S(1)}, u32[]{:S(2)}, u32[]{:S(2)}) %collective-permute-start.25) | collective-permute-done | bytes 262176 | tf_op jit(solution)/shard_map/ppermute | solution.py:34
  170.1 1.8 fusion.29
  172.8 3.4 %collective-permute-start.26 = (f32[256,256]{1,0:T(8,128)}, f32[256,256]{1,0:T(8,128)}, u32[]{:S(2)}, u32[]{:S(2)}) collective-permute-start(f32[256,256]{1,0:T(8,128)} %get-tuple-element.96), channel_id=1, source_target_pairs={{0,4},{1,5},{2,6},{3,7},{4,8},{5,9},{6,10},{7,11},{8,12},{9,13},{1... | collective-permute-start | bytes 786440 | tf_op jit(solution)/shard_map/ppermute | solution.py:34
  176.2 2.2 collective-permute-start.27
  179.4 4.8 %collective-permute-start.21 = (f32[512,512]{1,0:T(8,128)}, f32[512,512]{1,0:T(8,128)}, u32[]{:S(2)}, u32[]{:S(2)}) collective-permute-start(f32[512,512]{1,0:T(8,128)} %pad_maximum_fusion), channel_id=1, source_target_pairs={{0,12},{1,13},{2,14},{3,15},{4,8},{5,9},{6,10},{7,11},{8,4},{9,5},... | collective-permute-start | bytes 3145736 | tf_op jit(solution)/shard_map/ppermute | solution.py:34
  184.3 2.2 collective-permute-start.28
  188.1 23.9 %collective-permute-done.28 = f32[256,256]{1,0:T(8,128)} collective-permute-done((f32[256,256]{1,0:T(8,128)}, f32[256,256]{1,0:T(8,128)}, u32[]{:S(2)}, u32[]{:S(2)}) %collective-permute-start.28) | collective-permute-done | bytes 262176 | tf_op jit(solution)/shard_map/ppermute | solution.py:34
  215.1 1.9 slice_dynamic-update-slice_fusion.1
  217.0 1.9 slice_dynamic-update-slice_fusion
  218.9 3.5 %fusion.31 = f32[512,512]{1,0:T(8,128)S(1)} fusion(f32[512,1024]{1,0:T(8,128)S(1)} %copy-done.1, f32[1024,512]{1,0:T(8,128)} %slice_dynamic-update-slice_fusion), kind=kOutput, calls=%fused_computation.89 | convolution fusion | flops 1610612736 | bytes 5242880 | tf_op jit(solution)/shard_map/dot_general | solution.py:38
  222.3 3.5 %fusion.5 = f32[512,1024]{1,0:T(8,128)S(1)} fusion(f32[1024,512]{1,0:T(8,128)} %slice_dynamic-update-slice_fusion, f32[512,1024]{1,0:T(8,128)S(1)} %get-tuple-element.99, s32[]{:T(128)S(6)} %select_n.231), kind=kOutput, calls=%fused_computation.13 | convolution fusion | flops 1610612736 | bytes 5242884 | tf_op jit(solution)/shard_map/dot_general | solution.py:38
  225.9 1.5 broadcast_select_fusion
  227.4 1.9 collective-permute-start.29
  229.3 1.9 collective-permute-start.30
  231.3 1.3 collective-permute-start.32
  232.6 6.0 %collective-permute-start.31 = (f32[512,256]{1,0:T(8,128)S(1)}, f32[512,256]{1,0:T(8,128)S(1)}, u32[]{:S(2)}, u32[]{:S(2)}) collective-permute-start(f32[512,256]{1,0:T(8,128)S(1)} %fusion.30), channel_id=1, source_target_pairs={{0,32},{1,33},{2,34},{3,35},{4,36},{5,37},{6,38},{7,39},{8,40},{9,... | collective-permute-start | bytes 1572872 | tf_op jit(solution)/shard_map/ppermute | solution.py:34
  238.6 1.3 collective-permute-start.33
  239.8 19.4 %collective-permute-done.30 = f32[512,256]{1,0:T(8,128)S(1)} collective-permute-done((f32[512,256]{1,0:T(8,128)S(1)}, f32[512,256]{1,0:T(8,128)S(1)}, u32[]{:S(2)}, u32[]{:S(2)}) %collective-permute-start.30) | collective-permute-done | bytes 524320 | tf_op jit(solution)/shard_map/ppermute | solution.py:34
  259.2 5.7 %collective-permute-done.32 = f32[512,256]{1,0:T(8,128)S(1)} collective-permute-done((f32[512,256]{1,0:T(8,128)S(1)}, f32[512,256]{1,0:T(8,128)S(1)}, u32[]{:S(2)}, u32[]{:S(2)}) %collective-permute-start.32) | collective-permute-done | bytes 524320 | tf_op jit(solution)/shard_map/ppermute | solution.py:34
  264.9 18.1 %collective-permute-done.31 = f32[512,256]{1,0:T(8,128)S(1)} collective-permute-done((f32[512,256]{1,0:T(8,128)S(1)}, f32[512,256]{1,0:T(8,128)S(1)}, u32[]{:S(2)}, u32[]{:S(2)}) %collective-permute-start.31) | collective-permute-done | bytes 524320 | tf_op jit(solution)/shard_map/ppermute | solution.py:34
  283.0 2.7 collective-permute-done.33
  285.6 2.2 fusion
  (100 shorter events, 20.9 us)
Async XLA Ops:
  0.0 6.4 %collective-permute-start = (f32[512,1024]{1,0:T(8,128)}, f32[512,1024]{1,0:T(8,128)}, u32[]{:S(2)}, u32[]{:S(2)}) collective-permute-start(f32[512,1024]{1,0:T(8,128)} %bitcast.30), channel_id=1, source_target_pairs={{0,16},{1,17},{2,18},{3,19},{4,20},{5,21},{6,22},{7,23},{8,24},{9,... | collective-permute-start | bytes 6291464 | tf_op jit(solution)/shard_map/ppermute | solution.py:34
  9.1 2.0 copy-start
  13.2 18.3 %copy-start.15 = (s32[32]{0:T(128)S(1)}, s32[32]{0:T(128)}, u32[]{:S(2)}) copy-start(s32[32]{0:T(128)} %param.7) | copy-start | bytes 388
  13.2 20.0 %copy-start.17 = (f32[1024]{0:T(1024)S(1)}, f32[1024]{0:T(1024)}, u32[]{:S(2)}) copy-start(f32[1024]{0:T(1024)} %param.6) | copy-start | bytes 12292
  13.2 20.1 %copy-start.16 = (f32[32]{0:T(128)S(1)}, f32[32]{0:T(128)}, u32[]{:S(2)}) copy-start(f32[32]{0:T(128)} %param.5) | copy-start | bytes 388
  13.2 26.0 %collective-permute-start.1 = (f32[256,512]{1,0:T(8,128)S(1)}, f32[256,512]{1,0:T(8,128)S(1)}, u32[]{:S(2)}, u32[]{:S(2)}) collective-permute-start(f32[256,512]{1,0:T(8,128)S(1)} %get-tuple-element.109), channel_id=1, source_target_pairs={{0,4},{1,5},{2,6},{3,7},{4,8},{5,9},{6,10},{7,11},{8,12},{9,13},{1... | collective-permute-start | bytes 1572872 | tf_op jit(solution)/shard_map/ppermute | solution.py:34
  15.8 23.4 %collective-permute-start.2 = (f32[256,512]{1,0:T(8,128)S(1)}, f32[256,512]{1,0:T(8,128)S(1)}, u32[]{:S(2)}, u32[]{:S(2)}) collective-permute-start(f32[256,512]{1,0:T(8,128)S(1)} %get-tuple-element.108), channel_id=1, source_target_pairs={{0,8},{1,9},{2,10},{3,11},{4,12},{5,13},{6,14},{7,15},{8,0},{9,1},... | collective-permute-start | bytes 1572872 | tf_op jit(solution)/shard_map/ppermute | solution.py:34
  20.1 24.0 %collective-permute-start.3 = (f32[256,512]{1,0:T(8,128)S(1)}, f32[256,512]{1,0:T(8,128)S(1)}, u32[]{:S(2)}, u32[]{:S(2)}) collective-permute-start(f32[256,512]{1,0:T(8,128)S(1)} %get-tuple-element.107), channel_id=1, source_target_pairs={{0,12},{1,13},{2,14},{3,15},{4,0},{5,1},{6,2},{7,3},{8,4},{9,5},{1... | collective-permute-start | bytes 1572872 | tf_op jit(solution)/shard_map/ppermute | solution.py:34
  22.0 49.2 %collective-permute-start.5 = (f32[256,1024]{1,0:T(8,128)S(1)}, f32[256,1024]{1,0:T(8,128)}, u32[]{:S(2)}, u32[]{:S(2)}) collective-permute-start(f32[256,1024]{1,0:T(8,128)S(1)} %constant_dynamic-slice_fusion.12), channel_id=1, source_target_pairs={{0,480},{1,481},{2,482},{3,483},{4,484},{5,485},{6,486},{7,487},{8... | collective-permute-start | bytes 3145736 | tf_op jit(solution)/shard_map/ppermute | solution.py:34
  44.3 0.8 copy-start.5
  71.2 22.2 %collective-permute-start.6 = (f32[256,1024]{1,0:T(8,128)}, f32[256,1024]{1,0:T(8,128)}, u32[]{:S(2)}, u32[]{:S(2)}) collective-permute-start(f32[256,1024]{1,0:T(8,128)} %collective-permute-done.5), channel_id=1, source_target_pairs={{0,16},{1,17},{2,18},{3,19},{4,20},{5,21},{6,22},{7,23},{8,24},{9,... | collective-permute-start | bytes 3145736 | tf_op jit(solution)/shard_map/ppermute | solution.py:34
  73.2 36.1 %collective-permute-start.4 = (f32[128,512]{1,0:T(8,128)}, f32[128,512]{1,0:T(8,128)S(1)}, u32[]{:S(2)}, u32[]{:S(2)}) collective-permute-start(f32[128,512]{1,0:T(8,128)} %constant_dynamic-slice_fusion.13), channel_id=1, source_target_pairs={{0,1},{1,0},{2,3},{3,2},{4,5},{5,4},{6,7},{7,6},{8,9},{9,8},{10,11... | collective-permute-start | bytes 786440 | tf_op jit(solution)/shard_map/ppermute | solution.py:34
  88.7 2.3 copy-start.11
  94.5 1.0 copy-start.12
  98.3 11.0 %copy-start.6 = (f32[256,512]{1,0:T(8,128)S(1)}, f32[256,512]{1,0:T(8,128)}, u32[]{:S(2)}) copy-start(f32[256,512]{1,0:T(8,128)} %copy-done.5) | copy-start | bytes 1572868
  98.4 15.9 %collective-permute-start.10 = (f32[256,256]{1,0:T(8,128)S(1)}, f32[256,256]{1,0:T(8,128)S(1)}, u32[]{:S(2)}, u32[]{:S(2)}) collective-permute-start(f32[256,256]{1,0:T(8,128)S(1)} %get-tuple-element.115), channel_id=1, source_target_pairs={{0,12},{1,13},{2,14},{3,15},{4,0},{5,1},{6,2},{7,3},{8,4},{9,5},{1... | collective-permute-start | bytes 786440 | tf_op jit(solution)/shard_map/ppermute | solution.py:34
  101.2 17.2 %collective-permute-start.8 = (f32[256,256]{1,0:T(8,128)S(1)}, f32[256,256]{1,0:T(8,128)S(1)}, u32[]{:S(2)}, u32[]{:S(2)}) collective-permute-start(f32[256,256]{1,0:T(8,128)S(1)} %get-tuple-element.117), channel_id=1, source_target_pairs={{0,4},{1,5},{2,6},{3,7},{4,8},{5,9},{6,10},{7,11},{8,12},{9,13},{1... | collective-permute-start | bytes 786440 | tf_op jit(solution)/shard_map/ppermute | solution.py:34
  105.6 15.1 %collective-permute-start.9 = (f32[256,256]{1,0:T(8,128)S(1)}, f32[256,256]{1,0:T(8,128)S(1)}, u32[]{:S(2)}, u32[]{:S(2)}) collective-permute-start(f32[256,256]{1,0:T(8,128)S(1)} %get-tuple-element.116), channel_id=1, source_target_pairs={{0,8},{1,9},{2,10},{3,11},{4,12},{5,13},{6,14},{7,15},{8,0},{9,1},... | collective-permute-start | bytes 786440 | tf_op jit(solution)/shard_map/ppermute | solution.py:34
  109.4 15.8 %collective-permute-start.7 = (f32[128,512]{1,0:T(8,128)S(1)}, f32[128,512]{1,0:T(8,128)S(1)}, u32[]{:S(2)}, u32[]{:S(2)}) collective-permute-start(f32[128,512]{1,0:T(8,128)S(1)} %dynamic-slice_add_fusion), channel_id=1, source_target_pairs={{0,2},{1,3},{2,0},{3,1},{4,6},{5,7},{6,4},{7,5},{8,10},{9,11},{10,... | collective-permute-start | bytes 786440 | tf_op jit(solution)/shard_map/ppermute | solution.py:34
  111.4 13.8 %copy-start.13 = (f32[128,512]{1,0:T(8,128)S(1)}, f32[128,512]{1,0:T(8,128)}, u32[]{:S(2)}) copy-start(f32[128,512]{1,0:T(8,128)} %get-tuple-element.67) | copy-start | bytes 786436
  111.4 22.1 %collective-permute-start.12 = (f32[256,256]{1,0:T(8,128)S(1)}, f32[256,256]{1,0:T(8,128)S(1)}, u32[]{:S(2)}, u32[]{:S(2)}) collective-permute-start(f32[256,256]{1,0:T(8,128)S(1)} %get-tuple-element.113), channel_id=1, source_target_pairs={{0,4},{1,5},{2,6},{3,7},{4,8},{5,9},{6,10},{7,11},{8,12},{9,13},{1... | collective-permute-start | bytes 786440 | tf_op jit(solution)/shard_map/ppermute | solution.py:34
  114.3 19.3 %collective-permute-start.13 = (f32[256,256]{1,0:T(8,128)S(1)}, f32[256,256]{1,0:T(8,128)S(1)}, u32[]{:S(2)}, u32[]{:S(2)}) collective-permute-start(f32[256,256]{1,0:T(8,128)S(1)} %get-tuple-element.112), channel_id=1, source_target_pairs={{0,8},{1,9},{2,10},{3,11},{4,12},{5,13},{6,14},{7,15},{8,0},{9,1},... | collective-permute-start | bytes 786440 | tf_op jit(solution)/shard_map/ppermute | solution.py:34
  118.4 15.1 %collective-permute-start.14 = (f32[256,256]{1,0:T(8,128)S(1)}, f32[256,256]{1,0:T(8,128)S(1)}, u32[]{:S(2)}, u32[]{:S(2)}) collective-permute-start(f32[256,256]{1,0:T(8,128)S(1)} %get-tuple-element.111), channel_id=1, source_target_pairs={{0,12},{1,13},{2,14},{3,15},{4,0},{5,1},{6,2},{7,3},{8,4},{9,5},{1... | collective-permute-start | bytes 786440 | tf_op jit(solution)/shard_map/ppermute | solution.py:34
  120.8 7.1 %collective-permute-start.15 = (f32[128,256]{1,0:T(8,128)S(1)}, f32[128,256]{1,0:T(8,128)S(1)}, u32[]{:S(2)}, u32[]{:S(2)}) collective-permute-start(f32[128,256]{1,0:T(8,128)S(1)} %constant_dynamic-slice_fusion.1), channel_id=1, source_target_pairs={{0,1},{1,0},{2,3},{3,2},{4,5},{5,4},{6,7},{7,6},{8,9},{9,8},{10,11... | collective-permute-start | bytes 393224 | tf_op jit(solution)/shard_map/ppermute | solution.py:34
  125.2 13.9 %collective-permute-start.11 = (f32[128,512]{1,0:T(8,128)S(1)}, f32[128,512]{1,0:T(8,128)S(1)}, u32[]{:S(2)}, u32[]{:S(2)}) collective-permute-start(f32[128,512]{1,0:T(8,128)S(1)} %add_multiply_fusion), channel_id=1, source_target_pairs={{0,1},{1,0},{2,3},{3,2},{4,5},{5,4},{6,7},{7,6},{8,9},{9,8},{10,11... | collective-permute-start | bytes 786440 | tf_op jit(solution)/shard_map/ppermute | solution.py:34
  127.9 16.4 %collective-permute-start.18 = (f32[128,256]{1,0:T(8,128)S(1)}, f32[128,256]{1,0:T(8,128)S(1)}, u32[]{:S(2)}, u32[]{:S(2)}) collective-permute-start(f32[128,256]{1,0:T(8,128)S(1)} %dynamic-slice_add_fusion.2), channel_id=1, source_target_pairs={{0,2},{1,3},{2,0},{3,1},{4,6},{5,7},{6,4},{7,5},{8,10},{9,11},{10,... | collective-permute-start | bytes 393224 | tf_op jit(solution)/shard_map/ppermute | solution.py:34
  133.7 12.7 %collective-permute-start.17 = (f32[128,256]{1,0:T(8,128)S(1)}, f32[128,256]{1,0:T(8,128)S(1)}, u32[]{:S(2)}, u32[]{:S(2)}) collective-permute-start(f32[128,256]{1,0:T(8,128)S(1)} %constant_dynamic-slice_fusion), channel_id=1, source_target_pairs={{0,1},{1,0},{2,3},{3,2},{4,5},{5,4},{6,7},{7,6},{8,9},{9,8},{10,11... | collective-permute-start | bytes 393224 | tf_op jit(solution)/shard_map/ppermute | solution.py:34
  141.6 28.3 %copy-start.7 = (f32[256,512]{1,0:T(8,128)}, f32[256,512]{1,0:T(8,128)S(1)}, u32[]{:S(2)}) copy-start(f32[256,512]{1,0:T(8,128)S(1)} %get-tuple-element.98) | copy-start | bytes 1572868
  141.6 24.1 %collective-permute-start.16 = (f32[256,512]{1,0:T(8,128)S(1)}, f32[256,512]{1,0:T(8,128)S(1)}, u32[]{:S(2)}, u32[]{:S(2)}) collective-permute-start(f32[256,512]{1,0:T(8,128)S(1)} %get-tuple-element.98), channel_id=1, source_target_pairs={{0,4},{1,5},{2,6},{3,7},{4,0},{5,1},{6,2},{7,3},{8,12},{9,13},{10,... | collective-permute-start | bytes 1572872 | tf_op jit(solution)/shard_map/ppermute | solution.py:34
  144.4 8.0 %collective-permute-start.20 = (f32[128,256]{1,0:T(8,128)S(1)}, f32[128,256]{1,0:T(8,128)}, u32[]{:S(2)}, u32[]{:S(2)}) collective-permute-start(f32[128,256]{1,0:T(8,128)S(1)} %slice_multiply_fusion.1), channel_id=1, source_target_pairs={{0,1},{1,0},{2,3},{3,2},{4,5},{5,4},{6,7},{7,6},{8,9},{9,8},{10,11... | collective-permute-start | bytes 393224 | tf_op jit(solution)/shard_map/ppermute | solution.py:34
  147.0 15.8 %collective-permute-start.19 = (f32[128,256]{1,0:T(8,128)}, f32[128,256]{1,0:T(8,128)}, u32[]{:S(2)}, u32[]{:S(2)}) collective-permute-start(f32[128,256]{1,0:T(8,128)} %dynamic-slice_add_fusion.1), channel_id=1, source_target_pairs={{0,2},{1,3},{2,0},{3,1},{4,6},{5,7},{6,4},{7,5},{8,10},{9,11},{10,... | collective-permute-start | bytes 393224 | tf_op jit(solution)/shard_map/ppermute | solution.py:34
  153.4 13.2 %collective-permute-start.23 = (f32[256,256]{1,0:T(8,128)S(1)}, f32[256,256]{1,0:T(8,128)S(1)}, u32[]{:S(2)}, u32[]{:S(2)}) collective-permute-start(f32[256,256]{1,0:T(8,128)S(1)} %maximum_select_fusion.2), channel_id=1, source_target_pairs={{0,4},{1,5},{2,6},{3,7},{4,8},{5,9},{6,10},{7,11},{8,12},{9,13},{1... | collective-permute-start | bytes 786440 | tf_op jit(solution)/shard_map/ppermute | solution.py:34
  156.2 10.4 %collective-permute-start.24 = (f32[256,256]{1,0:T(8,128)S(1)}, f32[256,256]{1,0:T(8,128)S(1)}, u32[]{:S(2)}, u32[]{:S(2)}) collective-permute-start(f32[256,256]{1,0:T(8,128)S(1)} %maximum_select_fusion.2), channel_id=1, source_target_pairs={{0,8},{1,9},{2,10},{3,11},{4,12},{5,13},{6,14},{7,15},{8,0},{9,1},... | collective-permute-start | bytes 786440 | tf_op jit(solution)/shard_map/ppermute | solution.py:34
  160.4 9.5 %collective-permute-start.25 = (f32[256,256]{1,0:T(8,128)S(1)}, f32[256,256]{1,0:T(8,128)S(1)}, u32[]{:S(2)}, u32[]{:S(2)}) collective-permute-start(f32[256,256]{1,0:T(8,128)S(1)} %maximum_select_fusion.2), channel_id=1, source_target_pairs={{0,12},{1,13},{2,14},{3,15},{4,0},{5,1},{6,2},{7,3},{8,4},{9,5},{1... | collective-permute-start | bytes 786440 | tf_op jit(solution)/shard_map/ppermute | solution.py:34
  163.8 8.2 %collective-permute-start.22 = (f32[128,256]{1,0:T(8,128)S(1)}, f32[128,256]{1,0:T(8,128)S(1)}, u32[]{:S(2)}, u32[]{:S(2)}) collective-permute-start(f32[128,256]{1,0:T(8,128)S(1)} %slice_multiply_fusion), channel_id=1, source_target_pairs={{0,1},{1,0},{2,3},{3,2},{4,5},{5,4},{6,7},{7,6},{8,9},{9,8},{10,11... | collective-permute-start | bytes 393224 | tf_op jit(solution)/shard_map/ppermute | solution.py:34
  165.7 4.4 %copy-start.9 = (f32[256,512]{1,0:T(8,128)}, f32[256,512]{1,0:T(8,128)S(1)}, u32[]{:S(2)}) copy-start(f32[256,512]{1,0:T(8,128)S(1)} %collective-permute-done.16) | copy-start | bytes 1572868
  170.1 1.9 copy-start.2
  170.1 8.3 %copy-start.8 = (f32[256,512]{1,0:T(8,128)S(1)}, f32[256,512]{1,0:T(8,128)}, u32[]{:S(2)}) copy-start(f32[256,512]{1,0:T(8,128)} %copy-done.7) | copy-start | bytes 1572868
  171.9 6.4 %copy-start.10 = (f32[256,512]{1,0:T(8,128)S(1)}, f32[256,512]{1,0:T(8,128)}, u32[]{:S(2)}) copy-start(f32[256,512]{1,0:T(8,128)} %copy-done.9) | copy-start | bytes 1572868
  172.8 13.7 %collective-permute-start.26 = (f32[256,256]{1,0:T(8,128)}, f32[256,256]{1,0:T(8,128)}, u32[]{:S(2)}, u32[]{:S(2)}) collective-permute-start(f32[256,256]{1,0:T(8,128)} %get-tuple-element.96), channel_id=1, source_target_pairs={{0,4},{1,5},{2,6},{3,7},{4,8},{5,9},{6,10},{7,11},{8,12},{9,13},{1... | collective-permute-start | bytes 786440 | tf_op jit(solution)/shard_map/ppermute | solution.py:34
  176.2 11.9 %collective-permute-start.27 = (f32[256,256]{1,0:T(8,128)}, f32[256,256]{1,0:T(8,128)S(1)}, u32[]{:S(2)}, u32[]{:S(2)}) collective-permute-start(f32[256,256]{1,0:T(8,128)} %get-tuple-element.96), channel_id=1, source_target_pairs={{0,8},{1,9},{2,10},{3,11},{4,12},{5,13},{6,14},{7,15},{8,0},{9,1},... | collective-permute-start | bytes 786440 | tf_op jit(solution)/shard_map/ppermute | solution.py:34
  179.4 35.7 %collective-permute-start.21 = (f32[512,512]{1,0:T(8,128)}, f32[512,512]{1,0:T(8,128)}, u32[]{:S(2)}, u32[]{:S(2)}) collective-permute-start(f32[512,512]{1,0:T(8,128)} %pad_maximum_fusion), channel_id=1, source_target_pairs={{0,12},{1,13},{2,14},{3,15},{4,8},{5,9},{6,10},{7,11},{8,4},{9,5},... | collective-permute-start | bytes 3145736 | tf_op jit(solution)/shard_map/ppermute | solution.py:34
  184.3 27.8 %collective-permute-start.28 = (f32[256,256]{1,0:T(8,128)}, f32[256,256]{1,0:T(8,128)}, u32[]{:S(2)}, u32[]{:S(2)}) collective-permute-start(f32[256,256]{1,0:T(8,128)} %get-tuple-element.96), channel_id=1, source_target_pairs={{0,12},{1,13},{2,14},{3,15},{4,0},{5,1},{6,2},{7,3},{8,4},{9,5},{1... | collective-permute-start | bytes 786440 | tf_op jit(solution)/shard_map/ppermute | solution.py:34
  188.1 25.9 %copy-start.4 = (f32[512,512]{1,0:T(8,128)S(1)}, f32[512,512]{1,0:T(8,128)}, u32[]{:S(2)}) copy-start(f32[512,512]{1,0:T(8,128)} %maximum_select_fusion) | copy-start | bytes 3145732
  214.1 4.8 %copy-start.1 = (f32[512,1024]{1,0:T(8,128)S(1)}, f32[512,1024]{1,0:T(8,128)}, u32[]{:S(2)}) copy-start(f32[512,1024]{1,0:T(8,128)} %copy-done) | copy-start | bytes 6291460
  222.3 3.6 %copy-start.3 = (f32[1024,256]{1,0:T(8,128)S(1)}, f32[1024,256]{1,0:T(8,128)}, u32[]{:S(2)}) copy-start(f32[1024,256]{1,0:T(8,128)} %copy-done.2) | copy-start | bytes 3145732
  225.9 3.4 %copy-start.14 = (f32[512,256]{1,0:T(8,128)S(1)}, f32[512,256]{1,0:T(8,128)}, u32[]{:S(2)}) copy-start(f32[512,256]{1,0:T(8,128)} %fusion.29) | copy-start | bytes 1572868
  227.4 58.2 %collective-permute-start.29 = (f32[512,1024]{1,0:T(8,128)S(1)}, f32[512,1024]{1,0:T(8,128)S(1)}, u32[]{:S(2)}, u32[]{:S(2)}) collective-permute-start(f32[512,1024]{1,0:T(8,128)S(1)} %get-tuple-element.127), channel_id=1, source_target_pairs={{0,16},{1,17},{2,18},{3,19},{4,20},{5,21},{6,22},{7,23},{8,24},{9,... | collective-permute-start | bytes 6291464 | tf_op jit(solution)/shard_map/ppermute | solution.py:34
  229.3 29.9 %collective-permute-start.30 = (f32[512,256]{1,0:T(8,128)S(1)}, f32[512,256]{1,0:T(8,128)S(1)}, u32[]{:S(2)}, u32[]{:S(2)}) collective-permute-start(f32[512,256]{1,0:T(8,128)S(1)} %copy-done.14), channel_id=1, source_target_pairs={{0,32},{1,33},{2,34},{3,35},{4,36},{5,37},{6,38},{7,39},{8,40},{9,... | collective-permute-start | bytes 1572872 | tf_op jit(solution)/shard_map/ppermute | solution.py:34
  231.3 33.6 %collective-permute-start.32 = (f32[512,256]{1,0:T(8,128)S(1)}, f32[512,256]{1,0:T(8,128)S(1)}, u32[]{:S(2)}, u32[]{:S(2)}) collective-permute-start(f32[512,256]{1,0:T(8,128)S(1)} %copy-done.14), channel_id=1, source_target_pairs={{16,32},{17,33},{18,34},{19,35},{20,36},{21,37},{22,38},{23,39},{2... | collective-permute-start | bytes 1572872 | tf_op jit(solution)/shard_map/ppermute | solution.py:34
  232.6 50.4 %collective-permute-start.31 = (f32[512,256]{1,0:T(8,128)S(1)}, f32[512,256]{1,0:T(8,128)S(1)}, u32[]{:S(2)}, u32[]{:S(2)}) collective-permute-start(f32[512,256]{1,0:T(8,128)S(1)} %fusion.30), channel_id=1, source_target_pairs={{0,32},{1,33},{2,34},{3,35},{4,36},{5,37},{6,38},{7,39},{8,40},{9,... | collective-permute-start | bytes 1572872 | tf_op jit(solution)/shard_map/ppermute | solution.py:34
  238.6 47.1 %collective-permute-start.33 = (f32[512,256]{1,0:T(8,128)S(1)}, f32[512,256]{1,0:T(8,128)S(1)}, u32[]{:S(2)}, u32[]{:S(2)}) collective-permute-start(f32[512,256]{1,0:T(8,128)S(1)} %fusion.30), channel_id=1, source_target_pairs={{16,32},{17,33},{18,34},{19,35},{20,36},{21,37},{22,38},{23,39},{2... | collective-permute-start | bytes 1572872 | tf_op jit(solution)/shard_map/ppermute | solution.py:34

commit v6 on v4

--- a/solution.py
+++ b/solution.py
@@ -23,9 +23,10 @@
 
 
 SWAP = route(lambda o, x, z: (o ^ 1, x, z))
-DOWN = [route(lambda o, x, z: (o - 2 + c, x, z) if o % 2 == 0 else None) for c in (0, 1)]
+DOWN = route(lambda o, x, z: (o - 2, x, z))
 UP = [route(lambda o, x, z: (o + 2 - c, x, z) if o % 2 == c else None) for c in (0, 1)]
 AROUND = [route(lambda o, x, z: (o, x + r, z)) for r in range(X)]
+ACROSS = [route(lambda o, x, z: (o, x ^ d, z)) for d in range(X)]
 ALONG = [route(lambda o, x, z: (o, x, z ^ d)) for d in range(ZL)]
 
 
@@ -83,11 +84,10 @@
             total, (1 - bit) * HALF_Q, HALF_Q
         )
 
-    def weight(left, right, col, occupied_energy, virtual_energy, virtual_count):
-        row = px * QUARTER + bit * HALF_Q
-        rows = row + jnp.arange(HALF_Q, dtype=jnp.int32)
+    def weight(left, right, row, height, col, occupied_energy, virtual_energy, virtual_count):
+        rows = row + jnp.arange(height, dtype=jnp.int32)
         cols = col + jnp.arange(COLS, dtype=jnp.int32)
-        energy_rows = lax.dynamic_slice_in_dim(virtual_energy, row, HALF_Q)
+        energy_rows = lax.dynamic_slice_in_dim(virtual_energy, row, height)
         energy_cols = lax.dynamic_slice_in_dim(virtual_energy, col, COLS)
         keep_rows = (rows < virtual_count[left]).astype(jnp.float32)
         keep_cols = (cols < virtual_count[right]).astype(jnp.float32)
@@ -117,17 +117,19 @@
     one, two, three = base, base + 1, (base + 2) % ORB
 
     other = move(own, SWAP)
-    arrived = [move(own[c * ROWS : (c + 1) * ROWS], DOWN[c]) for c in (0, 1)]
     slab_one = jnp.where(first, own, other)
     slab_two = jnp.where(first, other, own)
+    near = move(rows_at(slab_one, core * ROWS, ROWS), DOWN)
     one_cols = cols_at(slab_one, at, COLS)
     two_cols = cols_at(slab_two, at, COLS)
 
-    inner_sends = send_x(pair_term(slab_one, slab_two, two_cols, one_cols))
+    inner = pair_term(slab_one, slab_two, two_cols, one_cols)
+    inner_sends = send_x(inner)
     inner_parts = around(inner_sends)
     energies = after((occupied_energy, virtual_energy, virtual_count), inner_sends)
-    inner_weight = weight(one, two, at, *energies)
-    outer_weight = weight(two, three, at, *energies)
+    row = px * QUARTER
+    inner_weight = weight(one, two, row + bit * HALF_Q, HALF_Q, at, *energies)
+    outer_weight = weight(two, three, row, QUARTER, at, *energies)
     near_two = rows_at(slab_two, core * ROWS, ROWS)
     far_two = rows_at(slab_two, (1 - core) * ROWS, ROWS)
     near_two_cols, far_two_cols = cols_at(near_two, at, COLS), cols_at(far_two, at, COLS)
@@ -137,8 +139,7 @@
     inner_kept, inner_sent = halves(add_x(inner_parts))
     inner_next = move(inner_sent, ALONG[1])
 
-    arrived = after(arrived, inner_sent)
-    near = arrived[0] + arrived[1]
+    near = after(near, inner_sent)
     far = move(near, SWAP)
     near_cols = cols_at(near, at, COLS)
     outer_near = pair_term(near_two, near, near_cols, near_two_cols)
@@ -149,40 +150,47 @@
     left, right = slice(0, CHUNK), slice(CHUNK, COLS)
     sends = [send_x(outer[:, w]) for w in (left, right)]
     parts = [around(sends[n]) for n in (0, 1)]
-    inner_kept = inner_kept + after(inner_next, sends)
+    kept_a = add_x(after(parts[0], sends))
+    next_a = move(kept_a, ALONG[1])
+    inner_kept = inner_kept + after(inner_next, kept_a)
+    kept_a = kept_a + after(next_a, inner_kept)
+    far_a = move(kept_a, ALONG[2])
     inner_far = move(inner_kept, ALONG[2])
-
-    kept_a, sent_a = halves(add_x(after(parts[0], inner_kept)))
-    kept_a = kept_a + move(sent_a, ALONG[1])
-    far_a = move(kept_a, ALONG[2])
-    kept_b, sent_b = halves(add_x(after(parts[1], kept_a)))
-    next_b = move(sent_b, ALONG[1])
-
-    inner_t = (inner_kept + after(inner_far, sent_b)) * inner_weight
+    parts_b = after(parts[1], kept_a)
+    kept_b = add_x(parts_b)
+    next_b = move(kept_b, ALONG[1])
+
+    quarter_a = (kept_a + after(far_a, kept_b)) * outer_weight[:, left]
+    pieces_a = around([quarter_a] * X)
+    inner_t = (inner_kept + after(inner_far, quarter_a)) * inner_weight
     inner_other = move(inner_t, ALONG[1])
-    t_a = (kept_a + after(far_a, inner_t)) * outer_weight[:, left]
-    other_a = move(t_a, ALONG[1])
-    kept_b = kept_b + after(next_b, t_a)
+    kept_b = kept_b + after(next_b, inner_t)
     far_b = move(kept_b, ALONG[2])
-
-    quarter_a = join(t_a, after(other_a, kept_b))
-    pieces_a = around([quarter_a] * X)
-    inner_quarter = join(inner_t, after(inner_other, quarter_a))
-    inner_pieces = around([inner_quarter] * X)
-    t_b = (kept_b + after(far_b, inner_quarter)) * outer_weight[:, right]
-    other_b = move(t_b, ALONG[1])
-
-    all_a = in_order(after(pieces_a, t_b))
+    inner_quarter = join(inner_t, after(inner_other, kept_b))
+    inner_next = move(inner_quarter, ACROSS[1])
+
+    all_a = in_order(after(pieces_a, inner_quarter))
     leaving_a = dot(slab_two, all_a, 1, 0)
     incoming_a = [move(leaving_a, UP[c]) for c in (0, 1)]
-    quarter_b = join(t_b, after(other_b, leaving_a))
+    held_weight = after(outer_weight, leaving_a)
+    weight_b = held_weight[:, right]
+    far_b, weight_b = after((far_b, weight_b))
+    quarter_b = (kept_b + far_b) * weight_b
     pieces_b = around([quarter_b] * X)
-    all_b = in_order(pieces_b)
+    inner_pair = jnp.concatenate([inner_quarter, after(inner_next, quarter_b)], 0)
+    inner_rest = move(inner_pair, ACROSS[3])
+    all_b = in_order(after(pieces_b, inner_pair))
     outgoing = dot(slab_two, all_b, 1, 0)
     incoming_b = [move(outgoing, UP[c]) for c in (0, 1)]
     incoming = [incoming_a[0], incoming_b[0], incoming_a[1], incoming_b[1]]
 
-    inner_all = in_order(after(inner_pieces, outgoing))
+    inner_all = jnp.zeros((X * QUARTER, COLS), jnp.float32)
+    inner_rest = after(inner_rest, outgoing)
+    for q, d in ((inner_pair, 0), (inner_rest, 3)):
+        for part, e in ((q[:QUARTER], d), (q[QUARTER:], d ^ 1)):
+            inner_all = lax.dynamic_update_slice_in_dim(
+                inner_all, part, (px ^ e) * QUARTER, 0
+            )
     to_one = dot(two_cols, inner_all, 1, 1)
     to_two = dot(slab_one, inner_all, 1, 0)
     three_cols = jnp.where(
@@ -199,9 +207,8 @@
         jnp.concatenate([blank, to_two], 1),
     )
     crossed = move(jnp.where(first, to_two, to_one), SWAP)
-    density = jnp.where(first, to_one, to_two) + crossed
-    incoming = after(incoming, density)
-    density = density + jnp.concatenate(incoming, 1)
+    crossed, incoming = after((crossed, incoming))
+    density = jnp.where(first, to_one, to_two) + crossed + jnp.concatenate(incoming, 1)
     return density[None]
 
 

time: 279 us -> 294 us (1.054)
  the two profiles are of different devices: /device:TPU:24 before, /device:TPU:62 now
where the time goes in v6:
time: 294 us; the launch traced here: 292 us
  waiting for transfers between devices  126 us (43%)
  starting transfers between devices  120 us (41%)
  other arithmetic  19.3 us (7%)
  matrix products  16.8 us (6%)
  local copies, waits for them, and re-layouts  9.03 us (3%)
    ppermute x32, waiting for transfers between devices, move(): return lax.ppermute(block, AXES, pairs)  126 us
    ppermute x32, starting transfers between devices, move(): return lax.ppermute(block, AXES, pairs)  120 us
    dot_general x12, matrix products, dot(): lax.dot_general(a, b, (((da,), (db,)), ((), ())), precision=lax.Precision...  16.8 us
  transfers between devices with their start and end apart: 32, of which 16 were waited for; matrix products, arithmetic and copies ran while one was open for 10% of the time, Pallas kernels for 0%

profile of v6, /device:TPU:62, one launch (start us, length us, event | category | flops | bytes accessed | tf_op | source)
XLA Modules:
  0.0 292.3 jit_solution(15129216427569841442)
XLA Ops:
  0.0 1.9 collective-permute-start
  2.1 4.3 %collective-permute-done = f32[512,1024]{1,0:T(8,128)} collective-permute-done((f32[512,1024]{1,0:T(8,128)}, f32[512,1024]{1,0:T(8,128)}, u32[]{:S(2)}, u32[]{:S(2)}) %collective-permute-start) | collective-permute-done | bytes 2097184 | tf_op jit(solution)/shard_map/ppermute | solution.py:34
  6.4 2.7 broadcast_select_fusion.2
  9.2 1.8 fusion.7
  11.2 1.9 multiply_subtract_fusion.1
  13.4 2.4 collective-permute-start.1
  15.8 4.3 %collective-permute-start.2 = (f32[256,512]{1,0:T(8,128)S(1)}, f32[256,512]{1,0:T(8,128)S(1)}, u32[]{:S(2)}, u32[]{:S(2)}) collective-permute-start(f32[256,512]{1,0:T(8,128)S(1)} %get-tuple-element.108), channel_id=1, source_target_pairs={{0,8},{1,9},{2,10},{3,11},{4,12},{5,13},{6,14},{7,15},{8,0},{9,1},... | collective-permute-start | bytes 1572872 | tf_op jit(solution)/shard_map/ppermute | solution.py:34
  20.1 1.9 collective-permute-start.3
  22.1 11.7 %collective-permute-start.5 = (f32[256,1024]{1,0:T(8,128)S(1)}, f32[256,1024]{1,0:T(8,128)S(1)}, u32[]{:S(2)}, u32[]{:S(2)}) collective-permute-start(f32[256,1024]{1,0:T(8,128)S(1)} %constant_dynamic-slice_fusion.10), channel_id=1, source_target_pairs={{0,480},{1,481},{2,482},{3,483},{4,484},{5,485},{6,486},{7,487},{8... | collective-permute-start | bytes 3145736 | tf_op jit(solution)/shard_map/ppermute | solution.py:34
  34.4 1.2 fusion.17
  38.2 2.1 subtract_divide_fusion.1
  40.3 2.2 subtract_divide_fusion
  42.5 1.6 collective-permute-done.3
  45.2 29.6 %collective-permute-done.5 = f32[256,1024]{1,0:T(8,128)S(1)} collective-permute-done((f32[256,1024]{1,0:T(8,128)S(1)}, f32[256,1024]{1,0:T(8,128)S(1)}, u32[]{:S(2)}, u32[]{:S(2)}) %collective-permute-start.5) | collective-permute-done | bytes 1048608 | tf_op jit(solution)/shard_map/ppermute | solution.py:34
  74.7 1.9 collective-permute-start.6
  76.7 1.0 fusion.23
  77.8 1.2 multiply_subtract_fusion
  79.3 1.0 fusion.24
  80.4 1.3 subtract_add_fusion
  81.9 4.9 %collective-permute-start.7 = (f32[256,256]{1,0:T(8,128)S(1)}, f32[256,256]{1,0:T(8,128)S(1)}, u32[]{:S(2)}, u32[]{:S(2)}) collective-permute-start(f32[256,256]{1,0:T(8,128)S(1)} %get-tuple-element.117), channel_id=1, source_target_pairs={{0,4},{1,5},{2,6},{3,7},{4,8},{5,9},{6,10},{7,11},{8,12},{9,13},{1... | collective-permute-start | bytes 786440 | tf_op jit(solution)/shard_map/ppermute | solution.py:34
  86.8 2.0 collective-permute-start.8
  88.7 3.3 %collective-permute-start.9 = (f32[256,256]{1,0:T(8,128)S(1)}, f32[256,256]{1,0:T(8,128)S(1)}, u32[]{:S(2)}, u32[]{:S(2)}) collective-permute-start(f32[256,256]{1,0:T(8,128)S(1)} %get-tuple-element.115), channel_id=1, source_target_pairs={{0,12},{1,13},{2,14},{3,15},{4,0},{5,1},{6,2},{7,3},{8,4},{9,5},{1... | collective-permute-start | bytes 786440 | tf_op jit(solution)/shard_map/ppermute | solution.py:34
  92.1 10.6 %collective-permute-start.4 = (f32[128,512]{1,0:T(8,128)}, f32[128,512]{1,0:T(8,128)}, u32[]{:S(2)}, u32[]{:S(2)}) collective-permute-start(f32[128,512]{1,0:T(8,128)} %constant_dynamic-slice_fusion.11), channel_id=1, source_target_pairs={{0,1},{1,0},{2,3},{3,2},{4,5},{5,4},{6,7},{7,6},{8,9},{9,8},{10,11... | collective-permute-start | bytes 786440 | tf_op jit(solution)/shard_map/ppermute | solution.py:34
  103.9 10.5 %collective-permute-start.11 = (f32[256,256]{1,0:T(8,128)S(1)}, f32[256,256]{1,0:T(8,128)}, u32[]{:S(2)}, u32[]{:S(2)}) collective-permute-start(f32[256,256]{1,0:T(8,128)S(1)} %add_add_fusion.2), channel_id=1, source_target_pairs={{0,1},{1,0},{2,3},{3,2},{4,5},{5,4},{6,7},{7,6},{8,9},{9,8},{10,11... | collective-permute-start | bytes 786440 | tf_op jit(solution)/shard_map/ppermute | solution.py:34
  114.4 2.5 collective-permute-start.13
  116.9 2.2 collective-permute-start.14
  119.1 3.1 %collective-permute-start.15 = (f32[256,256]{1,0:T(8,128)}, f32[256,256]{1,0:T(8,128)}, u32[]{:S(2)}, u32[]{:S(2)}) collective-permute-start(f32[256,256]{1,0:T(8,128)} %get-tuple-element.111), channel_id=1, source_target_pairs={{0,12},{1,13},{2,14},{3,15},{4,0},{5,1},{6,2},{7,3},{8,4},{9,5},{1... | collective-permute-start | bytes 786440 | tf_op jit(solution)/shard_map/ppermute | solution.py:34
  122.3 1.1 dynamic-slice_add_fusion
  124.4 6.9 %collective-permute-start.12 = (f32[256,256]{1,0:T(8,128)S(1)}, f32[256,256]{1,0:T(8,128)S(1)}, u32[]{:S(2)}, u32[]{:S(2)}) collective-permute-start(f32[256,256]{1,0:T(8,128)S(1)} %add.342), channel_id=1, source_target_pairs={{0,2},{1,3},{2,0},{3,1},{4,6},{5,7},{6,4},{7,5},{8,10},{9,11},{10,... | collective-permute-start | bytes 786440 | tf_op jit(solution)/shard_map/ppermute | solution.py:34
  131.3 1.9 collective-permute-start.10
  133.6 1.3 add_add_fusion.1
  134.9 3.5 %collective-permute-start.17 = (f32[256,256]{1,0:T(8,128)S(1)}, f32[256,256]{1,0:T(8,128)}, u32[]{:S(2)}, u32[]{:S(2)}) collective-permute-start(f32[256,256]{1,0:T(8,128)S(1)} %add_add_fusion.1), channel_id=1, source_target_pairs={{0,1},{1,0},{2,3},{3,2},{4,5},{5,4},{6,7},{7,6},{8,9},{9,8},{10,11... | collective-permute-start | bytes 786440 | tf_op jit(solution)/shard_map/ppermute | solution.py:34
  138.4 11.3 %collective-permute-done.12 = f32[256,256]{1,0:T(8,128)S(1)} collective-permute-done((f32[256,256]{1,0:T(8,128)S(1)}, f32[256,256]{1,0:T(8,128)S(1)}, u32[]{:S(2)}, u32[]{:S(2)}) %collective-permute-start.12) | collective-permute-done | bytes 262176 | tf_op jit(solution)/shard_map/ppermute | solution.py:34
  150.5 3.6 %collective-permute-done.10 = f32[128,512]{1,0:T(8,128)S(1)} collective-permute-done((f32[128,512]{1,0:T(8,128)S(1)}, f32[128,512]{1,0:T(8,128)S(1)}, u32[]{:S(2)}, u32[]{:S(2)}) %collective-permute-start.10) | collective-permute-done | bytes 262176 | tf_op jit(solution)/shard_map/ppermute | solution.py:34
  154.9 2.6 collective-permute-start.16
  157.5 4.6 %collective-permute-start.20 = (f32[256,256]{1,0:T(8,128)}, f32[256,256]{1,0:T(8,128)}, u32[]{:S(2)}, u32[]{:S(2)}) collective-permute-start(f32[256,256]{1,0:T(8,128)} %slice_multiply_fusion), channel_id=1, source_target_pairs={{0,4},{1,5},{2,6},{3,7},{4,8},{5,9},{6,10},{7,11},{8,12},{9,13},{1... | collective-permute-start | bytes 786440 | tf_op jit(solution)/shard_map/ppermute | solution.py:34
  162.1 3.1 %collective-permute-start.21 = (f32[256,256]{1,0:T(8,128)}, f32[256,256]{1,0:T(8,128)}, u32[]{:S(2)}, u32[]{:S(2)}) collective-permute-start(f32[256,256]{1,0:T(8,128)} %slice_multiply_fusion), channel_id=1, source_target_pairs={{0,8},{1,9},{2,10},{3,11},{4,12},{5,13},{6,14},{7,15},{8,0},{9,1},... | collective-permute-start | bytes 786440 | tf_op jit(solution)/shard_map/ppermute | solution.py:34
  165.2 3.3 %collective-permute-start.22 = (f32[256,256]{1,0:T(8,128)}, f32[256,256]{1,0:T(8,128)}, u32[]{:S(2)}, u32[]{:S(2)}) collective-permute-start(f32[256,256]{1,0:T(8,128)} %slice_multiply_fusion), channel_id=1, source_target_pairs={{0,12},{1,13},{2,14},{3,15},{4,0},{5,1},{6,2},{7,3},{8,4},{9,5},{1... | collective-permute-start | bytes 786440 | tf_op jit(solution)/shard_map/ppermute | solution.py:34
  169.6 5.3 %collective-permute-start.19 = (f32[256,256]{1,0:T(8,128)S(1)}, f32[256,256]{1,0:T(8,128)S(1)}, u32[]{:S(2)}, u32[]{:S(2)}) collective-permute-start(f32[256,256]{1,0:T(8,128)S(1)} %add.348), channel_id=1, source_target_pairs={{0,2},{1,3},{2,0},{3,1},{4,6},{5,7},{6,4},{7,5},{8,10},{9,11},{10,... | collective-permute-start | bytes 786440 | tf_op jit(solution)/shard_map/ppermute | solution.py:34
  175.2 1.3 constant_dynamic-update-slice_fusion.9
  176.5 2.8 collective-permute-start.18
  184.4 1.2 collective-permute-done.19
  185.6 4.0 %collective-permute-start.24 = (f32[256,256]{1,0:T(8,128)S(1)}, f32[256,256]{1,0:T(8,128)S(1)}, u32[]{:S(2)}, u32[]{:S(2)}) collective-permute-start(f32[256,256]{1,0:T(8,128)S(1)} %add_multiply_fusion), channel_id=1, source_target_pairs={{0,4},{1,5},{2,6},{3,7},{4,8},{5,9},{6,10},{7,11},{8,12},{9,13},{1... | collective-permute-start | bytes 786440 | tf_op jit(solution)/shard_map/ppermute | solution.py:34
  189.7 2.8 collective-permute-start.25
  192.4 1.9 collective-permute-start.26
  194.6 5.1 %collective-permute-start.23 = (f32[512,512]{1,0:T(8,128)S(1)}, f32[512,512]{1,0:T(8,128)S(1)}, u32[]{:S(2)}, u32[]{:S(2)}) collective-permute-start(f32[512,512]{1,0:T(8,128)S(1)} %pad_maximum_fusion), channel_id=1, source_target_pairs={{0,12},{1,13},{2,14},{3,15},{4,8},{5,9},{6,10},{7,11},{8,4},{9,5},... | collective-permute-start | bytes 3145736 | tf_op jit(solution)/shard_map/ppermute | solution.py:34
  199.7 2.6 collective-permute-done.25
  202.3 4.4 %collective-permute-done.26 = f32[256,256]{1,0:T(8,128)S(1)} collective-permute-done((f32[256,256]{1,0:T(8,128)S(1)}, f32[256,256]{1,0:T(8,128)S(1)}, u32[]{:S(2)}, u32[]{:S(2)}) %collective-permute-start.26) | collective-permute-done | bytes 262176 | tf_op jit(solution)/shard_map/ppermute | solution.py:34
  206.9 1.0 fusion.26
  208.0 1.1 fusion.10
  209.1 20.0 %collective-permute-done.23 = f32[512,512]{1,0:T(8,128)S(1)} collective-permute-done((f32[512,512]{1,0:T(8,128)S(1)}, f32[512,512]{1,0:T(8,128)S(1)}, u32[]{:S(2)}, u32[]{:S(2)}) %collective-permute-start.23) | collective-permute-done | bytes 1048608 | tf_op jit(solution)/shard_map/ppermute | solution.py:34
  229.2 1.9 fusion.27
  231.2 2.0 fusion.5
  233.1 1.5 broadcast_select_fusion
  234.6 1.9 collective-permute-start.27
  236.5 1.9 collective-permute-start.28
  238.5 1.3 collective-permute-start.30
  239.8 2.9 collective-permute-start.29
  242.7 1.3 collective-permute-start.31
  244.0 21.7 %collective-permute-done.28 = f32[512,256]{1,0:T(8,128)S(1)} collective-permute-done((f32[512,256]{1,0:T(8,128)S(1)}, f32[512,256]{1,0:T(8,128)S(1)}, u32[]{:S(2)}, u32[]{:S(2)}) %collective-permute-start.28) | collective-permute-done | bytes 524320 | tf_op jit(solution)/shard_map/ppermute | solution.py:34
  265.7 5.3 %collective-permute-done.30 = f32[512,256]{1,0:T(8,128)S(1)} collective-permute-done((f32[512,256]{1,0:T(8,128)S(1)}, f32[512,256]{1,0:T(8,128)S(1)}, u32[]{:S(2)}, u32[]{:S(2)}) %collective-permute-start.30) | collective-permute-done | bytes 524320 | tf_op jit(solution)/shard_map/ppermute | solution.py:34
  270.9 16.6 %collective-permute-done.29 = f32[512,256]{1,0:T(8,128)S(1)} collective-permute-done((f32[512,256]{1,0:T(8,128)S(1)}, f32[512,256]{1,0:T(8,128)S(1)}, u32[]{:S(2)}, u32[]{:S(2)}) %collective-permute-start.29) | collective-permute-done | bytes 524320 | tf_op jit(solution)/shard_map/ppermute | solution.py:34
  287.5 2.6 collective-permute-done.31
  290.2 2.2 fusion
  (78 shorter events, 16.3 us)
Async XLA Ops:
  0.0 6.4 %collective-permute-start = (f32[512,1024]{1,0:T(8,128)}, f32[512,1024]{1,0:T(8,128)}, u32[]{:S(2)}, u32[]{:S(2)}) collective-permute-start(f32[512,1024]{1,0:T(8,128)} %bitcast.30), channel_id=1, source_target_pairs={{0,16},{1,17},{2,18},{3,19},{4,20},{5,21},{6,22},{7,23},{8,24},{9,... | collective-permute-start | bytes 6291464 | tf_op jit(solution)/shard_map/ppermute | solution.py:34
  9.1 2.1 copy-start
  13.1 20.6 %copy-start.5 = (s32[32]{0:T(128)S(1)}, s32[32]{0:T(128)}, u32[]{:S(2)}) copy-start(s32[32]{0:T(128)} %param.7) | copy-start | bytes 388
  13.4 24.0 %copy-start.7 = (f32[1024]{0:T(1024)S(1)}, f32[1024]{0:T(1024)}, u32[]{:S(2)}) copy-start(f32[1024]{0:T(1024)} %param.6) | copy-start | bytes 12292
  13.4 24.2 %copy-start.6 = (f32[32]{0:T(128)S(1)}, f32[32]{0:T(128)}, u32[]{:S(2)}) copy-start(f32[32]{0:T(128)} %param.5) | copy-start | bytes 388
  13.4 29.1 %collective-permute-start.1 = (f32[256,512]{1,0:T(8,128)S(1)}, f32[256,512]{1,0:T(8,128)S(1)}, u32[]{:S(2)}, u32[]{:S(2)}) collective-permute-start(f32[256,512]{1,0:T(8,128)S(1)} %get-tuple-element.109), channel_id=1, source_target_pairs={{0,4},{1,5},{2,6},{3,7},{4,8},{5,9},{6,10},{7,11},{8,12},{9,13},{1... | collective-permute-start | bytes 1572872 | tf_op jit(solution)/shard_map/ppermute | solution.py:34
  15.8 26.7 %collective-permute-start.2 = (f32[256,512]{1,0:T(8,128)S(1)}, f32[256,512]{1,0:T(8,128)S(1)}, u32[]{:S(2)}, u32[]{:S(2)}) collective-permute-start(f32[256,512]{1,0:T(8,128)S(1)} %get-tuple-element.108), channel_id=1, source_target_pairs={{0,8},{1,9},{2,10},{3,11},{4,12},{5,13},{6,14},{7,15},{8,0},{9,1},... | collective-permute-start | bytes 1572872 | tf_op jit(solution)/shard_map/ppermute | solution.py:34
  20.1 24.0 %collective-permute-start.3 = (f32[256,512]{1,0:T(8,128)S(1)}, f32[256,512]{1,0:T(8,128)S(1)}, u32[]{:S(2)}, u32[]{:S(2)}) collective-permute-start(f32[256,512]{1,0:T(8,128)S(1)} %get-tuple-element.107), channel_id=1, source_target_pairs={{0,12},{1,13},{2,14},{3,15},{4,0},{5,1},{6,2},{7,3},{8,4},{9,5},{1... | collective-permute-start | bytes 1572872 | tf_op jit(solution)/shard_map/ppermute | solution.py:34
  22.1 52.7 %collective-permute-start.5 = (f32[256,1024]{1,0:T(8,128)S(1)}, f32[256,1024]{1,0:T(8,128)S(1)}, u32[]{:S(2)}, u32[]{:S(2)}) collective-permute-start(f32[256,1024]{1,0:T(8,128)S(1)} %constant_dynamic-slice_fusion.10), channel_id=1, source_target_pairs={{0,480},{1,481},{2,482},{3,483},{4,484},{5,485},{6,486},{7,487},{8... | collective-permute-start | bytes 3145736 | tf_op jit(solution)/shard_map/ppermute | solution.py:34
  44.4 32.3 %copy-start.2 = (f32[256,512]{1,0:T(8,128)}, f32[256,512]{1,0:T(8,128)S(1)}, u32[]{:S(2)}) copy-start(f32[256,512]{1,0:T(8,128)S(1)} %add_add_fusion) | copy-start | bytes 1572868
  74.7 4.5 %collective-permute-start.6 = (f32[256,1024]{1,0:T(8,128)S(1)}, f32[256,1024]{1,0:T(8,128)S(1)}, u32[]{:S(2)}, u32[]{:S(2)}) collective-permute-start(f32[256,1024]{1,0:T(8,128)S(1)} %collective-permute-done.5), channel_id=1, source_target_pairs={{0,16},{1,17},{2,18},{3,19},{4,20},{5,21},{6,22},{7,23},{8,24},{9,... | collective-permute-start | bytes 3145736 | tf_op jit(solution)/shard_map/ppermute | solution.py:34
  81.9 21.8 %collective-permute-start.7 = (f32[256,256]{1,0:T(8,128)S(1)}, f32[256,256]{1,0:T(8,128)S(1)}, u32[]{:S(2)}, u32[]{:S(2)}) collective-permute-start(f32[256,256]{1,0:T(8,128)S(1)} %get-tuple-element.117), channel_id=1, source_target_pairs={{0,4},{1,5},{2,6},{3,7},{4,8},{5,9},{6,10},{7,11},{8,12},{9,13},{1... | collective-permute-start | bytes 786440 | tf_op jit(solution)/shard_map/ppermute | solution.py:34
  86.8 17.0 %collective-permute-start.8 = (f32[256,256]{1,0:T(8,128)S(1)}, f32[256,256]{1,0:T(8,128)S(1)}, u32[]{:S(2)}, u32[]{:S(2)}) collective-permute-start(f32[256,256]{1,0:T(8,128)S(1)} %get-tuple-element.116), channel_id=1, source_target_pairs={{0,8},{1,9},{2,10},{3,11},{4,12},{5,13},{6,14},{7,15},{8,0},{9,1},... | collective-permute-start | bytes 786440 | tf_op jit(solution)/shard_map/ppermute | solution.py:34
  88.7 15.1 %collective-permute-start.9 = (f32[256,256]{1,0:T(8,128)S(1)}, f32[256,256]{1,0:T(8,128)S(1)}, u32[]{:S(2)}, u32[]{:S(2)}) collective-permute-start(f32[256,256]{1,0:T(8,128)S(1)} %get-tuple-element.115), channel_id=1, source_target_pairs={{0,12},{1,13},{2,14},{3,15},{4,0},{5,1},{6,2},{7,3},{8,4},{9,5},{1... | collective-permute-start | bytes 786440 | tf_op jit(solution)/shard_map/ppermute | solution.py:34
  92.1 30.2 %collective-permute-start.4 = (f32[128,512]{1,0:T(8,128)}, f32[128,512]{1,0:T(8,128)}, u32[]{:S(2)}, u32[]{:S(2)}) collective-permute-start(f32[128,512]{1,0:T(8,128)} %constant_dynamic-slice_fusion.11), channel_id=1, source_target_pairs={{0,1},{1,0},{2,3},{3,2},{4,5},{5,4},{6,7},{7,6},{8,9},{9,8},{10,11... | collective-permute-start | bytes 786440 | tf_op jit(solution)/shard_map/ppermute | solution.py:34
  103.9 19.5 %collective-permute-start.11 = (f32[256,256]{1,0:T(8,128)S(1)}, f32[256,256]{1,0:T(8,128)}, u32[]{:S(2)}, u32[]{:S(2)}) collective-permute-start(f32[256,256]{1,0:T(8,128)S(1)} %add_add_fusion.2), channel_id=1, source_target_pairs={{0,1},{1,0},{2,3},{3,2},{4,5},{5,4},{6,7},{7,6},{8,9},{9,8},{10,11... | collective-permute-start | bytes 786440 | tf_op jit(solution)/shard_map/ppermute | solution.py:34
  114.4 18.8 %collective-permute-start.13 = (f32[256,256]{1,0:T(8,128)}, f32[256,256]{1,0:T(8,128)}, u32[]{:S(2)}, u32[]{:S(2)}) collective-permute-start(f32[256,256]{1,0:T(8,128)} %get-tuple-element.113), channel_id=1, source_target_pairs={{0,4},{1,5},{2,6},{3,7},{4,8},{5,9},{6,10},{7,11},{8,12},{9,13},{1... | collective-permute-start | bytes 786440 | tf_op jit(solution)/shard_map/ppermute | solution.py:34
  116.9 16.3 %collective-permute-start.14 = (f32[256,256]{1,0:T(8,128)}, f32[256,256]{1,0:T(8,128)}, u32[]{:S(2)}, u32[]{:S(2)}) collective-permute-start(f32[256,256]{1,0:T(8,128)} %get-tuple-element.112), channel_id=1, source_target_pairs={{0,8},{1,9},{2,10},{3,11},{4,12},{5,13},{6,14},{7,15},{8,0},{9,1},... | collective-permute-start | bytes 786440 | tf_op jit(solution)/shard_map/ppermute | solution.py:34
  119.1 14.5 %collective-permute-start.15 = (f32[256,256]{1,0:T(8,128)}, f32[256,256]{1,0:T(8,128)}, u32[]{:S(2)}, u32[]{:S(2)}) collective-permute-start(f32[256,256]{1,0:T(8,128)} %get-tuple-element.111), channel_id=1, source_target_pairs={{0,12},{1,13},{2,14},{3,15},{4,0},{5,1},{6,2},{7,3},{8,4},{9,5},{1... | collective-permute-start | bytes 786440 | tf_op jit(solution)/shard_map/ppermute | solution.py:34
  122.2 27.5 %copy-start.3 = (f32[256,512]{1,0:T(8,128)S(1)}, f32[256,512]{1,0:T(8,128)}, u32[]{:S(2)}) copy-start(f32[256,512]{1,0:T(8,128)} %subtract_divide_fusion) | copy-start | bytes 1572868
  122.2 31.9 %copy-start.4 = (f32[128,512]{1,0:T(8,128)S(1)}, f32[128,512]{1,0:T(8,128)}, u32[]{:S(2)}) copy-start(f32[128,512]{1,0:T(8,128)} %subtract_divide_fusion.1) | copy-start | bytes 786436
  124.4 25.4 %collective-permute-start.12 = (f32[256,256]{1,0:T(8,128)S(1)}, f32[256,256]{1,0:T(8,128)S(1)}, u32[]{:S(2)}, u32[]{:S(2)}) collective-permute-start(f32[256,256]{1,0:T(8,128)S(1)} %add.342), channel_id=1, source_target_pairs={{0,2},{1,3},{2,0},{3,1},{4,6},{5,7},{6,4},{7,5},{8,10},{9,11},{10,... | collective-permute-start | bytes 786440 | tf_op jit(solution)/shard_map/ppermute | solution.py:34
  131.3 22.9 %collective-permute-start.10 = (f32[128,512]{1,0:T(8,128)S(1)}, f32[128,512]{1,0:T(8,128)S(1)}, u32[]{:S(2)}, u32[]{:S(2)}) collective-permute-start(f32[128,512]{1,0:T(8,128)S(1)} %dynamic-slice_add_fusion), channel_id=1, source_target_pairs={{0,2},{1,3},{2,0},{3,1},{4,6},{5,7},{6,4},{7,5},{8,10},{9,11},{10,... | collective-permute-start | bytes 786440 | tf_op jit(solution)/shard_map/ppermute | solution.py:34
  134.9 33.7 %collective-permute-start.17 = (f32[256,256]{1,0:T(8,128)S(1)}, f32[256,256]{1,0:T(8,128)}, u32[]{:S(2)}, u32[]{:S(2)}) collective-permute-start(f32[256,256]{1,0:T(8,128)S(1)} %add_add_fusion.1), channel_id=1, source_target_pairs={{0,1},{1,0},{2,3},{3,2},{4,5},{5,4},{6,7},{7,6},{8,9},{9,8},{10,11... | collective-permute-start | bytes 786440 | tf_op jit(solution)/shard_map/ppermute | solution.py:34
  154.9 20.0 %collective-permute-start.16 = (f32[128,512]{1,0:T(8,128)}, f32[128,512]{1,0:T(8,128)}, u32[]{:S(2)}, u32[]{:S(2)}) collective-permute-start(f32[128,512]{1,0:T(8,128)} %add_multiply_fusion.1), channel_id=1, source_target_pairs={{0,1},{1,0},{2,3},{3,2},{4,5},{5,4},{6,7},{7,6},{8,9},{9,8},{10,11... | collective-permute-start | bytes 786440 | tf_op jit(solution)/shard_map/ppermute | solution.py:34
  157.5 21.8 %collective-permute-start.20 = (f32[256,256]{1,0:T(8,128)}, f32[256,256]{1,0:T(8,128)}, u32[]{:S(2)}, u32[]{:S(2)}) collective-permute-start(f32[256,256]{1,0:T(8,128)} %slice_multiply_fusion), channel_id=1, source_target_pairs={{0,4},{1,5},{2,6},{3,7},{4,8},{5,9},{6,10},{7,11},{8,12},{9,13},{1... | collective-permute-start | bytes 786440 | tf_op jit(solution)/shard_map/ppermute | solution.py:34
  162.1 17.2 %collective-permute-start.21 = (f32[256,256]{1,0:T(8,128)}, f32[256,256]{1,0:T(8,128)}, u32[]{:S(2)}, u32[]{:S(2)}) collective-permute-start(f32[256,256]{1,0:T(8,128)} %slice_multiply_fusion), channel_id=1, source_target_pairs={{0,8},{1,9},{2,10},{3,11},{4,12},{5,13},{6,14},{7,15},{8,0},{9,1},... | collective-permute-start | bytes 786440 | tf_op jit(solution)/shard_map/ppermute | solution.py:34
  165.2 14.2 %collective-permute-start.22 = (f32[256,256]{1,0:T(8,128)}, f32[256,256]{1,0:T(8,128)}, u32[]{:S(2)}, u32[]{:S(2)}) collective-permute-start(f32[256,256]{1,0:T(8,128)} %slice_multiply_fusion), channel_id=1, source_target_pairs={{0,12},{1,13},{2,14},{3,15},{4,0},{5,1},{6,2},{7,3},{8,4},{9,5},{1... | collective-permute-start | bytes 786440 | tf_op jit(solution)/shard_map/ppermute | solution.py:34
  169.6 16.0 %collective-permute-start.19 = (f32[256,256]{1,0:T(8,128)S(1)}, f32[256,256]{1,0:T(8,128)S(1)}, u32[]{:S(2)}, u32[]{:S(2)}) collective-permute-start(f32[256,256]{1,0:T(8,128)S(1)} %add.348), channel_id=1, source_target_pairs={{0,2},{1,3},{2,0},{3,1},{4,6},{5,7},{6,4},{7,5},{8,10},{9,11},{10,... | collective-permute-start | bytes 786440 | tf_op jit(solution)/shard_map/ppermute | solution.py:34
  176.5 18.0 %collective-permute-start.18 = (f32[256,512]{1,0:T(8,128)S(1)}, f32[256,512]{1,0:T(8,128)S(1)}, u32[]{:S(2)}, u32[]{:S(2)}) collective-permute-start(f32[256,512]{1,0:T(8,128)S(1)} %get-tuple-element.98), channel_id=1, source_target_pairs={{0,4},{1,5},{2,6},{3,7},{4,0},{5,1},{6,2},{7,3},{8,12},{9,13},{10,... | collective-permute-start | bytes 1572872 | tf_op jit(solution)/shard_map/ppermute | solution.py:34
  183.3 2.3 slice-start
  185.6 14.1 %collective-permute-start.24 = (f32[256,256]{1,0:T(8,128)S(1)}, f32[256,256]{1,0:T(8,128)S(1)}, u32[]{:S(2)}, u32[]{:S(2)}) collective-permute-start(f32[256,256]{1,0:T(8,128)S(1)} %add_multiply_fusion), channel_id=1, source_target_pairs={{0,4},{1,5},{2,6},{3,7},{4,8},{5,9},{6,10},{7,11},{8,12},{9,13},{1... | collective-permute-start | bytes 786440 | tf_op jit(solution)/shard_map/ppermute | solution.py:34
  189.7 12.6 %collective-permute-start.25 = (f32[256,256]{1,0:T(8,128)S(1)}, f32[256,256]{1,0:T(8,128)S(1)}, u32[]{:S(2)}, u32[]{:S(2)}) collective-permute-start(f32[256,256]{1,0:T(8,128)S(1)} %add_multiply_fusion), channel_id=1, source_target_pairs={{0,8},{1,9},{2,10},{3,11},{4,12},{5,13},{6,14},{7,15},{8,0},{9,1},... | collective-permute-start | bytes 786440 | tf_op jit(solution)/shard_map/ppermute | solution.py:34
  192.4 14.3 %collective-permute-start.26 = (f32[256,256]{1,0:T(8,128)S(1)}, f32[256,256]{1,0:T(8,128)S(1)}, u32[]{:S(2)}, u32[]{:S(2)}) collective-permute-start(f32[256,256]{1,0:T(8,128)S(1)} %add_multiply_fusion), channel_id=1, source_target_pairs={{0,12},{1,13},{2,14},{3,15},{4,0},{5,1},{6,2},{7,3},{8,4},{9,5},{1... | collective-permute-start | bytes 786440 | tf_op jit(solution)/shard_map/ppermute | solution.py:34
  194.6 34.5 %collective-permute-start.23 = (f32[512,512]{1,0:T(8,128)S(1)}, f32[512,512]{1,0:T(8,128)S(1)}, u32[]{:S(2)}, u32[]{:S(2)}) collective-permute-start(f32[512,512]{1,0:T(8,128)S(1)} %pad_maximum_fusion), channel_id=1, source_target_pairs={{0,12},{1,13},{2,14},{3,15},{4,8},{5,9},{6,10},{7,11},{8,4},{9,5},... | collective-permute-start | bytes 3145736 | tf_op jit(solution)/shard_map/ppermute | solution.py:34
  208.0 21.2 %copy-start.1 = (f32[512,1024]{1,0:T(8,128)S(1)}, f32[512,1024]{1,0:T(8,128)}, u32[]{:S(2)}) copy-start(f32[512,1024]{1,0:T(8,128)} %copy-done) | copy-start | bytes 6291460
  234.6 55.6 %collective-permute-start.27 = (f32[512,1024]{1,0:T(8,128)S(1)}, f32[512,1024]{1,0:T(8,128)S(1)}, u32[]{:S(2)}, u32[]{:S(2)}) collective-permute-start(f32[512,1024]{1,0:T(8,128)S(1)} %get-tuple-element.125), channel_id=1, source_target_pairs={{0,16},{1,17},{2,18},{3,19},{4,20},{5,21},{6,22},{7,23},{8,24},{9,... | collective-permute-start | bytes 6291464 | tf_op jit(solution)/shard_map/ppermute | solution.py:34
  236.5 29.1 %collective-permute-start.28 = (f32[512,256]{1,0:T(8,128)S(1)}, f32[512,256]{1,0:T(8,128)S(1)}, u32[]{:S(2)}, u32[]{:S(2)}) collective-permute-start(f32[512,256]{1,0:T(8,128)S(1)} %fusion.25), channel_id=1, source_target_pairs={{0,32},{1,33},{2,34},{3,35},{4,36},{5,37},{6,38},{7,39},{8,40},{9,... | collective-permute-start | bytes 1572872 | tf_op jit(solution)/shard_map/ppermute | solution.py:34
  238.5 32.5 %collective-permute-start.30 = (f32[512,256]{1,0:T(8,128)S(1)}, f32[512,256]{1,0:T(8,128)S(1)}, u32[]{:S(2)}, u32[]{:S(2)}) collective-permute-start(f32[512,256]{1,0:T(8,128)S(1)} %fusion.25), channel_id=1, source_target_pairs={{16,32},{17,33},{18,34},{19,35},{20,36},{21,37},{22,38},{23,39},{2... | collective-permute-start | bytes 1572872 | tf_op jit(solution)/shard_map/ppermute | solution.py:34
  239.8 47.7 %collective-permute-start.29 = (f32[512,256]{1,0:T(8,128)S(1)}, f32[512,256]{1,0:T(8,128)S(1)}, u32[]{:S(2)}, u32[]{:S(2)}) collective-permute-start(f32[512,256]{1,0:T(8,128)S(1)} %fusion.26), channel_id=1, source_target_pairs={{0,32},{1,33},{2,34},{3,35},{4,36},{5,37},{6,38},{7,39},{8,40},{9,... | collective-permute-start | bytes 1572872 | tf_op jit(solution)/shard_map/ppermute | solution.py:34
  242.7 47.5 %collective-permute-start.31 = (f32[512,256]{1,0:T(8,128)S(1)}, f32[512,256]{1,0:T(8,128)S(1)}, u32[]{:S(2)}, u32[]{:S(2)}) collective-permute-start(f32[512,256]{1,0:T(8,128)S(1)} %fusion.26), channel_id=1, source_target_pairs={{16,32},{17,33},{18,34},{19,35},{20,36},{21,37},{22,38},{23,39},{2... | collective-permute-start | bytes 1572872 | tf_op jit(solution)/shard_map/ppermute | solution.py:34

commit v7 on v6

--- a/solution.py
+++ b/solution.py
@@ -106,12 +106,13 @@
             jnp.concatenate([other, part], 0),
         )
 
+    def place(whole, piece, quarter):
+        return lax.dynamic_update_slice_in_dim(whole, piece, quarter * QUARTER, 0)
+
     def in_order(pieces):
         whole = jnp.zeros((X * QUARTER, pieces[0].shape[1]), jnp.float32)
         for r, piece in enumerate(pieces):
-            whole = lax.dynamic_update_slice_in_dim(
-                whole, piece, (px - r) % X * QUARTER, 0
-            )
+            whole = place(whole, piece, (px - r) % X)
         return whole
 
     one, two, three = base, base + 1, (base + 2) % ORB
@@ -150,26 +151,30 @@
     left, right = slice(0, CHUNK), slice(CHUNK, COLS)
     sends = [send_x(outer[:, w]) for w in (left, right)]
     parts = [around(sends[n]) for n in (0, 1)]
-    kept_a = add_x(after(parts[0], sends))
+    inner_kept = inner_kept + after(inner_next, sends[0])
+    inner_far = move(inner_kept, ALONG[2])
+
+    kept_a = add_x(after(parts[0], sends, inner_kept))
     next_a = move(kept_a, ALONG[1])
-    inner_kept = inner_kept + after(inner_next, kept_a)
-    kept_a = kept_a + after(next_a, inner_kept)
+    held_weight = after(outer_weight, kept_a)
+    weight_a = held_weight[:, left]
+    inner_far, weight_a = after((inner_far, weight_a))
+    inner_t = (inner_kept + inner_far) * inner_weight
+    inner_other = move(inner_t, ALONG[1])
+    kept_a = kept_a + after(next_a, inner_t)
     far_a = move(kept_a, ALONG[2])
-    inner_far = move(inner_kept, ALONG[2])
     parts_b = after(parts[1], kept_a)
     kept_b = add_x(parts_b)
     next_b = move(kept_b, ALONG[1])
-
-    quarter_a = (kept_a + after(far_a, kept_b)) * outer_weight[:, left]
-    pieces_a = around([quarter_a] * X)
-    inner_t = (inner_kept + after(inner_far, quarter_a)) * inner_weight
-    inner_other = move(inner_t, ALONG[1])
-    kept_b = kept_b + after(next_b, inner_t)
-    far_b = move(kept_b, ALONG[2])
     inner_quarter = join(inner_t, after(inner_other, kept_b))
     inner_next = move(inner_quarter, ACROSS[1])
 
-    all_a = in_order(after(pieces_a, inner_quarter))
+    quarter_a = (kept_a + after(far_a, inner_quarter)) * weight_a
+    pieces_a = around([quarter_a] * X)
+    kept_b = kept_b + after(next_b, quarter_a)
+    far_b = move(kept_b, ALONG[2])
+
+    all_a = in_order(after(pieces_a, kept_b))
     leaving_a = dot(slab_two, all_a, 1, 0)
     incoming_a = [move(leaving_a, UP[c]) for c in (0, 1)]
     held_weight = after(outer_weight, leaving_a)
@@ -185,12 +190,12 @@
     incoming = [incoming_a[0], incoming_b[0], incoming_a[1], incoming_b[1]]
 
     inner_all = jnp.zeros((X * QUARTER, COLS), jnp.float32)
-    inner_rest = after(inner_rest, outgoing)
-    for q, d in ((inner_pair, 0), (inner_rest, 3)):
-        for part, e in ((q[:QUARTER], d), (q[QUARTER:], d ^ 1)):
-            inner_all = lax.dynamic_update_slice_in_dim(
-                inner_all, part, (px ^ e) * QUARTER, 0
-            )
+    inner_pair = after(inner_pair, outgoing)
+    inner_all = place(inner_all, inner_pair[:QUARTER], px)
+    inner_all = place(inner_all, inner_pair[QUARTER:], px ^ 1)
+    inner_rest = after(inner_rest, inner_all)
+    inner_all = place(inner_all, inner_rest[:QUARTER], px ^ 3)
+    inner_all = place(inner_all, inner_rest[QUARTER:], px ^ 2)
     to_one = dot(two_cols, inner_all, 1, 1)
     to_two = dot(slab_one, inner_all, 1, 0)
     three_cols = jnp.where(

time: 294 us -> 288 us (0.980)
  the two profiles are of different devices: /device:TPU:62 before, /device:TPU:6 now
where the time goes in v7:
time: 288 us; the launch traced here: 287 us
  waiting for transfers between devices  118 us (41%)
  starting transfers between devices  114 us (40%)
  other arithmetic  20.5 us (7%)
  matrix products  20.5 us (7%)
  local copies, waits for them, and re-layouts  12.5 us (4%)
    ppermute x32, waiting for transfers between devices, move(): return lax.ppermute(block, AXES, pairs)  118 us
    ppermute x32, starting transfers between devices, move(): return lax.ppermute(block, AXES, pairs)  114 us
    dot_general x12, matrix products, dot(): lax.dot_general(a, b, (((da,), (db,)), ((), ())), precision=lax.Precision...  20.5 us
  transfers between devices with their start and end apart: 32, of which 17 were waited for; matrix products, arithmetic and copies ran while one was open for 13% of the time, Pallas kernels for 0%

profile of v7, /device:TPU:6, one launch (start us, length us, event | category | flops | bytes accessed | tf_op | source)
XLA Modules:
  0.0 286.9 jit_solution(917911369849620900)
XLA Ops:
  0.0 1.9 collective-permute-start
  2.1 4.3 %collective-permute-done = f32[512,1024]{1,0:T(8,128)} collective-permute-done((f32[512,1024]{1,0:T(8,128)}, f32[512,1024]{1,0:T(8,128)}, u32[]{:S(2)}, u32[]{:S(2)}) %collective-permute-start) | collective-permute-done | bytes 2097184 | tf_op jit(solution)/shard_map/ppermute | solution.py:34
  6.4 2.7 broadcast_select_fusion.2
  9.1 1.7 constant_dynamic-slice_fusion.12
  10.8 1.8 fusion.7
  12.7 1.9 multiply_subtract_fusion.1
  14.9 7.7 %collective-permute-start.1 = (f32[256,512]{1,0:T(8,128)S(1)}, f32[256,512]{1,0:T(8,128)S(1)}, u32[]{:S(2)}, u32[]{:S(2)}) collective-permute-start(f32[256,512]{1,0:T(8,128)S(1)} %get-tuple-element.113), channel_id=1, source_target_pairs={{0,4},{1,5},{2,6},{3,7},{4,8},{5,9},{6,10},{7,11},{8,12},{9,13},{1... | collective-permute-start | bytes 1572872 | tf_op jit(solution)/shard_map/ppermute | solution.py:34
  22.6 1.9 collective-permute-start.2
  24.5 2.8 collective-permute-start.3
  27.3 10.0 %collective-permute-start.5 = (f32[256,1024]{1,0:T(8,128)S(1)}, f32[256,1024]{1,0:T(8,128)}, u32[]{:S(2)}, u32[]{:S(2)}) collective-permute-start(f32[256,1024]{1,0:T(8,128)S(1)} %constant_dynamic-slice_fusion.10), channel_id=1, source_target_pairs={{0,480},{1,481},{2,482},{3,483},{4,484},{5,485},{6,486},{7,487},{8... | collective-permute-start | bytes 3145736 | tf_op jit(solution)/shard_map/ppermute | solution.py:34
  38.0 1.2 fusion.17
  39.2 1.1 fusion.20
  42.5 2.1 subtract_divide_fusion.1
  44.6 2.2 subtract_divide_fusion
  46.8 4.1 %collective-permute-done.3 = f32[256,512]{1,0:T(8,128)S(1)} collective-permute-done((f32[256,512]{1,0:T(8,128)S(1)}, f32[256,512]{1,0:T(8,128)S(1)}, u32[]{:S(2)}, u32[]{:S(2)}) %collective-permute-start.3) | collective-permute-done | bytes 524320 | tf_op jit(solution)/shard_map/ppermute | solution.py:34
  52.0 27.3 %collective-permute-done.5 = f32[256,1024]{1,0:T(8,128)} collective-permute-done((f32[256,1024]{1,0:T(8,128)S(1)}, f32[256,1024]{1,0:T(8,128)}, u32[]{:S(2)}, u32[]{:S(2)}) %collective-permute-start.5) | collective-permute-done | bytes 1048608 | tf_op jit(solution)/shard_map/ppermute | solution.py:34
  79.3 1.9 collective-permute-start.6
  81.2 6.1 %collective-permute-start.4 = (f32[128,512]{1,0:T(8,128)S(1)}, f32[128,512]{1,0:T(8,128)S(1)}, u32[]{:S(2)}, u32[]{:S(2)}) collective-permute-start(f32[128,512]{1,0:T(8,128)S(1)} %constant_dynamic-slice_fusion.11), channel_id=1, source_target_pairs={{0,1},{1,0},{2,3},{3,2},{4,5},{5,4},{6,7},{7,6},{8,9},{9,8},{10,11... | collective-permute-start | bytes 786440 | tf_op jit(solution)/shard_map/ppermute | solution.py:34
  87.4 1.1 constant_dynamic-slice_fusion.9
  88.5 2.3 fusion.23
  90.7 2.5 multiply_subtract_fusion
  95.4 2.5 subtract_add_fusion
  98.2 2.8 collective-permute-start.10
  101.0 4.4 %collective-permute-start.8 = (f32[256,256]{1,0:T(8,128)S(1)}, f32[256,256]{1,0:T(8,128)S(1)}, u32[]{:S(2)}, u32[]{:S(2)}) collective-permute-start(f32[256,256]{1,0:T(8,128)S(1)} %get-tuple-element.121), channel_id=1, source_target_pairs={{0,4},{1,5},{2,6},{3,7},{4,8},{5,9},{6,10},{7,11},{8,12},{9,13},{1... | collective-permute-start | bytes 786440 | tf_op jit(solution)/shard_map/ppermute | solution.py:34
  105.4 3.7 %collective-permute-start.9 = (f32[256,256]{1,0:T(8,128)S(1)}, f32[256,256]{1,0:T(8,128)S(1)}, u32[]{:S(2)}, u32[]{:S(2)}) collective-permute-start(f32[256,256]{1,0:T(8,128)S(1)} %get-tuple-element.120), channel_id=1, source_target_pairs={{0,8},{1,9},{2,10},{3,11},{4,12},{5,13},{6,14},{7,15},{8,0},{9,1},... | collective-permute-start | bytes 786440 | tf_op jit(solution)/shard_map/ppermute | solution.py:34
  109.1 4.3 %collective-permute-start.7 = (f32[128,512]{1,0:T(8,128)S(1)}, f32[128,512]{1,0:T(8,128)S(1)}, u32[]{:S(2)}, u32[]{:S(2)}) collective-permute-start(f32[128,512]{1,0:T(8,128)S(1)} %dynamic-slice_add_fusion), channel_id=1, source_target_pairs={{0,2},{1,3},{2,0},{3,1},{4,6},{5,7},{6,4},{7,5},{8,10},{9,11},{10,... | collective-permute-start | bytes 786440 | tf_op jit(solution)/shard_map/ppermute | solution.py:34
  114.5 2.2 collective-permute-done.8
  117.4 2.2 collective-permute-start.15
  119.6 5.6 %collective-permute-start.12 = (f32[256,256]{1,0:T(8,128)}, f32[256,256]{1,0:T(8,128)}, u32[]{:S(2)}, u32[]{:S(2)}) collective-permute-start(f32[256,256]{1,0:T(8,128)} %get-tuple-element.117), channel_id=1, source_target_pairs={{0,4},{1,5},{2,6},{3,7},{4,8},{5,9},{6,10},{7,11},{8,12},{9,13},{1... | collective-permute-start | bytes 786440 | tf_op jit(solution)/shard_map/ppermute | solution.py:34
  125.2 3.3 %collective-permute-start.13 = (f32[256,256]{1,0:T(8,128)}, f32[256,256]{1,0:T(8,128)}, u32[]{:S(2)}, u32[]{:S(2)}) collective-permute-start(f32[256,256]{1,0:T(8,128)} %get-tuple-element.116), channel_id=1, source_target_pairs={{0,8},{1,9},{2,10},{3,11},{4,12},{5,13},{6,14},{7,15},{8,0},{9,1},... | collective-permute-start | bytes 786440 | tf_op jit(solution)/shard_map/ppermute | solution.py:34
  128.6 1.9 collective-permute-start.14
  131.3 3.6 %collective-permute-start.11 = (f32[128,512]{1,0:T(8,128)}, f32[128,512]{1,0:T(8,128)}, u32[]{:S(2)}, u32[]{:S(2)}) collective-permute-start(f32[128,512]{1,0:T(8,128)} %add_multiply_fusion.2), channel_id=1, source_target_pairs={{0,1},{1,0},{2,3},{3,2},{4,5},{5,4},{6,7},{7,6},{8,9},{9,8},{10,11... | collective-permute-start | bytes 786440 | tf_op jit(solution)/shard_map/ppermute | solution.py:34
  136.0 4.4 %collective-permute-start.18 = (f32[256,256]{1,0:T(8,128)S(1)}, f32[256,256]{1,0:T(8,128)S(1)}, u32[]{:S(2)}, u32[]{:S(2)}) collective-permute-start(f32[256,256]{1,0:T(8,128)S(1)} %add.343), channel_id=1, source_target_pairs={{0,2},{1,3},{2,0},{3,1},{4,6},{5,7},{6,4},{7,5},{8,10},{9,11},{10,... | collective-permute-start | bytes 786440 | tf_op jit(solution)/shard_map/ppermute | solution.py:34
  141.3 2.0 add_add_fusion.1
  143.3 3.4 %collective-permute-start.17 = (f32[256,256]{1,0:T(8,128)}, f32[256,256]{1,0:T(8,128)}, u32[]{:S(2)}, u32[]{:S(2)}) collective-permute-start(f32[256,256]{1,0:T(8,128)} %add_add_fusion.1), channel_id=1, source_target_pairs={{0,1},{1,0},{2,3},{3,2},{4,5},{5,4},{6,7},{7,6},{8,9},{9,8},{10,11... | collective-permute-start | bytes 786440 | tf_op jit(solution)/shard_map/ppermute | solution.py:34
  146.7 2.1 maximum_select_fusion.1
  148.8 2.0 collective-permute-done.18
  151.6 4.4 %collective-permute-start.20 = (f32[256,256]{1,0:T(8,128)}, f32[256,256]{1,0:T(8,128)S(1)}, u32[]{:S(2)}, u32[]{:S(2)}) collective-permute-start(f32[256,256]{1,0:T(8,128)} %add_multiply_fusion.1), channel_id=1, source_target_pairs={{0,4},{1,5},{2,6},{3,7},{4,8},{5,9},{6,10},{7,11},{8,12},{9,13},{1... | collective-permute-start | bytes 786440 | tf_op jit(solution)/shard_map/ppermute | solution.py:34
  155.9 3.5 %collective-permute-start.21 = (f32[256,256]{1,0:T(8,128)}, f32[256,256]{1,0:T(8,128)}, u32[]{:S(2)}, u32[]{:S(2)}) collective-permute-start(f32[256,256]{1,0:T(8,128)} %add_multiply_fusion.1), channel_id=1, source_target_pairs={{0,8},{1,9},{2,10},{3,11},{4,12},{5,13},{6,14},{7,15},{8,0},{9,1},... | collective-permute-start | bytes 786440 | tf_op jit(solution)/shard_map/ppermute | solution.py:34
  159.5 1.9 collective-permute-start.22
  161.5 3.8 %collective-permute-start.16 = (f32[256,512]{1,0:T(8,128)}, f32[256,512]{1,0:T(8,128)S(1)}, u32[]{:S(2)}, u32[]{:S(2)}) collective-permute-start(f32[256,512]{1,0:T(8,128)} %maximum_select_fusion.1), channel_id=1, source_target_pairs={{0,4},{1,5},{2,6},{3,7},{4,0},{5,1},{6,2},{7,3},{8,12},{9,13},{10,... | collective-permute-start | bytes 1572872 | tf_op jit(solution)/shard_map/ppermute | solution.py:34
  166.3 1.9 collective-permute-start.19
  168.8 3.2 %collective-permute-done.22 = f32[256,256]{1,0:T(8,128)} collective-permute-done((f32[256,256]{1,0:T(8,128)}, f32[256,256]{1,0:T(8,128)}, u32[]{:S(2)}, u32[]{:S(2)}) %collective-permute-start.22) | collective-permute-done | bytes 262176 | tf_op jit(solution)/shard_map/ppermute | solution.py:34
  176.2 3.6 %collective-permute-done.19 = f32[256,256]{1,0:T(8,128)S(1)} collective-permute-done((f32[256,256]{1,0:T(8,128)S(1)}, f32[256,256]{1,0:T(8,128)S(1)}, u32[]{:S(2)}, u32[]{:S(2)}) %collective-permute-start.19) | collective-permute-done | bytes 262176 | tf_op jit(solution)/shard_map/ppermute | solution.py:34
  179.8 4.4 %collective-permute-start.23 = (f32[256,256]{1,0:T(8,128)S(1)}, f32[256,256]{1,0:T(8,128)S(1)}, u32[]{:S(2)}, u32[]{:S(2)}) collective-permute-start(f32[256,256]{1,0:T(8,128)S(1)} %add_multiply_fusion), channel_id=1, source_target_pairs={{0,4},{1,5},{2,6},{3,7},{4,8},{5,9},{6,10},{7,11},{8,12},{9,13},{1... | collective-permute-start | bytes 786440 | tf_op jit(solution)/shard_map/ppermute | solution.py:34
  184.2 3.1 %collective-permute-start.24 = (f32[256,256]{1,0:T(8,128)S(1)}, f32[256,256]{1,0:T(8,128)S(1)}, u32[]{:S(2)}, u32[]{:S(2)}) collective-permute-start(f32[256,256]{1,0:T(8,128)S(1)} %add_multiply_fusion), channel_id=1, source_target_pairs={{0,8},{1,9},{2,10},{3,11},{4,12},{5,13},{6,14},{7,15},{8,0},{9,1},... | collective-permute-start | bytes 786440 | tf_op jit(solution)/shard_map/ppermute | solution.py:34
  187.3 3.3 %collective-permute-start.25 = (f32[256,256]{1,0:T(8,128)S(1)}, f32[256,256]{1,0:T(8,128)S(1)}, u32[]{:S(2)}, u32[]{:S(2)}) collective-permute-start(f32[256,256]{1,0:T(8,128)S(1)} %add_multiply_fusion), channel_id=1, source_target_pairs={{0,12},{1,13},{2,14},{3,15},{4,0},{5,1},{6,2},{7,3},{8,4},{9,5},{1... | collective-permute-start | bytes 786440 | tf_op jit(solution)/shard_map/ppermute | solution.py:34
  190.8 3.7 %collective-permute-start.26 = (f32[512,512]{1,0:T(8,128)S(1)}, f32[512,512]{1,0:T(8,128)S(1)}, u32[]{:S(2)}, u32[]{:S(2)}) collective-permute-start(f32[512,512]{1,0:T(8,128)S(1)} %pad_maximum_fusion), channel_id=1, source_target_pairs={{0,12},{1,13},{2,14},{3,15},{4,8},{5,9},{6,10},{7,11},{8,4},{9,5},... | collective-permute-start | bytes 3145736 | tf_op jit(solution)/shard_map/ppermute | solution.py:34
  195.1 1.6 collective-permute-done.24
  196.8 4.2 %collective-permute-done.25 = f32[256,256]{1,0:T(8,128)S(1)} collective-permute-done((f32[256,256]{1,0:T(8,128)S(1)}, f32[256,256]{1,0:T(8,128)S(1)}, u32[]{:S(2)}, u32[]{:S(2)}) %collective-permute-start.25) | collective-permute-done | bytes 262176 | tf_op jit(solution)/shard_map/ppermute | solution.py:34
  203.7 18.8 %collective-permute-done.26 = f32[512,512]{1,0:T(8,128)S(1)} collective-permute-done((f32[512,512]{1,0:T(8,128)S(1)}, f32[512,512]{1,0:T(8,128)S(1)}, u32[]{:S(2)}, u32[]{:S(2)}) %collective-permute-start.26) | collective-permute-done | bytes 1048608 | tf_op jit(solution)/shard_map/ppermute | solution.py:34
  222.6 1.9 fusion.27
  224.5 2.0 fusion.5
  226.5 1.5 broadcast_select_fusion
  228.0 1.9 collective-permute-start.27
  229.9 5.6 %collective-permute-start.28 = (f32[512,256]{1,0:T(8,128)S(1)}, f32[512,256]{1,0:T(8,128)S(1)}, u32[]{:S(2)}, u32[]{:S(2)}) collective-permute-start(f32[512,256]{1,0:T(8,128)S(1)} %fusion.25), channel_id=1, source_target_pairs={{0,32},{1,33},{2,34},{3,35},{4,36},{5,37},{6,38},{7,39},{8,40},{9,... | collective-permute-start | bytes 1572872 | tf_op jit(solution)/shard_map/ppermute | solution.py:34
  235.5 1.3 collective-permute-start.30
  236.8 1.9 collective-permute-start.29
  238.7 1.3 collective-permute-start.31
  240.0 18.6 %collective-permute-done.28 = f32[512,256]{1,0:T(8,128)S(1)} collective-permute-done((f32[512,256]{1,0:T(8,128)S(1)}, f32[512,256]{1,0:T(8,128)S(1)}, u32[]{:S(2)}, u32[]{:S(2)}) %collective-permute-start.28) | collective-permute-done | bytes 524320 | tf_op jit(solution)/shard_map/ppermute | solution.py:34
  258.6 13.3 %collective-permute-done.30 = f32[512,256]{1,0:T(8,128)S(1)} collective-permute-done((f32[512,256]{1,0:T(8,128)S(1)}, f32[512,256]{1,0:T(8,128)S(1)}, u32[]{:S(2)}, u32[]{:S(2)}) %collective-permute-start.30) | collective-permute-done | bytes 524320 | tf_op jit(solution)/shard_map/ppermute | solution.py:34
  271.9 8.4 %collective-permute-done.29 = f32[512,256]{1,0:T(8,128)S(1)} collective-permute-done((f32[512,256]{1,0:T(8,128)S(1)}, f32[512,256]{1,0:T(8,128)S(1)}, u32[]{:S(2)}, u32[]{:S(2)}) %collective-permute-start.29) | collective-permute-done | bytes 524320 | tf_op jit(solution)/shard_map/ppermute | solution.py:34
  280.3 4.5 %collective-permute-done.31 = f32[512,256]{1,0:T(8,128)S(1)} collective-permute-done((f32[512,256]{1,0:T(8,128)S(1)}, f32[512,256]{1,0:T(8,128)S(1)}, u32[]{:S(2)}, u32[]{:S(2)}) %collective-permute-start.31) | collective-permute-done | bytes 524320 | tf_op jit(solution)/shard_map/ppermute | solution.py:34
  284.8 2.2 fusion
  (87 shorter events, 21.0 us)
Async XLA Ops:
  0.0 6.4 %collective-permute-start = (f32[512,1024]{1,0:T(8,128)}, f32[512,1024]{1,0:T(8,128)}, u32[]{:S(2)}, u32[]{:S(2)}) collective-permute-start(f32[512,1024]{1,0:T(8,128)} %bitcast.30), channel_id=1, source_target_pairs={{0,16},{1,17},{2,18},{3,19},{4,20},{5,21},{6,22},{7,23},{8,24},{9,... | collective-permute-start | bytes 6291464 | tf_op jit(solution)/shard_map/ppermute | solution.py:34
  9.1 3.6 %copy-start = (f32[512,1024]{1,0:T(8,128)}, f32[512,1024]{1,0:T(8,128)S(1)}, u32[]{:S(2)}) copy-start(f32[512,1024]{1,0:T(8,128)S(1)} %get-tuple-element.104) | copy-start | bytes 6291460
  14.6 22.7 %copy-start.8 = (s32[32]{0:T(128)S(1)}, s32[32]{0:T(128)}, u32[]{:S(2)}) copy-start(s32[32]{0:T(128)} %param.7) | copy-start | bytes 388
  14.9 26.7 %copy-start.10 = (f32[1024]{0:T(1024)S(1)}, f32[1024]{0:T(1024)}, u32[]{:S(2)}) copy-start(f32[1024]{0:T(1024)} %param.6) | copy-start | bytes 12292
  14.9 27.0 %copy-start.9 = (f32[32]{0:T(128)S(1)}, f32[32]{0:T(128)}, u32[]{:S(2)}) copy-start(f32[32]{0:T(128)} %param.5) | copy-start | bytes 388
  14.9 31.9 %collective-permute-start.1 = (f32[256,512]{1,0:T(8,128)S(1)}, f32[256,512]{1,0:T(8,128)S(1)}, u32[]{:S(2)}, u32[]{:S(2)}) collective-permute-start(f32[256,512]{1,0:T(8,128)S(1)} %get-tuple-element.113), channel_id=1, source_target_pairs={{0,4},{1,5},{2,6},{3,7},{4,8},{5,9},{6,10},{7,11},{8,12},{9,13},{1... | collective-permute-start | bytes 1572872 | tf_op jit(solution)/shard_map/ppermute | solution.py:34
  22.6 24.2 %collective-permute-start.2 = (f32[256,512]{1,0:T(8,128)S(1)}, f32[256,512]{1,0:T(8,128)S(1)}, u32[]{:S(2)}, u32[]{:S(2)}) collective-permute-start(f32[256,512]{1,0:T(8,128)S(1)} %get-tuple-element.112), channel_id=1, source_target_pairs={{0,8},{1,9},{2,10},{3,11},{4,12},{5,13},{6,14},{7,15},{8,0},{9,1},... | collective-permute-start | bytes 1572872 | tf_op jit(solution)/shard_map/ppermute | solution.py:34
  24.5 26.4 %collective-permute-start.3 = (f32[256,512]{1,0:T(8,128)S(1)}, f32[256,512]{1,0:T(8,128)S(1)}, u32[]{:S(2)}, u32[]{:S(2)}) collective-permute-start(f32[256,512]{1,0:T(8,128)S(1)} %get-tuple-element.111), channel_id=1, source_target_pairs={{0,12},{1,13},{2,14},{3,15},{4,0},{5,1},{6,2},{7,3},{8,4},{9,5},{1... | collective-permute-start | bytes 1572872 | tf_op jit(solution)/shard_map/ppermute | solution.py:34
  27.3 52.0 %collective-permute-start.5 = (f32[256,1024]{1,0:T(8,128)S(1)}, f32[256,1024]{1,0:T(8,128)}, u32[]{:S(2)}, u32[]{:S(2)}) collective-permute-start(f32[256,1024]{1,0:T(8,128)S(1)} %constant_dynamic-slice_fusion.10), channel_id=1, source_target_pairs={{0,480},{1,481},{2,482},{3,483},{4,484},{5,485},{6,486},{7,487},{8... | collective-permute-start | bytes 3145736 | tf_op jit(solution)/shard_map/ppermute | solution.py:34
  51.2 0.8 copy-start.3
  79.3 13.9 %collective-permute-start.6 = (f32[256,1024]{1,0:T(8,128)}, f32[256,1024]{1,0:T(8,128)}, u32[]{:S(2)}, u32[]{:S(2)}) collective-permute-start(f32[256,1024]{1,0:T(8,128)} %collective-permute-done.5), channel_id=1, source_target_pairs={{0,16},{1,17},{2,18},{3,19},{4,20},{5,21},{6,22},{7,23},{8,24},{9,... | collective-permute-start | bytes 3145736 | tf_op jit(solution)/shard_map/ppermute | solution.py:34
  81.2 27.8 %collective-permute-start.4 = (f32[128,512]{1,0:T(8,128)S(1)}, f32[128,512]{1,0:T(8,128)S(1)}, u32[]{:S(2)}, u32[]{:S(2)}) collective-permute-start(f32[128,512]{1,0:T(8,128)S(1)} %constant_dynamic-slice_fusion.11), channel_id=1, source_target_pairs={{0,1},{1,0},{2,3},{3,2},{4,5},{5,4},{6,7},{7,6},{8,9},{9,8},{10,11... | collective-permute-start | bytes 786440 | tf_op jit(solution)/shard_map/ppermute | solution.py:34
  90.7 3.6 %copy-start.2 = (f32[256,1024]{1,0:T(8,128)S(1)}, f32[256,1024]{1,0:T(8,128)}, u32[]{:S(2)}) copy-start(f32[256,1024]{1,0:T(8,128)} %get-tuple-element.109) | copy-start | bytes 3145732
  94.3 1.0 copy-start.6
  98.1 11.0 %copy-start.4 = (f32[256,512]{1,0:T(8,128)S(1)}, f32[256,512]{1,0:T(8,128)}, u32[]{:S(2)}) copy-start(f32[256,512]{1,0:T(8,128)} %copy-done.3) | copy-start | bytes 1572868
  98.2 16.3 %collective-permute-start.10 = (f32[256,256]{1,0:T(8,128)S(1)}, f32[256,256]{1,0:T(8,128)S(1)}, u32[]{:S(2)}, u32[]{:S(2)}) collective-permute-start(f32[256,256]{1,0:T(8,128)S(1)} %get-tuple-element.119), channel_id=1, source_target_pairs={{0,12},{1,13},{2,14},{3,15},{4,0},{5,1},{6,2},{7,3},{8,4},{9,5},{1... | collective-permute-start | bytes 786440 | tf_op jit(solution)/shard_map/ppermute | solution.py:34
  101.0 15.7 %collective-permute-start.8 = (f32[256,256]{1,0:T(8,128)S(1)}, f32[256,256]{1,0:T(8,128)S(1)}, u32[]{:S(2)}, u32[]{:S(2)}) collective-permute-start(f32[256,256]{1,0:T(8,128)S(1)} %get-tuple-element.121), channel_id=1, source_target_pairs={{0,4},{1,5},{2,6},{3,7},{4,8},{5,9},{6,10},{7,11},{8,12},{9,13},{1... | collective-permute-start | bytes 786440 | tf_op jit(solution)/shard_map/ppermute | solution.py:34
  105.4 11.3 %collective-permute-start.9 = (f32[256,256]{1,0:T(8,128)S(1)}, f32[256,256]{1,0:T(8,128)S(1)}, u32[]{:S(2)}, u32[]{:S(2)}) collective-permute-start(f32[256,256]{1,0:T(8,128)S(1)} %get-tuple-element.120), channel_id=1, source_target_pairs={{0,8},{1,9},{2,10},{3,11},{4,12},{5,13},{6,14},{7,15},{8,0},{9,1},... | collective-permute-start | bytes 786440 | tf_op jit(solution)/shard_map/ppermute | solution.py:34
  109.1 21.4 %copy-start.7 = (f32[128,512]{1,0:T(8,128)S(1)}, f32[128,512]{1,0:T(8,128)}, u32[]{:S(2)}) copy-start(f32[128,512]{1,0:T(8,128)} %subtract_divide_fusion.1) | copy-start | bytes 786436
  109.1 21.4 %collective-permute-start.7 = (f32[128,512]{1,0:T(8,128)S(1)}, f32[128,512]{1,0:T(8,128)S(1)}, u32[]{:S(2)}, u32[]{:S(2)}) collective-permute-start(f32[128,512]{1,0:T(8,128)S(1)} %dynamic-slice_add_fusion), channel_id=1, source_target_pairs={{0,2},{1,3},{2,0},{3,1},{4,6},{5,7},{6,4},{7,5},{8,10},{9,11},{10,... | collective-permute-start | bytes 786440 | tf_op jit(solution)/shard_map/ppermute | solution.py:34
  117.4 17.5 %collective-permute-start.15 = (f32[256,256]{1,0:T(8,128)}, f32[256,256]{1,0:T(8,128)}, u32[]{:S(2)}, u32[]{:S(2)}) collective-permute-start(f32[256,256]{1,0:T(8,128)} %add_add_fusion.2), channel_id=1, source_target_pairs={{0,1},{1,0},{2,3},{3,2},{4,5},{5,4},{6,7},{7,6},{8,9},{9,8},{10,11... | collective-permute-start | bytes 786440 | tf_op jit(solution)/shard_map/ppermute | solution.py:34
  119.6 20.7 %collective-permute-start.12 = (f32[256,256]{1,0:T(8,128)}, f32[256,256]{1,0:T(8,128)}, u32[]{:S(2)}, u32[]{:S(2)}) collective-permute-start(f32[256,256]{1,0:T(8,128)} %get-tuple-element.117), channel_id=1, source_target_pairs={{0,4},{1,5},{2,6},{3,7},{4,8},{5,9},{6,10},{7,11},{8,12},{9,13},{1... | collective-permute-start | bytes 786440 | tf_op jit(solution)/shard_map/ppermute | solution.py:34
  125.2 15.2 %collective-permute-start.13 = (f32[256,256]{1,0:T(8,128)}, f32[256,256]{1,0:T(8,128)}, u32[]{:S(2)}, u32[]{:S(2)}) collective-permute-start(f32[256,256]{1,0:T(8,128)} %get-tuple-element.116), channel_id=1, source_target_pairs={{0,8},{1,9},{2,10},{3,11},{4,12},{5,13},{6,14},{7,15},{8,0},{9,1},... | collective-permute-start | bytes 786440 | tf_op jit(solution)/shard_map/ppermute | solution.py:34
  128.6 12.7 %collective-permute-start.14 = (f32[256,256]{1,0:T(8,128)}, f32[256,256]{1,0:T(8,128)}, u32[]{:S(2)}, u32[]{:S(2)}) collective-permute-start(f32[256,256]{1,0:T(8,128)} %get-tuple-element.115), channel_id=1, source_target_pairs={{0,12},{1,13},{2,14},{3,15},{4,0},{5,1},{6,2},{7,3},{8,4},{9,5},{1... | collective-permute-start | bytes 786440 | tf_op jit(solution)/shard_map/ppermute | solution.py:34
  130.5 20.3 %slice-start = ((f32[256,512]{1,0:T(8,128)}), f32[256,256]{1,0:T(8,128)S(1)}, s32[]{:S(2)}) async-start(f32[256,512]{1,0:T(8,128)} %subtract_divide_fusion), calls=%async_computation | async-start | bytes 524288 | tf_op jit(solution)/shard_map/slice | solution.py:160
  131.3 15.4 %collective-permute-start.11 = (f32[128,512]{1,0:T(8,128)}, f32[128,512]{1,0:T(8,128)}, u32[]{:S(2)}, u32[]{:S(2)}) collective-permute-start(f32[128,512]{1,0:T(8,128)} %add_multiply_fusion.2), channel_id=1, source_target_pairs={{0,1},{1,0},{2,3},{3,2},{4,5},{5,4},{6,7},{7,6},{8,9},{9,8},{10,11... | collective-permute-start | bytes 786440 | tf_op jit(solution)/shard_map/ppermute | solution.py:34
  136.0 14.8 %collective-permute-start.18 = (f32[256,256]{1,0:T(8,128)S(1)}, f32[256,256]{1,0:T(8,128)S(1)}, u32[]{:S(2)}, u32[]{:S(2)}) collective-permute-start(f32[256,256]{1,0:T(8,128)S(1)} %add.343), channel_id=1, source_target_pairs={{0,2},{1,3},{2,0},{3,1},{4,6},{5,7},{6,4},{7,5},{8,10},{9,11},{10,... | collective-permute-start | bytes 786440 | tf_op jit(solution)/shard_map/ppermute | solution.py:34
  143.3 22.0 %collective-permute-start.17 = (f32[256,256]{1,0:T(8,128)}, f32[256,256]{1,0:T(8,128)}, u32[]{:S(2)}, u32[]{:S(2)}) collective-permute-start(f32[256,256]{1,0:T(8,128)} %add_add_fusion.1), channel_id=1, source_target_pairs={{0,1},{1,0},{2,3},{3,2},{4,5},{5,4},{6,7},{7,6},{8,9},{9,8},{10,11... | collective-permute-start | bytes 786440 | tf_op jit(solution)/shard_map/ppermute | solution.py:34
  151.6 16.7 %collective-permute-start.20 = (f32[256,256]{1,0:T(8,128)}, f32[256,256]{1,0:T(8,128)S(1)}, u32[]{:S(2)}, u32[]{:S(2)}) collective-permute-start(f32[256,256]{1,0:T(8,128)} %add_multiply_fusion.1), channel_id=1, source_target_pairs={{0,4},{1,5},{2,6},{3,7},{4,8},{5,9},{6,10},{7,11},{8,12},{9,13},{1... | collective-permute-start | bytes 786440 | tf_op jit(solution)/shard_map/ppermute | solution.py:34
  155.9 12.9 %collective-permute-start.21 = (f32[256,256]{1,0:T(8,128)}, f32[256,256]{1,0:T(8,128)}, u32[]{:S(2)}, u32[]{:S(2)}) collective-permute-start(f32[256,256]{1,0:T(8,128)} %add_multiply_fusion.1), channel_id=1, source_target_pairs={{0,8},{1,9},{2,10},{3,11},{4,12},{5,13},{6,14},{7,15},{8,0},{9,1},... | collective-permute-start | bytes 786440 | tf_op jit(solution)/shard_map/ppermute | solution.py:34
  159.5 12.6 %collective-permute-start.22 = (f32[256,256]{1,0:T(8,128)}, f32[256,256]{1,0:T(8,128)}, u32[]{:S(2)}, u32[]{:S(2)}) collective-permute-start(f32[256,256]{1,0:T(8,128)} %add_multiply_fusion.1), channel_id=1, source_target_pairs={{0,12},{1,13},{2,14},{3,15},{4,0},{5,1},{6,2},{7,3},{8,4},{9,5},{1... | collective-permute-start | bytes 786440 | tf_op jit(solution)/shard_map/ppermute | solution.py:34
  161.5 29.2 %collective-permute-start.16 = (f32[256,512]{1,0:T(8,128)}, f32[256,512]{1,0:T(8,128)S(1)}, u32[]{:S(2)}, u32[]{:S(2)}) collective-permute-start(f32[256,512]{1,0:T(8,128)} %maximum_select_fusion.1), channel_id=1, source_target_pairs={{0,4},{1,5},{2,6},{3,7},{4,0},{5,1},{6,2},{7,3},{8,12},{9,13},{10,... | collective-permute-start | bytes 1572872 | tf_op jit(solution)/shard_map/ppermute | solution.py:34
  166.3 13.4 %collective-permute-start.19 = (f32[256,256]{1,0:T(8,128)S(1)}, f32[256,256]{1,0:T(8,128)S(1)}, u32[]{:S(2)}, u32[]{:S(2)}) collective-permute-start(f32[256,256]{1,0:T(8,128)S(1)} %add.348), channel_id=1, source_target_pairs={{0,2},{1,3},{2,0},{3,1},{4,6},{5,7},{6,4},{7,5},{8,10},{9,11},{10,... | collective-permute-start | bytes 786440 | tf_op jit(solution)/shard_map/ppermute | solution.py:34
  175.1 4.6 %slice-start.1 = ((f32[256,512]{1,0:T(8,128)}), f32[256,256]{1,0:T(8,128)S(1)}, s32[]{:S(2)}) async-start(f32[256,512]{1,0:T(8,128)} %subtract_divide_fusion), calls=%async_computation.1 | async-start | bytes 524288 | tf_op jit(solution)/shard_map/slice | solution.py:181
  176.2 14.6 %copy-start.5 = (f32[256,512]{1,0:T(8,128)S(1)}, f32[256,512]{1,0:T(8,128)}, u32[]{:S(2)}) copy-start(f32[256,512]{1,0:T(8,128)} %maximum_select_fusion.1) | copy-start | bytes 1572868
  179.8 15.4 %collective-permute-start.23 = (f32[256,256]{1,0:T(8,128)S(1)}, f32[256,256]{1,0:T(8,128)S(1)}, u32[]{:S(2)}, u32[]{:S(2)}) collective-permute-start(f32[256,256]{1,0:T(8,128)S(1)} %add_multiply_fusion), channel_id=1, source_target_pairs={{0,4},{1,5},{2,6},{3,7},{4,8},{5,9},{6,10},{7,11},{8,12},{9,13},{1... | collective-permute-start | bytes 786440 | tf_op jit(solution)/shard_map/ppermute | solution.py:34
  184.2 12.6 %collective-permute-start.24 = (f32[256,256]{1,0:T(8,128)S(1)}, f32[256,256]{1,0:T(8,128)S(1)}, u32[]{:S(2)}, u32[]{:S(2)}) collective-permute-start(f32[256,256]{1,0:T(8,128)S(1)} %add_multiply_fusion), channel_id=1, source_target_pairs={{0,8},{1,9},{2,10},{3,11},{4,12},{5,13},{6,14},{7,15},{8,0},{9,1},... | collective-permute-start | bytes 786440 | tf_op jit(solution)/shard_map/ppermute | solution.py:34
  187.3 13.7 %collective-permute-start.25 = (f32[256,256]{1,0:T(8,128)S(1)}, f32[256,256]{1,0:T(8,128)S(1)}, u32[]{:S(2)}, u32[]{:S(2)}) collective-permute-start(f32[256,256]{1,0:T(8,128)S(1)} %add_multiply_fusion), channel_id=1, source_target_pairs={{0,12},{1,13},{2,14},{3,15},{4,0},{5,1},{6,2},{7,3},{8,4},{9,5},{1... | collective-permute-start | bytes 786440 | tf_op jit(solution)/shard_map/ppermute | solution.py:34
  190.8 31.7 %collective-permute-start.26 = (f32[512,512]{1,0:T(8,128)S(1)}, f32[512,512]{1,0:T(8,128)S(1)}, u32[]{:S(2)}, u32[]{:S(2)}) collective-permute-start(f32[512,512]{1,0:T(8,128)S(1)} %pad_maximum_fusion), channel_id=1, source_target_pairs={{0,12},{1,13},{2,14},{3,15},{4,8},{5,9},{6,10},{7,11},{8,4},{9,5},... | collective-permute-start | bytes 3145736 | tf_op jit(solution)/shard_map/ppermute | solution.py:34
  202.6 20.0 %copy-start.1 = (f32[512,1024]{1,0:T(8,128)S(1)}, f32[512,1024]{1,0:T(8,128)}, u32[]{:S(2)}) copy-start(f32[512,1024]{1,0:T(8,128)} %copy-done) | copy-start | bytes 6291460
  228.0 56.8 %collective-permute-start.27 = (f32[512,1024]{1,0:T(8,128)S(1)}, f32[512,1024]{1,0:T(8,128)S(1)}, u32[]{:S(2)}, u32[]{:S(2)}) collective-permute-start(f32[512,1024]{1,0:T(8,128)S(1)} %get-tuple-element.129), channel_id=1, source_target_pairs={{0,16},{1,17},{2,18},{3,19},{4,20},{5,21},{6,22},{7,23},{8,24},{9,... | collective-permute-start | bytes 6291464 | tf_op jit(solution)/shard_map/ppermute | solution.py:34
  229.9 28.7 %collective-permute-start.28 = (f32[512,256]{1,0:T(8,128)S(1)}, f32[512,256]{1,0:T(8,128)S(1)}, u32[]{:S(2)}, u32[]{:S(2)}) collective-permute-start(f32[512,256]{1,0:T(8,128)S(1)} %fusion.25), channel_id=1, source_target_pairs={{0,32},{1,33},{2,34},{3,35},{4,36},{5,37},{6,38},{7,39},{8,40},{9,... | collective-permute-start | bytes 1572872 | tf_op jit(solution)/shard_map/ppermute | solution.py:34
  235.5 36.4 %collective-permute-start.30 = (f32[512,256]{1,0:T(8,128)S(1)}, f32[512,256]{1,0:T(8,128)S(1)}, u32[]{:S(2)}, u32[]{:S(2)}) collective-permute-start(f32[512,256]{1,0:T(8,128)S(1)} %fusion.25), channel_id=1, source_target_pairs={{16,32},{17,33},{18,34},{19,35},{20,36},{21,37},{22,38},{23,39},{2... | collective-permute-start | bytes 1572872 | tf_op jit(solution)/shard_map/ppermute | solution.py:34
  236.8 43.5 %collective-permute-start.29 = (f32[512,256]{1,0:T(8,128)S(1)}, f32[512,256]{1,0:T(8,128)S(1)}, u32[]{:S(2)}, u32[]{:S(2)}) collective-permute-start(f32[512,256]{1,0:T(8,128)S(1)} %fusion.26), channel_id=1, source_target_pairs={{0,32},{1,33},{2,34},{3,35},{4,36},{5,37},{6,38},{7,39},{8,40},{9,... | collective-permute-start | bytes 1572872 | tf_op jit(solution)/shard_map/ppermute | solution.py:34
  238.7 46.0 %collective-permute-start.31 = (f32[512,256]{1,0:T(8,128)S(1)}, f32[512,256]{1,0:T(8,128)S(1)}, u32[]{:S(2)}, u32[]{:S(2)}) collective-permute-start(f32[512,256]{1,0:T(8,128)S(1)} %fusion.26), channel_id=1, source_target_pairs={{16,32},{17,33},{18,34},{19,35},{20,36},{21,37},{22,38},{23,39},{2... | collective-permute-start | bytes 1572872 | tf_op jit(solution)/shard_map/ppermute | solution.py:34

commit v8 on v4

--- a/solution.py
+++ b/solution.py
@@ -23,9 +23,10 @@
 
 
 SWAP = route(lambda o, x, z: (o ^ 1, x, z))
-DOWN = [route(lambda o, x, z: (o - 2 + c, x, z) if o % 2 == 0 else None) for c in (0, 1)]
+DOWN = route(lambda o, x, z: (o - 2, x, z))
 UP = [route(lambda o, x, z: (o + 2 - c, x, z) if o % 2 == c else None) for c in (0, 1)]
 AROUND = [route(lambda o, x, z: (o, x + r, z)) for r in range(X)]
+ACROSS = [route(lambda o, x, z: (o, x ^ d, z)) for d in range(X)]
 ALONG = [route(lambda o, x, z: (o, x, z ^ d)) for d in range(ZL)]
 
 
@@ -117,13 +118,14 @@
     one, two, three = base, base + 1, (base + 2) % ORB
 
     other = move(own, SWAP)
-    arrived = [move(own[c * ROWS : (c + 1) * ROWS], DOWN[c]) for c in (0, 1)]
     slab_one = jnp.where(first, own, other)
     slab_two = jnp.where(first, other, own)
+    near = move(rows_at(slab_one, core * ROWS, ROWS), DOWN)
     one_cols = cols_at(slab_one, at, COLS)
     two_cols = cols_at(slab_two, at, COLS)
 
-    inner_sends = send_x(pair_term(slab_one, slab_two, two_cols, one_cols))
+    inner = pair_term(slab_one, slab_two, two_cols, one_cols)
+    inner_sends = send_x(inner)
     inner_parts = around(inner_sends)
     energies = after((occupied_energy, virtual_energy, virtual_count), inner_sends)
     inner_weight = weight(one, two, at, *energies)
@@ -137,8 +139,7 @@
     inner_kept, inner_sent = halves(add_x(inner_parts))
     inner_next = move(inner_sent, ALONG[1])
 
-    arrived = after(arrived, inner_sent)
-    near = arrived[0] + arrived[1]
+    near = after(near, inner_sent)
     far = move(near, SWAP)
     near_cols = cols_at(near, at, COLS)
     outer_near = pair_term(near_two, near, near_cols, near_two_cols)
@@ -149,13 +150,15 @@
     left, right = slice(0, CHUNK), slice(CHUNK, COLS)
     sends = [send_x(outer[:, w]) for w in (left, right)]
     parts = [around(sends[n]) for n in (0, 1)]
-    inner_kept = inner_kept + after(inner_next, sends)
+    kept_a, sent_a = halves(add_x(after(parts[0], sends)))
+    next_a = move(sent_a, ALONG[1])
+    inner_kept = inner_kept + after(inner_next, sent_a)
     inner_far = move(inner_kept, ALONG[2])
-
-    kept_a, sent_a = halves(add_x(after(parts[0], inner_kept)))
-    kept_a = kept_a + move(sent_a, ALONG[1])
+    kept_a = kept_a + after(next_a, inner_kept)
     far_a = move(kept_a, ALONG[2])
-    kept_b, sent_b = halves(add_x(after(parts[1], kept_a)))
+    parts_b = after(parts[1], kept_a)
+    sum_b = add_x(parts_b)
+    kept_b, sent_b = halves(sum_b)
     next_b = move(sent_b, ALONG[1])
 
     inner_t = (inner_kept + after(inner_far, sent_b)) * inner_weight
@@ -168,7 +171,7 @@
     quarter_a = join(t_a, after(other_a, kept_b))
     pieces_a = around([quarter_a] * X)
     inner_quarter = join(inner_t, after(inner_other, quarter_a))
-    inner_pieces = around([inner_quarter] * X)
+    inner_next = move(inner_quarter, ACROSS[1])
     t_b = (kept_b + after(far_b, inner_quarter)) * outer_weight[:, right]
     other_b = move(t_b, ALONG[1])
 
@@ -177,12 +180,20 @@
     incoming_a = [move(leaving_a, UP[c]) for c in (0, 1)]
     quarter_b = join(t_b, after(other_b, leaving_a))
     pieces_b = around([quarter_b] * X)
-    all_b = in_order(pieces_b)
+    inner_pair = jnp.concatenate([inner_quarter, after(inner_next, quarter_b)], 0)
+    inner_rest = move(inner_pair, ACROSS[3])
+    all_b = in_order(after(pieces_b, inner_pair))
     outgoing = dot(slab_two, all_b, 1, 0)
     incoming_b = [move(outgoing, UP[c]) for c in (0, 1)]
     incoming = [incoming_a[0], incoming_b[0], incoming_a[1], incoming_b[1]]
 
-    inner_all = in_order(after(inner_pieces, outgoing))
+    inner_all = jnp.zeros((X * QUARTER, COLS), jnp.float32)
+    inner_rest = after(inner_rest, outgoing)
+    for q, d in ((inner_pair, 0), (inner_rest, 3)):
+        for part, e in ((q[:QUARTER], d), (q[QUARTER:], d ^ 1)):
+            inner_all = lax.dynamic_update_slice_in_dim(
+                inner_all, part, (px ^ e) * QUARTER, 0
+            )
     to_one = dot(two_cols, inner_all, 1, 1)
     to_two = dot(slab_one, inner_all, 1, 0)
     three_cols = jnp.where(
@@ -199,9 +210,8 @@
         jnp.concatenate([blank, to_two], 1),
     )
     crossed = move(jnp.where(first, to_two, to_one), SWAP)
-    density = jnp.where(first, to_one, to_two) + crossed
-    incoming = after(incoming, density)
-    density = density + jnp.concatenate(incoming, 1)
+    crossed, incoming = after((crossed, incoming))
+    density = jnp.where(first, to_one, to_two) + crossed + jnp.concatenate(incoming, 1)
     return density[None]
 
 

time: 279 us -> 280 us (level)
  the two profiles are of different devices: /device:TPU:24 before, /device:TPU:152 now
where the time goes in v8:
time: 280 us; the launch traced here: 279 us
  waiting for transfers between devices  133 us (48%)
  starting transfers between devices  109 us (39%)
  matrix products  16.8 us (6%)
  other arithmetic  12.2 us (4%)
  local copies, waits for them, and re-layouts  7.23 us (3%)
    ppermute x34, waiting for transfers between devices, move(): return lax.ppermute(block, AXES, pairs)  133 us
    ppermute x34, starting transfers between devices, move(): return lax.ppermute(block, AXES, pairs)  109 us
    dot_general x12, matrix products, dot(): lax.dot_general(a, b, (((da,), (db,)), ((), ())), precision=lax.Precision...  16.8 us
  transfers between devices with their start and end apart: 34, of which 20 were waited for; matrix products, arithmetic and copies ran while one was open for 6% of the time, Pallas kernels for 0%

profile of v8, /device:TPU:152, one launch (start us, length us, event | category | flops | bytes accessed | tf_op | source)
XLA Modules:
  0.0 278.7 jit_solution(5317450077598419526)
XLA Ops:
  0.0 1.9 collective-permute-start
  2.1 4.3 %collective-permute-done = f32[512,1024]{1,0:T(8,128)} collective-permute-done((f32[512,1024]{1,0:T(8,128)}, f32[512,1024]{1,0:T(8,128)}, u32[]{:S(2)}, u32[]{:S(2)}) %collective-permute-start) | collective-permute-done | bytes 2097184 | tf_op jit(solution)/shard_map/ppermute | solution.py:34
  6.4 2.7 broadcast_select_fusion.2
  9.2 1.8 fusion.7
  11.0 1.9 multiply_subtract_fusion.1
  13.2 3.5 %collective-permute-start.1 = (f32[256,512]{1,0:T(8,128)S(1)}, f32[256,512]{1,0:T(8,128)S(1)}, u32[]{:S(2)}, u32[]{:S(2)}) collective-permute-start(f32[256,512]{1,0:T(8,128)S(1)} %get-tuple-element.109), channel_id=1, source_target_pairs={{0,4},{1,5},{2,6},{3,7},{4,8},{5,9},{6,10},{7,11},{8,12},{9,13},{1... | collective-permute-start | bytes 1572872 | tf_op jit(solution)/shard_map/ppermute | solution.py:34
  16.7 4.6 %collective-permute-start.2 = (f32[256,512]{1,0:T(8,128)S(1)}, f32[256,512]{1,0:T(8,128)S(1)}, u32[]{:S(2)}, u32[]{:S(2)}) collective-permute-start(f32[256,512]{1,0:T(8,128)S(1)} %get-tuple-element.108), channel_id=1, source_target_pairs={{0,8},{1,9},{2,10},{3,11},{4,12},{5,13},{6,14},{7,15},{8,0},{9,1},... | collective-permute-start | bytes 1572872 | tf_op jit(solution)/shard_map/ppermute | solution.py:34
  21.4 3.3 %collective-permute-start.3 = (f32[256,512]{1,0:T(8,128)S(1)}, f32[256,512]{1,0:T(8,128)S(1)}, u32[]{:S(2)}, u32[]{:S(2)}) collective-permute-start(f32[256,512]{1,0:T(8,128)S(1)} %get-tuple-element.107), channel_id=1, source_target_pairs={{0,12},{1,13},{2,14},{3,15},{4,0},{5,1},{6,2},{7,3},{8,4},{9,5},{1... | collective-permute-start | bytes 1572872 | tf_op jit(solution)/shard_map/ppermute | solution.py:34
  24.7 9.0 %collective-permute-start.5 = (f32[256,1024]{1,0:T(8,128)S(1)}, f32[256,1024]{1,0:T(8,128)S(1)}, u32[]{:S(2)}, u32[]{:S(2)}) collective-permute-start(f32[256,1024]{1,0:T(8,128)S(1)} %constant_dynamic-slice_fusion.12), channel_id=1, source_target_pairs={{0,480},{1,481},{2,482},{3,483},{4,484},{5,485},{6,486},{7,487},{8... | collective-permute-start | bytes 3145736 | tf_op jit(solution)/shard_map/ppermute | solution.py:34
  34.8 1.2 compare_convert_fusion
  36.8 1.2 fusion.21
  38.2 2.9 %fusion.15 = (f32[128,512]{1,0:T(8,128)}, f32[128,512]{1,0:T(8,128)}) fusion(f32[]{:T(128)} %bitcast.6, f32[512]{0:T(512)S(1)} %get-tuple-element.130, f32[128]{0:T(128)S(1)} %get-tuple-element.131, f32[]{:T(128)} %bitcast.4, f32[512]{0:T(512)S(1)} %dynamic_slice.118, f32[128]{0:T(128)S(1)} %dynamic_slice.117, f32[]{:T(128)} %bitcast.3, ...), kind=kLoop, calls=%fused_computation.29 | loop fusion | flops 589824 | bytes 531980 | tf_op jit(solution)/shard_map/div | solution.py:101
  41.1 1.5 collective-permute-done.2
  42.6 1.6 collective-permute-done.3
  45.2 41.3 %collective-permute-done.5 = f32[256,1024]{1,0:T(8,128)S(1)} collective-permute-done((f32[256,1024]{1,0:T(8,128)S(1)}, f32[256,1024]{1,0:T(8,128)S(1)}, u32[]{:S(2)}, u32[]{:S(2)}) %collective-permute-start.5) | collective-permute-done | bytes 1048608 | tf_op jit(solution)/shard_map/ppermute | solution.py:34
  86.4 1.9 collective-permute-start.6
  89.5 1.2 multiply_subtract_fusion
  92.1 1.3 subtract_add_fusion
  95.4 2.5 collective-permute-start.7
  97.9 3.1 %collective-permute-start.8 = (f32[256,256]{1,0:T(8,128)}, f32[256,256]{1,0:T(8,128)}, u32[]{:S(2)}, u32[]{:S(2)}) collective-permute-start(f32[256,256]{1,0:T(8,128)} %get-tuple-element.116), channel_id=1, source_target_pairs={{0,8},{1,9},{2,10},{3,11},{4,12},{5,13},{6,14},{7,15},{8,0},{9,1},... | collective-permute-start | bytes 786440 | tf_op jit(solution)/shard_map/ppermute | solution.py:34
  101.0 3.4 %collective-permute-start.9 = (f32[256,256]{1,0:T(8,128)}, f32[256,256]{1,0:T(8,128)}, u32[]{:S(2)}, u32[]{:S(2)}) collective-permute-start(f32[256,256]{1,0:T(8,128)} %get-tuple-element.115), channel_id=1, source_target_pairs={{0,12},{1,13},{2,14},{3,15},{4,0},{5,1},{6,2},{7,3},{8,4},{9,5},{1... | collective-permute-start | bytes 786440 | tf_op jit(solution)/shard_map/ppermute | solution.py:34
  104.5 2.2 collective-permute-start.4
  106.8 1.3 constant_dynamic-slice_fusion.2
  108.1 2.7 collective-permute-start.11
  110.8 2.0 collective-permute-done.7
  112.8 2.0 collective-permute-start.12
  114.8 4.5 %collective-permute-start.13 = (f32[256,256]{1,0:T(8,128)S(1)}, f32[256,256]{1,0:T(8,128)S(1)}, u32[]{:S(2)}, u32[]{:S(2)}) collective-permute-start(f32[256,256]{1,0:T(8,128)S(1)} %get-tuple-element.111), channel_id=1, source_target_pairs={{0,12},{1,13},{2,14},{3,15},{4,0},{5,1},{6,2},{7,3},{8,4},{9,5},{1... | collective-permute-start | bytes 786440 | tf_op jit(solution)/shard_map/ppermute | solution.py:34
  119.4 1.2 add_add_fusion.2
  120.6 4.1 %collective-permute-start.14 = (f32[128,256]{1,0:T(8,128)S(1)}, f32[128,256]{1,0:T(8,128)S(1)}, u32[]{:S(2)}, u32[]{:S(2)}) collective-permute-start(f32[128,256]{1,0:T(8,128)S(1)} %constant_dynamic-slice_fusion.1), channel_id=1, source_target_pairs={{0,1},{1,0},{2,3},{3,2},{4,5},{5,4},{6,7},{7,6},{8,9},{9,8},{10,11... | collective-permute-start | bytes 393224 | tf_op jit(solution)/shard_map/ppermute | solution.py:34
  124.8 1.9 collective-permute-start.10
  126.7 2.3 collective-permute-done.14
  129.1 2.5 collective-permute-start.16
  131.7 3.2 %collective-permute-start.18 = (f32[128,256]{1,0:T(8,128)S(1)}, f32[128,256]{1,0:T(8,128)S(1)}, u32[]{:S(2)}, u32[]{:S(2)}) collective-permute-start(f32[128,256]{1,0:T(8,128)S(1)} %constant_dynamic-slice_fusion), channel_id=1, source_target_pairs={{0,1},{1,0},{2,3},{3,2},{4,5},{5,4},{6,7},{7,6},{8,9},{9,8},{10,11... | collective-permute-start | bytes 393224 | tf_op jit(solution)/shard_map/ppermute | solution.py:34
  134.9 5.2 %collective-permute-done.10 = f32[128,512]{1,0:T(8,128)S(1)} collective-permute-done((f32[128,512]{1,0:T(8,128)S(1)}, f32[128,512]{1,0:T(8,128)S(1)}, u32[]{:S(2)}, u32[]{:S(2)}) %collective-permute-start.10) | collective-permute-done | bytes 262176 | tf_op jit(solution)/shard_map/ppermute | solution.py:34
  140.1 5.6 %collective-permute-start.15 = (f32[128,512]{1,0:T(8,128)S(1)}, f32[128,512]{1,0:T(8,128)S(1)}, u32[]{:S(2)}, u32[]{:S(2)}) collective-permute-start(f32[128,512]{1,0:T(8,128)S(1)} %add_multiply_fusion), channel_id=1, source_target_pairs={{0,1},{1,0},{2,3},{3,2},{4,5},{5,4},{6,7},{7,6},{8,9},{9,8},{10,11... | collective-permute-start | bytes 786440 | tf_op jit(solution)/shard_map/ppermute | solution.py:34
  145.8 1.9 collective-permute-start.17
  147.8 3.6 %collective-permute-start.20 = (f32[128,256]{1,0:T(8,128)S(1)}, f32[128,256]{1,0:T(8,128)S(1)}, u32[]{:S(2)}, u32[]{:S(2)}) collective-permute-start(f32[128,256]{1,0:T(8,128)S(1)} %dynamic-slice_add_fusion.1), channel_id=1, source_target_pairs={{0,2},{1,3},{2,0},{3,1},{4,6},{5,7},{6,4},{7,5},{8,10},{9,11},{10,... | collective-permute-start | bytes 393224 | tf_op jit(solution)/shard_map/ppermute | solution.py:34
  151.4 2.9 %collective-permute-done.17 = f32[128,256]{1,0:T(8,128)S(1)} collective-permute-done((f32[128,256]{1,0:T(8,128)S(1)}, f32[128,256]{1,0:T(8,128)S(1)}, u32[]{:S(2)}, u32[]{:S(2)}) %collective-permute-start.17) | collective-permute-done | bytes 131104 | tf_op jit(solution)/shard_map/ppermute | solution.py:34
  154.3 1.9 collective-permute-start.22
  156.3 5.0 %collective-permute-start.23 = (f32[256,256]{1,0:T(8,128)S(1)}, f32[256,256]{1,0:T(8,128)S(1)}, u32[]{:S(2)}, u32[]{:S(2)}) collective-permute-start(f32[256,256]{1,0:T(8,128)S(1)} %maximum_select_fusion.2), channel_id=1, source_target_pairs={{0,8},{1,9},{2,10},{3,11},{4,12},{5,13},{6,14},{7,15},{8,0},{9,1},... | collective-permute-start | bytes 786440 | tf_op jit(solution)/shard_map/ppermute | solution.py:34
  161.3 2.8 %collective-permute-start.24 = (f32[256,256]{1,0:T(8,128)S(1)}, f32[256,256]{1,0:T(8,128)S(1)}, u32[]{:S(2)}, u32[]{:S(2)}) collective-permute-start(f32[256,256]{1,0:T(8,128)S(1)} %maximum_select_fusion.2), channel_id=1, source_target_pairs={{0,12},{1,13},{2,14},{3,15},{4,0},{5,1},{6,2},{7,3},{8,4},{9,5},{1... | collective-permute-start | bytes 786440 | tf_op jit(solution)/shard_map/ppermute | solution.py:34
  164.5 3.0 %collective-permute-start.19 = (f32[256,512]{1,0:T(8,128)S(1)}, f32[256,512]{1,0:T(8,128)S(1)}, u32[]{:S(2)}, u32[]{:S(2)}) collective-permute-start(f32[256,512]{1,0:T(8,128)S(1)} %get-tuple-element.98), channel_id=1, source_target_pairs={{0,4},{1,5},{2,6},{3,7},{4,0},{5,1},{6,2},{7,3},{8,12},{9,13},{10,... | collective-permute-start | bytes 1572872 | tf_op jit(solution)/shard_map/ppermute | solution.py:34
  167.6 4.0 %collective-permute-start.21 = (f32[128,256]{1,0:T(8,128)S(1)}, f32[128,256]{1,0:T(8,128)S(1)}, u32[]{:S(2)}, u32[]{:S(2)}) collective-permute-start(f32[128,256]{1,0:T(8,128)S(1)} %slice_multiply_fusion), channel_id=1, source_target_pairs={{0,1},{1,0},{2,3},{3,2},{4,5},{5,4},{6,7},{7,6},{8,9},{9,8},{10,11... | collective-permute-start | bytes 393224 | tf_op jit(solution)/shard_map/ppermute | solution.py:34
  172.1 2.9 %collective-permute-done.24 = f32[256,256]{1,0:T(8,128)S(1)} collective-permute-done((f32[256,256]{1,0:T(8,128)S(1)}, f32[256,256]{1,0:T(8,128)S(1)}, u32[]{:S(2)}, u32[]{:S(2)}) %collective-permute-start.24) | collective-permute-done | bytes 262176 | tf_op jit(solution)/shard_map/ppermute | solution.py:34
  176.3 1.9 collective-permute-start.26
  178.2 3.3 %collective-permute-start.27 = (f32[256,256]{1,0:T(8,128)S(1)}, f32[256,256]{1,0:T(8,128)S(1)}, u32[]{:S(2)}, u32[]{:S(2)}) collective-permute-start(f32[256,256]{1,0:T(8,128)S(1)} %maximum_select_fusion.3), channel_id=1, source_target_pairs={{0,8},{1,9},{2,10},{3,11},{4,12},{5,13},{6,14},{7,15},{8,0},{9,1},... | collective-permute-start | bytes 786440 | tf_op jit(solution)/shard_map/ppermute | solution.py:34
  181.5 4.5 %collective-permute-start.28 = (f32[256,256]{1,0:T(8,128)S(1)}, f32[256,256]{1,0:T(8,128)S(1)}, u32[]{:S(2)}, u32[]{:S(2)}) collective-permute-start(f32[256,256]{1,0:T(8,128)S(1)} %maximum_select_fusion.3), channel_id=1, source_target_pairs={{0,12},{1,13},{2,14},{3,15},{4,0},{5,1},{6,2},{7,3},{8,4},{9,5},{1... | collective-permute-start | bytes 786440 | tf_op jit(solution)/shard_map/ppermute | solution.py:34
  186.3 1.9 collective-permute-start.25
  188.3 4.0 %collective-permute-done.27 = f32[256,256]{1,0:T(8,128)S(1)} collective-permute-done((f32[256,256]{1,0:T(8,128)S(1)}, f32[256,256]{1,0:T(8,128)S(1)}, u32[]{:S(2)}, u32[]{:S(2)}) %collective-permute-start.27) | collective-permute-done | bytes 262176 | tf_op jit(solution)/shard_map/ppermute | solution.py:34
  192.3 2.4 collective-permute-done.28
  197.0 16.8 %collective-permute-done.25 = f32[512,512]{1,0:T(8,128)S(1)} collective-permute-done((f32[512,512]{1,0:T(8,128)S(1)}, f32[512,512]{1,0:T(8,128)S(1)}, u32[]{:S(2)}, u32[]{:S(2)}) %collective-permute-start.25) | collective-permute-done | bytes 1048608 | tf_op jit(solution)/shard_map/ppermute | solution.py:34
  214.0 1.9 fusion.31
  215.9 2.0 fusion.5
  217.9 1.5 broadcast_select_fusion
  219.4 1.9 collective-permute-start.29
  221.3 1.9 collective-permute-start.30
  223.2 1.3 collective-permute-start.32
  224.5 5.9 %collective-permute-start.31 = (f32[512,256]{1,0:T(8,128)S(1)}, f32[512,256]{1,0:T(8,128)S(1)}, u32[]{:S(2)}, u32[]{:S(2)}) collective-permute-start(f32[512,256]{1,0:T(8,128)S(1)} %fusion.30), channel_id=1, source_target_pairs={{0,32},{1,33},{2,34},{3,35},{4,36},{5,37},{6,38},{7,39},{8,40},{9,... | collective-permute-start | bytes 1572872 | tf_op jit(solution)/shard_map/ppermute | solution.py:34
  230.5 1.3 collective-permute-start.33
  231.8 20.6 %collective-permute-done.30 = f32[512,256]{1,0:T(8,128)S(1)} collective-permute-done((f32[512,256]{1,0:T(8,128)S(1)}, f32[512,256]{1,0:T(8,128)S(1)}, u32[]{:S(2)}, u32[]{:S(2)}) %collective-permute-start.30) | collective-permute-done | bytes 524320 | tf_op jit(solution)/shard_map/ppermute | solution.py:34
  252.4 6.0 %collective-permute-done.32 = f32[512,256]{1,0:T(8,128)S(1)} collective-permute-done((f32[512,256]{1,0:T(8,128)S(1)}, f32[512,256]{1,0:T(8,128)S(1)}, u32[]{:S(2)}, u32[]{:S(2)}) %collective-permute-start.32) | collective-permute-done | bytes 524320 | tf_op jit(solution)/shard_map/ppermute | solution.py:34
  258.4 16.8 %collective-permute-done.31 = f32[512,256]{1,0:T(8,128)S(1)} collective-permute-done((f32[512,256]{1,0:T(8,128)S(1)}, f32[512,256]{1,0:T(8,128)S(1)}, u32[]{:S(2)}, u32[]{:S(2)}) %collective-permute-start.31) | collective-permute-done | bytes 524320 | tf_op jit(solution)/shard_map/ppermute | solution.py:34
  275.2 1.4 collective-permute-done.33
  276.5 2.2 fusion
  (83 shorter events, 12.9 us)
Async XLA Ops:
  0.0 6.4 %collective-permute-start = (f32[512,1024]{1,0:T(8,128)}, f32[512,1024]{1,0:T(8,128)}, u32[]{:S(2)}, u32[]{:S(2)}) collective-permute-start(f32[512,1024]{1,0:T(8,128)} %bitcast.30), channel_id=1, source_target_pairs={{0,16},{1,17},{2,18},{3,19},{4,20},{5,21},{6,22},{7,23},{8,24},{9,... | collective-permute-start | bytes 6291464 | tf_op jit(solution)/shard_map/ppermute | solution.py:34
  9.1 2.0 copy-start
  13.1 20.9 %copy-start.6 = (s32[32]{0:T(128)S(1)}, s32[32]{0:T(128)}, u32[]{:S(2)}) copy-start(s32[32]{0:T(128)} %param.7) | copy-start | bytes 388
  13.2 22.8 %copy-start.8 = (f32[1024]{0:T(1024)S(1)}, f32[1024]{0:T(1024)}, u32[]{:S(2)}) copy-start(f32[1024]{0:T(1024)} %param.6) | copy-start | bytes 12292
  13.2 23.0 %copy-start.7 = (f32[32]{0:T(128)S(1)}, f32[32]{0:T(128)}, u32[]{:S(2)}) copy-start(f32[32]{0:T(128)} %param.5) | copy-start | bytes 388
  13.2 27.9 %collective-permute-start.1 = (f32[256,512]{1,0:T(8,128)S(1)}, f32[256,512]{1,0:T(8,128)S(1)}, u32[]{:S(2)}, u32[]{:S(2)}) collective-permute-start(f32[256,512]{1,0:T(8,128)S(1)} %get-tuple-element.109), channel_id=1, source_target_pairs={{0,4},{1,5},{2,6},{3,7},{4,8},{5,9},{6,10},{7,11},{8,12},{9,13},{1... | collective-permute-start | bytes 1572872 | tf_op jit(solution)/shard_map/ppermute | solution.py:34
  16.7 25.9 %collective-permute-start.2 = (f32[256,512]{1,0:T(8,128)S(1)}, f32[256,512]{1,0:T(8,128)S(1)}, u32[]{:S(2)}, u32[]{:S(2)}) collective-permute-start(f32[256,512]{1,0:T(8,128)S(1)} %get-tuple-element.108), channel_id=1, source_target_pairs={{0,8},{1,9},{2,10},{3,11},{4,12},{5,13},{6,14},{7,15},{8,0},{9,1},... | collective-permute-start | bytes 1572872 | tf_op jit(solution)/shard_map/ppermute | solution.py:34
  21.4 22.8 %collective-permute-start.3 = (f32[256,512]{1,0:T(8,128)S(1)}, f32[256,512]{1,0:T(8,128)S(1)}, u32[]{:S(2)}, u32[]{:S(2)}) collective-permute-start(f32[256,512]{1,0:T(8,128)S(1)} %get-tuple-element.107), channel_id=1, source_target_pairs={{0,12},{1,13},{2,14},{3,15},{4,0},{5,1},{6,2},{7,3},{8,4},{9,5},{1... | collective-permute-start | bytes 1572872 | tf_op jit(solution)/shard_map/ppermute | solution.py:34
  24.7 61.7 %collective-permute-start.5 = (f32[256,1024]{1,0:T(8,128)S(1)}, f32[256,1024]{1,0:T(8,128)S(1)}, u32[]{:S(2)}, u32[]{:S(2)}) collective-permute-start(f32[256,1024]{1,0:T(8,128)S(1)} %constant_dynamic-slice_fusion.12), channel_id=1, source_target_pairs={{0,480},{1,481},{2,482},{3,483},{4,484},{5,485},{6,486},{7,487},{8... | collective-permute-start | bytes 3145736 | tf_op jit(solution)/shard_map/ppermute | solution.py:34
  44.4 44.0 %copy-start.2 = (f32[256,512]{1,0:T(8,128)}, f32[256,512]{1,0:T(8,128)S(1)}, u32[]{:S(2)}) copy-start(f32[256,512]{1,0:T(8,128)S(1)} %add_add_fusion) | copy-start | bytes 1572868
  86.4 4.5 %collective-permute-start.6 = (f32[256,1024]{1,0:T(8,128)S(1)}, f32[256,1024]{1,0:T(8,128)S(1)}, u32[]{:S(2)}, u32[]{:S(2)}) collective-permute-start(f32[256,1024]{1,0:T(8,128)S(1)} %collective-permute-done.5), channel_id=1, source_target_pairs={{0,16},{1,17},{2,18},{3,19},{4,20},{5,21},{6,22},{7,23},{8,24},{9,... | collective-permute-start | bytes 3145736 | tf_op jit(solution)/shard_map/ppermute | solution.py:34
  95.4 17.4 %collective-permute-start.7 = (f32[256,256]{1,0:T(8,128)}, f32[256,256]{1,0:T(8,128)}, u32[]{:S(2)}, u32[]{:S(2)}) collective-permute-start(f32[256,256]{1,0:T(8,128)} %get-tuple-element.117), channel_id=1, source_target_pairs={{0,4},{1,5},{2,6},{3,7},{4,8},{5,9},{6,10},{7,11},{8,12},{9,13},{1... | collective-permute-start | bytes 786440 | tf_op jit(solution)/shard_map/ppermute | solution.py:34
  97.9 16.9 %collective-permute-start.8 = (f32[256,256]{1,0:T(8,128)}, f32[256,256]{1,0:T(8,128)}, u32[]{:S(2)}, u32[]{:S(2)}) collective-permute-start(f32[256,256]{1,0:T(8,128)} %get-tuple-element.116), channel_id=1, source_target_pairs={{0,8},{1,9},{2,10},{3,11},{4,12},{5,13},{6,14},{7,15},{8,0},{9,1},... | collective-permute-start | bytes 786440 | tf_op jit(solution)/shard_map/ppermute | solution.py:34
  101.0 18.4 %collective-permute-start.9 = (f32[256,256]{1,0:T(8,128)}, f32[256,256]{1,0:T(8,128)}, u32[]{:S(2)}, u32[]{:S(2)}) collective-permute-start(f32[256,256]{1,0:T(8,128)} %get-tuple-element.115), channel_id=1, source_target_pairs={{0,12},{1,13},{2,14},{3,15},{4,0},{5,1},{6,2},{7,3},{8,4},{9,5},{1... | collective-permute-start | bytes 786440 | tf_op jit(solution)/shard_map/ppermute | solution.py:34
  104.5 20.2 %copy-start.3 = (f32[256,512]{1,0:T(8,128)S(1)}, f32[256,512]{1,0:T(8,128)}, u32[]{:S(2)}) copy-start(f32[256,512]{1,0:T(8,128)} %copy-done.2) | copy-start | bytes 1572868
  104.5 20.2 %collective-permute-start.4 = (f32[128,512]{1,0:T(8,128)}, f32[128,512]{1,0:T(8,128)S(1)}, u32[]{:S(2)}, u32[]{:S(2)}) collective-permute-start(f32[128,512]{1,0:T(8,128)} %constant_dynamic-slice_fusion.13), channel_id=1, source_target_pairs={{0,1},{1,0},{2,3},{3,2},{4,5},{5,4},{6,7},{7,6},{8,9},{9,8},{10,11... | collective-permute-start | bytes 786440 | tf_op jit(solution)/shard_map/ppermute | solution.py:34
  108.1 23.5 %collective-permute-start.11 = (f32[256,256]{1,0:T(8,128)S(1)}, f32[256,256]{1,0:T(8,128)S(1)}, u32[]{:S(2)}, u32[]{:S(2)}) collective-permute-start(f32[256,256]{1,0:T(8,128)S(1)} %get-tuple-element.113), channel_id=1, source_target_pairs={{0,4},{1,5},{2,6},{3,7},{4,8},{5,9},{6,10},{7,11},{8,12},{9,13},{1... | collective-permute-start | bytes 786440 | tf_op jit(solution)/shard_map/ppermute | solution.py:34
  112.8 18.8 %collective-permute-start.12 = (f32[256,256]{1,0:T(8,128)S(1)}, f32[256,256]{1,0:T(8,128)S(1)}, u32[]{:S(2)}, u32[]{:S(2)}) collective-permute-start(f32[256,256]{1,0:T(8,128)S(1)} %get-tuple-element.112), channel_id=1, source_target_pairs={{0,8},{1,9},{2,10},{3,11},{4,12},{5,13},{6,14},{7,15},{8,0},{9,1},... | collective-permute-start | bytes 786440 | tf_op jit(solution)/shard_map/ppermute | solution.py:34
  114.8 16.8 %collective-permute-start.13 = (f32[256,256]{1,0:T(8,128)S(1)}, f32[256,256]{1,0:T(8,128)S(1)}, u32[]{:S(2)}, u32[]{:S(2)}) collective-permute-start(f32[256,256]{1,0:T(8,128)S(1)} %get-tuple-element.111), channel_id=1, source_target_pairs={{0,12},{1,13},{2,14},{3,15},{4,0},{5,1},{6,2},{7,3},{8,4},{9,5},{1... | collective-permute-start | bytes 786440 | tf_op jit(solution)/shard_map/ppermute | solution.py:34
  119.4 20.7 %copy-start.5 = (f32[128,512]{1,0:T(8,128)S(1)}, f32[128,512]{1,0:T(8,128)}, u32[]{:S(2)}) copy-start(f32[128,512]{1,0:T(8,128)} %get-tuple-element.71) | copy-start | bytes 786436
  120.6 25.2 %copy-start.4 = (f32[128,512]{1,0:T(8,128)S(1)}, f32[128,512]{1,0:T(8,128)}, u32[]{:S(2)}) copy-start(f32[128,512]{1,0:T(8,128)} %get-tuple-element.73) | copy-start | bytes 786436
  120.6 8.4 %collective-permute-start.14 = (f32[128,256]{1,0:T(8,128)S(1)}, f32[128,256]{1,0:T(8,128)S(1)}, u32[]{:S(2)}, u32[]{:S(2)}) collective-permute-start(f32[128,256]{1,0:T(8,128)S(1)} %constant_dynamic-slice_fusion.1), channel_id=1, source_target_pairs={{0,1},{1,0},{2,3},{3,2},{4,5},{5,4},{6,7},{7,6},{8,9},{9,8},{10,11... | collective-permute-start | bytes 393224 | tf_op jit(solution)/shard_map/ppermute | solution.py:34
  124.8 15.3 %collective-permute-start.10 = (f32[128,512]{1,0:T(8,128)S(1)}, f32[128,512]{1,0:T(8,128)S(1)}, u32[]{:S(2)}, u32[]{:S(2)}) collective-permute-start(f32[128,512]{1,0:T(8,128)S(1)} %dynamic-slice_add_fusion), channel_id=1, source_target_pairs={{0,2},{1,3},{2,0},{3,1},{4,6},{5,7},{6,4},{7,5},{8,10},{9,11},{10,... | collective-permute-start | bytes 786440 | tf_op jit(solution)/shard_map/ppermute | solution.py:34
  129.1 16.7 %collective-permute-start.16 = (f32[128,256]{1,0:T(8,128)S(1)}, f32[128,256]{1,0:T(8,128)S(1)}, u32[]{:S(2)}, u32[]{:S(2)}) collective-permute-start(f32[128,256]{1,0:T(8,128)S(1)} %dynamic-slice_add_fusion.2), channel_id=1, source_target_pairs={{0,2},{1,3},{2,0},{3,1},{4,6},{5,7},{6,4},{7,5},{8,10},{9,11},{10,... | collective-permute-start | bytes 393224 | tf_op jit(solution)/shard_map/ppermute | solution.py:34
  131.7 16.0 %collective-permute-start.18 = (f32[128,256]{1,0:T(8,128)S(1)}, f32[128,256]{1,0:T(8,128)S(1)}, u32[]{:S(2)}, u32[]{:S(2)}) collective-permute-start(f32[128,256]{1,0:T(8,128)S(1)} %constant_dynamic-slice_fusion), channel_id=1, source_target_pairs={{0,1},{1,0},{2,3},{3,2},{4,5},{5,4},{6,7},{7,6},{8,9},{9,8},{10,11... | collective-permute-start | bytes 393224 | tf_op jit(solution)/shard_map/ppermute | solution.py:34
  140.1 24.0 %collective-permute-start.15 = (f32[128,512]{1,0:T(8,128)S(1)}, f32[128,512]{1,0:T(8,128)S(1)}, u32[]{:S(2)}, u32[]{:S(2)}) collective-permute-start(f32[128,512]{1,0:T(8,128)S(1)} %add_multiply_fusion), channel_id=1, source_target_pairs={{0,1},{1,0},{2,3},{3,2},{4,5},{5,4},{6,7},{7,6},{8,9},{9,8},{10,11... | collective-permute-start | bytes 786440 | tf_op jit(solution)/shard_map/ppermute | solution.py:34
  145.8 8.5 %collective-permute-start.17 = (f32[128,256]{1,0:T(8,128)S(1)}, f32[128,256]{1,0:T(8,128)S(1)}, u32[]{:S(2)}, u32[]{:S(2)}) collective-permute-start(f32[128,256]{1,0:T(8,128)S(1)} %slice_multiply_fusion.1), channel_id=1, source_target_pairs={{0,1},{1,0},{2,3},{3,2},{4,5},{5,4},{6,7},{7,6},{8,9},{9,8},{10,11... | collective-permute-start | bytes 393224 | tf_op jit(solution)/shard_map/ppermute | solution.py:34
  147.8 19.8 %collective-permute-start.20 = (f32[128,256]{1,0:T(8,128)S(1)}, f32[128,256]{1,0:T(8,128)S(1)}, u32[]{:S(2)}, u32[]{:S(2)}) collective-permute-start(f32[128,256]{1,0:T(8,128)S(1)} %dynamic-slice_add_fusion.1), channel_id=1, source_target_pairs={{0,2},{1,3},{2,0},{3,1},{4,6},{5,7},{6,4},{7,5},{8,10},{9,11},{10,... | collective-permute-start | bytes 393224 | tf_op jit(solution)/shard_map/ppermute | solution.py:34
  154.3 17.3 %collective-permute-start.22 = (f32[256,256]{1,0:T(8,128)S(1)}, f32[256,256]{1,0:T(8,128)S(1)}, u32[]{:S(2)}, u32[]{:S(2)}) collective-permute-start(f32[256,256]{1,0:T(8,128)S(1)} %maximum_select_fusion.2), channel_id=1, source_target_pairs={{0,4},{1,5},{2,6},{3,7},{4,8},{5,9},{6,10},{7,11},{8,12},{9,13},{1... | collective-permute-start | bytes 786440 | tf_op jit(solution)/shard_map/ppermute | solution.py:34
  156.3 15.9 %collective-permute-start.23 = (f32[256,256]{1,0:T(8,128)S(1)}, f32[256,256]{1,0:T(8,128)S(1)}, u32[]{:S(2)}, u32[]{:S(2)}) collective-permute-start(f32[256,256]{1,0:T(8,128)S(1)} %maximum_select_fusion.2), channel_id=1, source_target_pairs={{0,8},{1,9},{2,10},{3,11},{4,12},{5,13},{6,14},{7,15},{8,0},{9,1},... | collective-permute-start | bytes 786440 | tf_op jit(solution)/shard_map/ppermute | solution.py:34
  161.3 13.7 %collective-permute-start.24 = (f32[256,256]{1,0:T(8,128)S(1)}, f32[256,256]{1,0:T(8,128)S(1)}, u32[]{:S(2)}, u32[]{:S(2)}) collective-permute-start(f32[256,256]{1,0:T(8,128)S(1)} %maximum_select_fusion.2), channel_id=1, source_target_pairs={{0,12},{1,13},{2,14},{3,15},{4,0},{5,1},{6,2},{7,3},{8,4},{9,5},{1... | collective-permute-start | bytes 786440 | tf_op jit(solution)/shard_map/ppermute | solution.py:34
  164.5 21.7 %collective-permute-start.19 = (f32[256,512]{1,0:T(8,128)S(1)}, f32[256,512]{1,0:T(8,128)S(1)}, u32[]{:S(2)}, u32[]{:S(2)}) collective-permute-start(f32[256,512]{1,0:T(8,128)S(1)} %get-tuple-element.98), channel_id=1, source_target_pairs={{0,4},{1,5},{2,6},{3,7},{4,0},{5,1},{6,2},{7,3},{8,12},{9,13},{10,... | collective-permute-start | bytes 1572872 | tf_op jit(solution)/shard_map/ppermute | solution.py:34
  167.6 8.6 %collective-permute-start.21 = (f32[128,256]{1,0:T(8,128)S(1)}, f32[128,256]{1,0:T(8,128)S(1)}, u32[]{:S(2)}, u32[]{:S(2)}) collective-permute-start(f32[128,256]{1,0:T(8,128)S(1)} %slice_multiply_fusion), channel_id=1, source_target_pairs={{0,1},{1,0},{2,3},{3,2},{4,5},{5,4},{6,7},{7,6},{8,9},{9,8},{10,11... | collective-permute-start | bytes 393224 | tf_op jit(solution)/shard_map/ppermute | solution.py:34
  176.3 12.0 %collective-permute-start.26 = (f32[256,256]{1,0:T(8,128)S(1)}, f32[256,256]{1,0:T(8,128)S(1)}, u32[]{:S(2)}, u32[]{:S(2)}) collective-permute-start(f32[256,256]{1,0:T(8,128)S(1)} %maximum_select_fusion.3), channel_id=1, source_target_pairs={{0,4},{1,5},{2,6},{3,7},{4,8},{5,9},{6,10},{7,11},{8,12},{9,13},{1... | collective-permute-start | bytes 786440 | tf_op jit(solution)/shard_map/ppermute | solution.py:34
  178.2 14.1 %collective-permute-start.27 = (f32[256,256]{1,0:T(8,128)S(1)}, f32[256,256]{1,0:T(8,128)S(1)}, u32[]{:S(2)}, u32[]{:S(2)}) collective-permute-start(f32[256,256]{1,0:T(8,128)S(1)} %maximum_select_fusion.3), channel_id=1, source_target_pairs={{0,8},{1,9},{2,10},{3,11},{4,12},{5,13},{6,14},{7,15},{8,0},{9,1},... | collective-permute-start | bytes 786440 | tf_op jit(solution)/shard_map/ppermute | solution.py:34
  181.5 13.1 %collective-permute-start.28 = (f32[256,256]{1,0:T(8,128)S(1)}, f32[256,256]{1,0:T(8,128)S(1)}, u32[]{:S(2)}, u32[]{:S(2)}) collective-permute-start(f32[256,256]{1,0:T(8,128)S(1)} %maximum_select_fusion.3), channel_id=1, source_target_pairs={{0,12},{1,13},{2,14},{3,15},{4,0},{5,1},{6,2},{7,3},{8,4},{9,5},{1... | collective-permute-start | bytes 786440 | tf_op jit(solution)/shard_map/ppermute | solution.py:34
  186.3 27.6 %collective-permute-start.25 = (f32[512,512]{1,0:T(8,128)S(1)}, f32[512,512]{1,0:T(8,128)S(1)}, u32[]{:S(2)}, u32[]{:S(2)}) collective-permute-start(f32[512,512]{1,0:T(8,128)S(1)} %pad_maximum_fusion), channel_id=1, source_target_pairs={{0,12},{1,13},{2,14},{3,15},{4,8},{5,9},{6,10},{7,11},{8,4},{9,5},... | collective-permute-start | bytes 3145736 | tf_op jit(solution)/shard_map/ppermute | solution.py:34
  196.0 18.0 %copy-start.1 = (f32[512,1024]{1,0:T(8,128)S(1)}, f32[512,1024]{1,0:T(8,128)}, u32[]{:S(2)}) copy-start(f32[512,1024]{1,0:T(8,128)} %copy-done) | copy-start | bytes 6291460
  219.4 57.1 %collective-permute-start.29 = (f32[512,1024]{1,0:T(8,128)S(1)}, f32[512,1024]{1,0:T(8,128)S(1)}, u32[]{:S(2)}, u32[]{:S(2)}) collective-permute-start(f32[512,1024]{1,0:T(8,128)S(1)} %get-tuple-element.127), channel_id=1, source_target_pairs={{0,16},{1,17},{2,18},{3,19},{4,20},{5,21},{6,22},{7,23},{8,24},{9,... | collective-permute-start | bytes 6291464 | tf_op jit(solution)/shard_map/ppermute | solution.py:34
  221.3 31.0 %collective-permute-start.30 = (f32[512,256]{1,0:T(8,128)S(1)}, f32[512,256]{1,0:T(8,128)S(1)}, u32[]{:S(2)}, u32[]{:S(2)}) collective-permute-start(f32[512,256]{1,0:T(8,128)S(1)} %fusion.29), channel_id=1, source_target_pairs={{0,32},{1,33},{2,34},{3,35},{4,36},{5,37},{6,38},{7,39},{8,40},{9,... | collective-permute-start | bytes 1572872 | tf_op jit(solution)/shard_map/ppermute | solution.py:34
  223.2 35.1 %collective-permute-start.32 = (f32[512,256]{1,0:T(8,128)S(1)}, f32[512,256]{1,0:T(8,128)S(1)}, u32[]{:S(2)}, u32[]{:S(2)}) collective-permute-start(f32[512,256]{1,0:T(8,128)S(1)} %fusion.29), channel_id=1, source_target_pairs={{16,32},{17,33},{18,34},{19,35},{20,36},{21,37},{22,38},{23,39},{2... | collective-permute-start | bytes 1572872 | tf_op jit(solution)/shard_map/ppermute | solution.py:34
  224.5 50.6 %collective-permute-start.31 = (f32[512,256]{1,0:T(8,128)S(1)}, f32[512,256]{1,0:T(8,128)S(1)}, u32[]{:S(2)}, u32[]{:S(2)}) collective-permute-start(f32[512,256]{1,0:T(8,128)S(1)} %fusion.30), channel_id=1, source_target_pairs={{0,32},{1,33},{2,34},{3,35},{4,36},{5,37},{6,38},{7,39},{8,40},{9,... | collective-permute-start | bytes 1572872 | tf_op jit(solution)/shard_map/ppermute | solution.py:34
  230.5 46.0 %collective-permute-start.33 = (f32[512,256]{1,0:T(8,128)S(1)}, f32[512,256]{1,0:T(8,128)S(1)}, u32[]{:S(2)}, u32[]{:S(2)}) collective-permute-start(f32[512,256]{1,0:T(8,128)S(1)} %fusion.30), channel_id=1, source_target_pairs={{16,32},{17,33},{18,34},{19,35},{20,36},{21,37},{22,38},{23,39},{2... | collective-permute-start | bytes 1572872 | tf_op jit(solution)/shard_map/ppermute | solution.py:34
